TPU v7x, 256 devices: a whole 4x4x8 slice. The times are simulated.
256 devices in a mesh: ka: 16 (over x_lo, y, core), pw: 16 (over z, x_hi).
Axes of the slice: x: 4 (x_hi: 2, x_lo: 2; x = x_hi * 2 + x_lo), y: 4, z: 8, core: 2. Of those that a mesh axis runs over, the one named last changes fastest.
Arguments:
- coeffs: bfloat16 [256, 2, 6144, 256], P('ka', None, 'pw'), may hold values from -1.75 to 1.75
- neighbour: int32 [256], P('ka'), may hold values from 0 to 255, as said below
- gshift: int32 [6144], replicated, may hold values from 0 to 6143, each once
Outputs:
- inner_products: float32 [256, 256, 2, 256], P('pw', 'ka')
Inputs may be any that keep to these rules, and one draw needn't show every extreme that they name: neighbour[k] lies in the slab of 16 k-points that starts 2 * 16 points after the start of the slab of k, counted cyclically over the 256 points; the neighbours of one slab's points are distinct. `gshift`: each row appears once.
All inputs are finite; a program needn't handle non-finite values.
Results may differ from a plain program's by a relative error of at most 0.0003.
Values may be sent and summed in bfloat16 or wider, within the bound.
No kernel may reach another device: no remote copies, remote signals or barrier semaphores. Data moves between devices by JAX's collectives and lax.ppermute only.
A program may use at most 128 MiB of HBM per device.

v0:
```python
import jax
import jax.numpy as jnp
from jax import lax
from jax.sharding import PartitionSpec as P

SHIFT_DEV = 2


def passed_along(block, axis, distance):
    devices = range(lax.axis_size(axis))
    route = [((i - distance) % len(devices), i) for i in devices]
    return lax.ppermute(block, axis, route)


def band_major_rows(own_rows, partner_block):
    products_all = jnp.einsum(
        "mkcg,kdgn->mkcdn", own_rows, partner_block, preferred_element_type=jnp.float32
    )
    real_part = products_all[:, :, 0, 0] + products_all[:, :, 1, 1]
    imag_part = products_all[:, :, 0, 1] - products_all[:, :, 1, 0]
    return jnp.stack([real_part, imag_part], axis=2)


def on_device(coeffs, neighbour, gshift):
    slab_points = coeffs.shape[0]
    ka_count = lax.axis_size("ka")
    wrapped = lax.axis_index("ka") >= ka_count - SHIFT_DEV
    arrived = passed_along(coeffs, "ka", -SHIFT_DEV)
    local_order = neighbour % slab_points
    partner = jnp.take(arrived, local_order, axis=0)
    permuted = jnp.take(
        lax.all_to_all(partner, "pw", split_axis=0, concat_axis=2, tiled=True), gshift, axis=2
    )
    permuted_all = lax.all_to_all(permuted, "pw", split_axis=2, concat_axis=0, tiled=True)
    partner = jnp.where(wrapped, permuted_all, partner)
    band_major = jnp.transpose(coeffs, (3, 0, 1, 2))
    return lax.psum_scatter(
        band_major_rows(band_major, partner), "pw", scatter_dimension=0, tiled=True
    )


def solution(mesh):
    placed = (P("ka", None, "pw", None), P("ka"), P())
    return jax.shard_map(
        on_device, mesh=mesh, in_specs=placed, out_specs=P("pw", "ka", None, None), check_vma=False
    )
```

profile of v0, /device:TPU:26, one launch (start us, length us, event | category | flops | bytes accessed | tf_op | source)
XLA Modules:
  0.0 851.2 jit_solution(2646045167288103525)
XLA Ops:
  6.5 0.7 collective-permute-start
  7.3 0.7 compare_and_fusion.1
  8.0 138.3 %collective-permute-done = bf16[16,2,384,256]{3,2,1,0:T(8,128)(2,1)} collective-permute-done((bf16[16,2,384,256]{3,2,1,0:T(8,128)(2,1)}, bf16[16,2,384,256]{3,2,1,0:T(8,128)(2,1)}, u32[]{:S(2)}, u32[]{:S(2)}) %collective-permute-start) | collective-permute-done | bytes 6291488 | tf_op jit(solution)/shard_map/ppermute | solution.py:12
  146.2 6.4 gather_fusion
  152.6 6.1 broadcast_select_fusion.1
  158.7 0.0 copy-start
  158.7 10.3 %all-to-all-start = ((bf16[16,2,384,256]{3,2,1,0:T(8,128)(2,1)}), bf16[16,2,384,256]{3,2,1,0:T(8,128)(2,1)}, u32[]{:S(2)}, u32[]{:S(2)}) async-start(bf16[16,2,384,256]{3,2,1,0:T(8,128)(2,1)} %broadcast_select_fusion.1), calls=%async_computation | async-start | bytes 12582912 | tf_op jit(solution)/shard_map/all_to_all | solution.py:32
  169.0 0.0 copy-done
  169.0 144.9 %all-to-all-done = bf16[16,2,384,256]{3,2,1,0:T(8,128)(2,1)} async-done(((bf16[16,2,384,256]{3,2,1,0:T(8,128)(2,1)}), bf16[16,2,384,256]{3,2,1,0:T(8,128)(2,1)}, u32[]{:S(2)}, u32[]{:S(2)}) %all-to-all-start) | async-done | bytes 6291488 | tf_op jit(solution)/shard_map/all_to_all | solution.py:32
  313.9 3.2 copy.25
  317.1 40.4 %copy.26 = bf16[2,6144,256]{2,0,1:T(2,128)(2,1)} copy(bf16[2,6144,256]{2,1,0:T(8,128)(2,1)S(1)} %bitcast.48) | data formatting | bytes 12582912 | tf_op jit(solution)/shard_map/all_to_all | solution.py:32
  357.6 51.0 %gather_fusion.1 = bf16[6144,2,256]{2,1,0:T(2,128)(2,1)} fusion(bf16[2,6144,256]{2,0,1:T(2,128)(2,1)} %copy.26, s32[6144]{0:T(1024)S(1)} %fusion.8), kind=kCustom, calls=%fused_computation.1 | custom fusion | bytes 12607488 | tf_op jit(solution)/shard_map/jit(_take)/gather | solution.py:31
  408.6 24.1 %fusion.3 = bf16[1,2,6144,256]{3,1,0,2:T(2,128)(2,1)} fusion(bf16[6144,2,256]{2,1,0:T(2,128)(2,1)} %gather_fusion.1, pred[6144]{0:T(1024)(128)(4,1)S(1)} %compare_and_fusion), kind=kLoop, calls=%fused_computation.9 | loop fusion | flops 3145728 | bytes 12589056 | tf_op jit(solution)/shard_map/jit(_take)/select_n | solution.py:31
  432.7 6.0 all-to-all-start.1
  438.7 0.2 reduce-scatter.2.cloned.1.call-start
  439.0 144.4 %all-to-all-done.1 = bf16[1,2,6144,256]{3,1,0,2:T(2,128)(2,1)} async-done(((bf16[1,2,6144,256]{3,1,0,2:T(2,128)(2,1)}), bf16[1,2,6144,256]{3,1,0,2:T(2,128)(2,1)}, u32[]{:S(2)}, u32[]{:S(2)}) %all-to-all-start.1) | async-done | bytes 6291488 | tf_op jit(solution)/shard_map/all_to_all | solution.py:34
  583.3 14.9 %convolution_bitcast_fusion = f32[256,16,2,2,256]{0,4,2,3,1:T(8,128)} fusion(bf16[16,2,384,256]{3,2,1,0:T(8,128)(2,1)} %param.3, bf16[16,2,384,256]{3,2,1,0:T(8,128)(2,1)} %broadcast_select_fusion.1, bf16[1,2,16,384,256]{4,1,3,2,0:T(2,128)(2,1)} %bitcast.6, pred[]{:T(512)S(6)} %ge.15), kind=kOutput, calls=%fused_computation.3 | convolution fusion | flops 3224371200 | bytes 35651584 | tf_op jit(solution)/shard_map/mkcg,kdgn->mkcdn/dot_general | solution.py:16
  598.2 4.0 fusion.5
  602.2 4.0 fusion.7
  606.2 3.8 pad_maximum_fusion
  610.0 10.3 %copy.34 = f32[256,16,2,256]{3,1,2,0:T(8,128)} copy(f32[256,16,2,256]{0,3,1,2:T(8,128)} %pad_maximum_fusion) | data formatting | bytes 16777216 | tf_op jit(solution)/shard_map/stack | solution.py:21
  620.3 0.0 reduce-scatter.2.cloned.1.call-update
  620.3 221.8 %reduce-scatter.2.cloned.1.call-done = f32[16,16,2,256]{3,1,2,0:T(8,128)} async-done(((f32[256,16,2,256]{3,1,2,0:T(8,128)}), f32[16,16,2,256]{3,1,2,0:T(8,128)}) %reduce-scatter.2.cloned.1.call-update) | async-done | bytes 524304 | tf_op jit(solution)/shard_map/reduce_scatter | solution.py:37
  842.1 2.2 copy.35
  (3 shorter events, 0.0 us)
Async XLA Ops:
  6.5 139.7 %collective-permute-start = (bf16[16,2,384,256]{3,2,1,0:T(8,128)(2,1)}, bf16[16,2,384,256]{3,2,1,0:T(8,128)(2,1)}, u32[]{:S(2)}, u32[]{:S(2)}) collective-permute-start(bf16[16,2,384,256]{3,2,1,0:T(8,128)(2,1)} %param.3), channel_id=1, source_target_pairs={{32,0},{48,16},{64,32},{80,48},{96,64},{112,80},{128,96},{144,112}... | collective-permute-start | bytes 18874376 | tf_op jit(solution)/shard_map/ppermute | solution.py:12
  158.7 10.3 %copy-start = (s32[6144]{0:T(1024)S(1)}, s32[6144]{0:T(1024)}, u32[]{:S(2)}) copy-start(s32[6144]{0:T(1024)} %param.5) | copy-start | bytes 73732
  158.7 155.3 %all-to-all-start = ((bf16[16,2,384,256]{3,2,1,0:T(8,128)(2,1)}), bf16[16,2,384,256]{3,2,1,0:T(8,128)(2,1)}, u32[]{:S(2)}, u32[]{:S(2)}) async-start(bf16[16,2,384,256]{3,2,1,0:T(8,128)(2,1)} %broadcast_select_fusion.1), calls=%async_computation | async-start | bytes 12582912 | tf_op jit(solution)/shard_map/all_to_all | solution.py:32
  432.7 150.6 %all-to-all-start.1 = ((bf16[1,2,6144,256]{3,1,0,2:T(2,128)(2,1)}), bf16[1,2,6144,256]{3,1,0,2:T(2,128)(2,1)}, u32[]{:S(2)}, u32[]{:S(2)}) async-start(bf16[1,2,6144,256]{3,1,0,2:T(2,128)(2,1)} %fusion.3), calls=%async_computation.1 | async-start | bytes 12582912 | tf_op jit(solution)/shard_map/all_to_all | solution.py:34
  438.7 403.4 %reduce-scatter.2.cloned.1.call-start = ((), (), s32[]{:S(2)}) async-start(), calls=%async_computation.3 | async-start | bytes 8912896 | tf_op jit(solution)/shard_map/reduce_scatter | solution.py:37
Sparse Core Ops, SparseCore 0:
  620.5 221.5 reduce-scatter.1
where the time goes:
time: 853 us; the launch traced here: 851 us
  waiting for transfers between devices  649 us (76%)
  local copies, waits for them, and re-layouts  114 us (13%)
  other arithmetic  42.7 us (5%)
  starting transfers between devices  17.3 us (2%)
  matrix products  14.9 us (2%)
  between operations  13.5 us (2%)
    reduce_scatter x1, waiting for transfers between devices, on_device(): lax.psum_scatter(band_major_rows(band_major, partner), 'pw', scatter_dime...  222 us
    all_to_all x1, waiting for transfers between devices, on_device(): lax.all_to_all(partner, 'pw', split_axis=0, concat_axis=2, tiled=True)  145 us
    all_to_all x1, waiting for transfers between devices, on_device(): lax.all_to_all(permuted, 'pw', split_axis=2, concat_axis=0, tiled=True)  144 us
    ppermute x1, waiting for transfers between devices, passed_along(): return lax.ppermute(block, axis, route)  138 us
    gather x1, local copies, waits for them, and re-layouts, on_device(): jnp.take(lax.all_to_all(partner, 'pw', split_axis=0, concat_axis=2, tiled...  51 us
    all_to_all x2, local copies, waits for them, and re-layouts, on_device(): lax.all_to_all(partner, 'pw', split_axis=0, concat_axis=2, tiled=True)  43.6 us
    select_n x1, other arithmetic, on_device(): jnp.take(lax.all_to_all(partner, 'pw', split_axis=0, concat_axis=2, tiled...  24.1 us
  transfers between devices with their start and end apart: 4, of which 4 were waited for; matrix products, arithmetic and copies ran while one was open for 0% of the time, Pallas kernels for 0%

commit v1 on v0

v1 whole, which is shorter than its diff:
```python
import jax
import jax.numpy as jnp
from jax import lax
from jax.experimental import pallas as pl
from jax.experimental.pallas import tpu as pltpu
from jax.sharding import PartitionSpec as P

SHIFT_DEV = 2


def reorder_kernel(order, source, result, sems):
    count = result.shape[0]

    def block(i):
        return pltpu.make_async_copy(source.at[order[i]], result.at[i], sems.at[i])

    for i in range(count):
        block(i).start()
    for i in range(count):
        block(i).wait()


def reordered(source, order):
    return pl.pallas_call(
        reorder_kernel,
        grid_spec=pltpu.PrefetchScalarGridSpec(
            num_scalar_prefetch=1,
            grid=(),
            in_specs=[pl.BlockSpec(memory_space=pl.ANY)],
            out_specs=pl.BlockSpec(memory_space=pl.ANY),
            scratch_shapes=[pltpu.SemaphoreType.DMA((source.shape[0],))],
        ),
        out_shape=jax.ShapeDtypeStruct(source.shape, source.dtype),
        cost_estimate=pl.CostEstimate(flops=0, bytes_accessed=2 * source.size * 2, transcendentals=0),
    )(order, source)


def scatter_rows_kernel(target_ref, own_ref, out_ref):
    sources, parts, rows, bands = own_ref.shape
    height = out_ref.shape[1]
    first = pl.program_id(0) * height
    pair = 2
    wanted = first + lax.broadcasted_iota(jnp.int32, (height, pair * rows), 0)
    totals = [jnp.zeros((height, bands), jnp.float32) for _ in range(parts)]
    for s in range(0, sources, pair):
        hot = (target_ref[:, s * rows : (s + pair) * rows] == wanted).astype(jnp.bfloat16)
        for c in range(parts):
            block = own_ref[s : s + pair, c].reshape(pair * rows, bands)
            totals[c] += jnp.dot(hot, block, preferred_element_type=jnp.float32)
    for c in range(parts):
        out_ref[c] = totals[c].astype(out_ref.dtype)


def scattered_rows(own, target):
    sources, parts, rows, bands = own.shape
    total = sources * rows
    height = 256
    return pl.pallas_call(
        scatter_rows_kernel,
        grid=(total // height,),
        in_specs=[
            pl.BlockSpec((1, total), lambda i: (0, 0)),
            pl.BlockSpec(own.shape, lambda i: (0, 0, 0, 0), pipeline_mode=pl.Buffered(1)),
        ],
        out_specs=pl.BlockSpec((parts, height, bands), lambda i: (0, i, 0)),
        out_shape=jax.ShapeDtypeStruct((parts, total, bands), own.dtype),
        compiler_params=pltpu.CompilerParams(vmem_limit_bytes=40 << 20),
        cost_estimate=pl.CostEstimate(
            flops=2 * total * total * parts * bands, bytes_accessed=4 * own.size, transcendentals=0
        ),
    )(target.reshape(1, total), own)


def pair_kernel(own_ref, partner_ref, out_ref, acc_ref):
    step = pl.program_id(0)

    @pl.when(step == 0)
    def _():
        acc_ref[...] = jnp.zeros_like(acc_ref)

    sources, parts, rows, bands = partner_ref.shape
    own = [own_ref[c] for c in range(2)]
    partner = [partner_ref[:, d].reshape(sources * rows, bands) for d in range(2)]

    def product(c, d):
        return lax.dot_general(
            own[c], partner[d], (((0,), (0,)), ((), ())), preferred_element_type=jnp.float32
        )

    acc_ref[0] += product(0, 0) + product(1, 1)
    acc_ref[1] += product(0, 1) - product(1, 0)

    @pl.when(step == pl.num_programs(0) - 1)
    def _():
        for d in range(2):
            out_ref[:, d * bands : (d + 1) * bands] = acc_ref[d]


def pair_products(own, partner):
    sources, parts, rows, bands = partner.shape
    take = 2
    return pl.pallas_call(
        pair_kernel,
        grid=(sources // take,),
        in_specs=[
            pl.BlockSpec((parts, take * rows, bands), lambda i: (0, i, 0)),
            pl.BlockSpec((take, parts, rows, bands), lambda i: (i, 0, 0, 0)),
        ],
        out_specs=pl.BlockSpec((bands, 2 * bands), lambda i: (0, 0)),
        out_shape=jax.ShapeDtypeStruct((bands, 2 * bands), jnp.float32),
        scratch_shapes=[pltpu.VMEM((2, bands, bands), jnp.float32)],
        compiler_params=pltpu.CompilerParams(vmem_limit_bytes=40 << 20),
        cost_estimate=pl.CostEstimate(
            flops=8 * sources * rows * bands * bands, bytes_accessed=4 * partner.size, transcendentals=0
        ),
    )(own, partner)


def on_device(coeffs, neighbour, gshift):
    slab_points, parts, rows, bands = coeffs.shape
    ka_count = lax.axis_size("ka")
    wrapped = lax.axis_index("ka") >= ka_count - SHIFT_DEV
    route = [((i + SHIFT_DEV) % ka_count, i) for i in range(ka_count)]
    arrived = lax.ppermute(coeffs, "ka", route)
    own = lax.all_to_all(coeffs, "pw", split_axis=0, concat_axis=0, tiled=True)
    partner = reordered(arrived, neighbour % slab_points)
    partner = lax.all_to_all(partner, "pw", split_axis=0, concat_axis=0, tiled=True)
    target = jnp.where(wrapped, gshift, lax.iota(jnp.int32, gshift.shape[0]))
    products = pair_products(scattered_rows(own, target), partner)
    products = lax.all_to_all(products, "pw", split_axis=0, concat_axis=0, tiled=True)
    products = products.reshape(slab_points, bands // slab_points, 2, bands)
    return jnp.transpose(products, (1, 0, 2, 3))


def solution(mesh):
    placed = (P("ka", None, "pw", None), P("ka"), P())
    return jax.shard_map(
        on_device, mesh=mesh, in_specs=placed, out_specs=P("pw", "ka", None, None), check_vma=False
    )
```

time: 853 us -> 597 us (0.70)
  waiting for transfers between devices: 649 us -> 299 us
  Pallas kernels: 0 us -> 247 us
  local copies, waits for them, and re-layouts: 114 us -> 6.86 us
  other arithmetic: 42.7 us -> 0.52 us
  blocking collectives: 0 us -> 22.8 us
  matrix products: 14.9 us -> 0 us
  between operations: 13.5 us -> 0.09 us
    pallas_call x0 -> x3, Pallas kernels: none -> 247 us  [the longest x1 192 us: reordered(): pl.pallas_call(reorder_kernel, grid_spec=pltpu.PrefetchScalarGridSpec(num...]
    reduce_scatter x1 -> x0, waiting for transfers between devices: 222 us -> none  [on_device(): lax.psum_scatter(band_major_rows(band_major, partner), 'pw', scatter_dime...]
    all_to_all x2, waiting for transfers between devices: 289 us -> 95.9 us  [the longest x1 95.9 us: on_device(): lax.all_to_all(partner, 'pw', split_axis=0, concat_axis=0, tiled=True)]
    ppermute x1, waiting for transfers between devices: 138 us -> 203 us  [on_device(): arrived = lax.ppermute(coeffs, 'ka', route)]
    gather x2 -> x0, local copies, waits for them, and re-layouts: 57.4 us -> none  [the longest x1 51 us: on_device(): jnp.take(lax.all_to_all(partner, 'pw', split_axis=0, concat_axis=2, tiled...]
    all_to_all x2 -> x0, local copies, waits for them, and re-layouts: 43.6 us -> none  [on_device(): lax.all_to_all(partner, 'pw', split_axis=0, concat_axis=2, tiled=True)]
    select_n x2, other arithmetic: 30.2 us -> 0.52 us  [the longest x1 0.52 us: on_device(): partner = reordered(arrived, neighbour % slab_points)]
    all_to_all x0 -> x1, blocking collectives: none -> 22.8 us  [on_device(): lax.all_to_all(products, 'pw', split_axis=0, concat_axis=0, tiled=True)]
  transfers between devices with their start and end apart: 4 -> 3, of which waited for: 4 -> 2; matrix products, arithmetic and copies ran while one was open for 0% -> 0% of each run, Pallas kernels for 0% -> 40%
where the time goes in v1:
time: 597 us; the launch traced here: 596 us
  waiting for transfers between devices  299 us (50%)
  Pallas kernels  247 us (41%)
  blocking collectives  22.8 us (4%)
  starting transfers between devices  20 us (3%)
  local copies, waits for them, and re-layouts  6.86 us (1%)
    ppermute x1, waiting for transfers between devices, on_device(): arrived = lax.ppermute(coeffs, 'ka', route)  203 us
    pallas_call x1, Pallas kernels, reordered(): pl.pallas_call(reorder_kernel, grid_spec=pltpu.PrefetchScalarGridSpec(num...  192 us
    all_to_all x1, waiting for transfers between devices, on_device(): lax.all_to_all(partner, 'pw', split_axis=0, concat_axis=0, tiled=True)  95.9 us
    pallas_call x1, Pallas kernels, scattered_rows(): pl.pallas_call(scatter_rows_kernel, grid=(total // height,), in_specs=[pl...  46.1 us
    all_to_all x1, blocking collectives, on_device(): lax.all_to_all(products, 'pw', split_axis=0, concat_axis=0, tiled=True)  22.8 us
  transfers between devices with their start and end apart: 3, of which 2 were waited for; matrix products, arithmetic and copies ran while one was open for 0% of the time, Pallas kernels for 40%

profile of v1, /device:TPU:26, one launch (start us, length us, event | category | flops | bytes accessed | tf_op | source)
XLA Modules:
  0.0 595.5 jit_solution(13816446388062787450)
XLA Ops:
  0.0 0.0 copy-start.3
  0.0 10.3 %all-to-all-start = ((bf16[16,2,384,256]{3,2,1,0:T(8,128)(2,1)}), bf16[16,2,384,256]{3,2,1,0:T(8,128)(2,1)}, u32[]{:S(2)}, u32[]{:S(2)}) async-start(bf16[16,2,384,256]{3,2,1,0:T(8,128)(2,1)} %param.3), calls=%async_computation | async-start | bytes 12582912 | tf_op jit(solution)/shard_map/all_to_all | solution.py:125
  10.3 0.8 collective-permute-start
  11.1 0.0 copy-done.3
  11.1 0.5 and_select_fusion.order
  11.7 202.6 %collective-permute-done.source = bf16[16,2,384,256]{3,2,1,0:T(8,128)(2,1)} collective-permute-done((bf16[16,2,384,256]{3,2,1,0:T(8,128)(2,1)}, bf16[16,2,384,256]{3,2,1,0:T(8,128)(2,1)}, u32[]{:S(2)}, u32[]{:S(2)}) %collective-permute-start) | collective-permute-done | bytes 6291488 | tf_op jit(solution)/shard_map/ppermute | solution.py:124
  214.3 192.5 %shard_map.38 = bf16[16,2,384,256]{3,2,1,0:T(8,128)(2,1)} custom-call(s32[16]{0:T(128)} %and_select_fusion.order, bf16[16,2,384,256]{3,2,1,0:T(8,128)(2,1)} %collective-permute-done.source), custom_call_target="tpu_custom_call" | custom-call | bytes 12582912 | tf_op jit(solution)/shard_map/pallas_call | solution.py:24
  406.8 0.0 copy-start.2
  406.8 0.0 all-to-all-done.own_ref
  406.8 8.8 %all-to-all-start.1 = ((bf16[16,2,384,256]{3,2,1,0:T(8,128)(2,1)}), bf16[16,2,384,256]{3,2,1,0:T(8,128)(2,1)}, u32[]{:S(2)}, u32[]{:S(2)}) async-start(bf16[16,2,384,256]{3,2,1,0:T(8,128)(2,1)} %shard_map.38), calls=%async_computation.1 | async-start | bytes 12582912 | tf_op jit(solution)/shard_map/all_to_all | solution.py:127
  415.6 0.0 copy-done.2
  415.7 46.1 %shard_map.37.own_ref = bf16[2,6144,256]{2,1,0:T(8,128)(2,1)S(1)} custom-call(s32[1,6144]{1,0:T(1,128)S(1)} %bitcast.6, bf16[16,2,384,256]{3,2,1,0:T(8,128)(2,1)} %all-to-all-done.own_ref), custom_call_target="tpu_custom_call" | custom-call | flops 38654705664 | bytes 12582912 | tf_op jit(solution)/shard_map/pallas_call | solution.py:58
  461.8 0.0 copy-start
  461.8 2.7 copy-done
  464.5 95.9 %all-to-all-done.1.partner_ref = bf16[16,2,384,256]{3,2,1,0:T(8,128)(2,1)} async-done(((bf16[16,2,384,256]{3,2,1,0:T(8,128)(2,1)}), bf16[16,2,384,256]{3,2,1,0:T(8,128)(2,1)}, u32[]{:S(2)}, u32[]{:S(2)}) %all-to-all-start.1) | async-done | bytes 6291488 | tf_op jit(solution)/shard_map/all_to_all | solution.py:127
  560.4 0.0 copy-start.1
  560.4 2.8 copy-done.1
  563.2 8.1 %shard_map.39 = f32[256,512]{1,0:T(8,128)S(1)} custom-call(bf16[2,6144,256]{2,1,0:T(8,128)(2,1)S(1)} %copy-done.1, bf16[16,2,384,256]{3,2,1,0:T(8,128)(2,1)} %all-to-all-done.1.partner_ref), custom_call_target="tpu_custom_call" | custom-call | flops 3221225472 | bytes 12582912 | tf_op jit(solution)/shard_map/pallas_call | solution.py:102
  571.3 22.8 %all_to_all.19 = f32[16,16,512]{2,1,0:T(8,128)S(1)} all-to-all(f32[16,16,512]{2,1,0:T(8,128)S(1)} %bitcast.5), channel_id=1, replica_groups=mesh['ka'=16,'pw'=16] {'pw'}, dimensions={0} | all-to-all | bytes 1048576 | tf_op jit(solution)/shard_map/all_to_all | solution.py:130
  594.1 0.3 reshape.11
  594.4 1.1 copy.7
  (1 shorter events, 0.0 us)
Async XLA Ops:
  0.0 11.1 %copy-start.3 = (s32[16]{0:T(128)S(1)}, s32[16]{0:T(128)}, u32[]{:S(2)}) copy-start(s32[16]{0:T(128)} %param.4) | copy-start | bytes 196
  0.0 406.8 %all-to-all-start = ((bf16[16,2,384,256]{3,2,1,0:T(8,128)(2,1)}), bf16[16,2,384,256]{3,2,1,0:T(8,128)(2,1)}, u32[]{:S(2)}, u32[]{:S(2)}) async-start(bf16[16,2,384,256]{3,2,1,0:T(8,128)(2,1)} %param.3), calls=%async_computation | async-start | bytes 12582912 | tf_op jit(solution)/shard_map/all_to_all | solution.py:125
  10.3 203.9 %collective-permute-start = (bf16[16,2,384,256]{3,2,1,0:T(8,128)(2,1)}, bf16[16,2,384,256]{3,2,1,0:T(8,128)(2,1)}, u32[]{:S(2)}, u32[]{:S(2)}) collective-permute-start(bf16[16,2,384,256]{3,2,1,0:T(8,128)(2,1)} %param.3), channel_id=1, source_target_pairs={{32,0},{48,16},{64,32},{80,48},{96,64},{112,80},{128,96},{144,112}... | collective-permute-start | bytes 18874376 | tf_op jit(solution)/shard_map/ppermute | solution.py:124
  406.8 8.9 %copy-start.2 = (s32[6144]{0:T(1024)S(1)}, s32[6144]{0:T(1024)}, u32[]{:S(2)}) copy-start(s32[6144]{0:T(1024)} %param.5) | copy-start | bytes 73732
  406.8 153.6 %all-to-all-start.1 = ((bf16[16,2,384,256]{3,2,1,0:T(8,128)(2,1)}), bf16[16,2,384,256]{3,2,1,0:T(8,128)(2,1)}, u32[]{:S(2)}, u32[]{:S(2)}) async-start(bf16[16,2,384,256]{3,2,1,0:T(8,128)(2,1)} %shard_map.38), calls=%async_computation.1 | async-start | bytes 12582912 | tf_op jit(solution)/shard_map/all_to_all | solution.py:127
  461.8 2.7 copy-start
  560.4 2.8 copy-start.1

commit v2 on v1

v2 whole, which is shorter than its diff:
```python
import jax
import jax.numpy as jnp
from jax import lax
from jax.experimental import pallas as pl
from jax.experimental.pallas import tpu as pltpu
from jax.sharding import PartitionSpec as P

SHIFT_DEV = 2


def reorder_kernel(order, source, result):
    result[...] = source[...]


def reordered(source, order):
    block = (1,) + source.shape[1:]
    return pl.pallas_call(
        reorder_kernel,
        grid_spec=pltpu.PrefetchScalarGridSpec(
            num_scalar_prefetch=1,
            grid=(source.shape[0],),
            in_specs=[pl.BlockSpec(block, lambda i, order: (order[i], 0, 0))],
            out_specs=pl.BlockSpec(block, lambda i, order: (i, 0, 0)),
        ),
        out_shape=jax.ShapeDtypeStruct(source.shape, source.dtype),
        cost_estimate=pl.CostEstimate(flops=0, bytes_accessed=4 * source.size, transcendentals=0),
    )(order, source)


def scatter_rows_kernel(target_ref, own_ref, out_ref):
    sources, parts, rows, bands = own_ref.shape
    height = out_ref.shape[1]
    first = pl.program_id(0) * height
    pair = 2
    wanted = first + lax.broadcasted_iota(jnp.int32, (height, pair * rows), 0)
    totals = [jnp.zeros((height, bands), jnp.float32) for _ in range(parts)]
    for s in range(0, sources, pair):
        hot = (target_ref[:, s * rows : (s + pair) * rows] == wanted).astype(jnp.bfloat16)
        for c in range(parts):
            block = own_ref[s : s + pair, c].reshape(pair * rows, bands)
            totals[c] += jnp.dot(hot, block, preferred_element_type=jnp.float32)
    for c in range(parts):
        out_ref[c] = totals[c].astype(out_ref.dtype)


def scattered_rows(own, target):
    sources, parts, rows, bands = own.shape
    total = sources * rows
    height = 256
    return pl.pallas_call(
        scatter_rows_kernel,
        grid=(total // height,),
        in_specs=[
            pl.BlockSpec((1, total), lambda i: (0, 0)),
            pl.BlockSpec(own.shape, lambda i: (0, 0, 0, 0), pipeline_mode=pl.Buffered(1)),
        ],
        out_specs=pl.BlockSpec((parts, height, bands), lambda i: (0, i, 0)),
        out_shape=jax.ShapeDtypeStruct((parts, total, bands), own.dtype),
        compiler_params=pltpu.CompilerParams(vmem_limit_bytes=40 << 20),
        cost_estimate=pl.CostEstimate(
            flops=2 * total * total * parts * bands, bytes_accessed=4 * own.size, transcendentals=0
        ),
    )(target.reshape(1, total), own)


def plane_products(own_ref, partner_ref):
    sources, rows, bands = partner_ref.shape
    partner = partner_ref[...].reshape(sources * rows, bands)
    return [
        lax.dot_general(
            own_ref[c], partner, (((0,), (0,)), ((), ())), preferred_element_type=jnp.float32
        )
        for c in range(2)
    ]


def first_plane_kernel(own_ref, partner_ref, out_ref):
    @pl.when(pl.program_id(0) == 0)
    def _():
        out_ref[...] = jnp.zeros_like(out_ref)

    real, imag = plane_products(own_ref, partner_ref)
    out_ref[0] += real
    out_ref[1] -= imag


def second_plane_kernel(own_ref, partner_ref, first_ref, out_ref, acc_ref):
    step = pl.program_id(0)

    @pl.when(step == 0)
    def _():
        acc_ref[...] = first_ref[...]

    imag, real = plane_products(own_ref, partner_ref)
    acc_ref[0] += real
    acc_ref[1] += imag

    @pl.when(step == pl.num_programs(0) - 1)
    def _():
        bands = acc_ref.shape[1]
        for d in range(2):
            out_ref[:, d * bands : (d + 1) * bands] = acc_ref[d]


TAKE = 2


def pair_specs(own, partner):
    sources, rows, bands = partner.shape
    specs = [
        pl.BlockSpec((own.shape[0], TAKE * rows, bands), lambda i: (0, i, 0)),
        pl.BlockSpec((TAKE, rows, bands), lambda i: (i, 0, 0)),
    ]
    cost = pl.CostEstimate(
        flops=4 * sources * rows * bands * bands, bytes_accessed=6 * partner.size, transcendentals=0
    )
    return (sources // TAKE,), specs, cost


def first_plane(own, partner):
    grid, specs, cost = pair_specs(own, partner)
    bands = own.shape[-1]
    return pl.pallas_call(
        first_plane_kernel,
        grid=grid,
        in_specs=specs,
        out_specs=pl.BlockSpec((2, bands, bands), lambda i: (0, 0, 0)),
        out_shape=jax.ShapeDtypeStruct((2, bands, bands), jnp.float32),
        compiler_params=pltpu.CompilerParams(vmem_limit_bytes=32 << 20),
        cost_estimate=cost,
    )(own, partner)


def second_plane(own, partner, first):
    grid, specs, cost = pair_specs(own, partner)
    bands = own.shape[-1]
    return pl.pallas_call(
        second_plane_kernel,
        grid=grid,
        in_specs=specs + [pl.BlockSpec(first.shape, lambda i: (0, 0, 0))],
        out_specs=pl.BlockSpec((bands, 2 * bands), lambda i: (0, 0)),
        out_shape=jax.ShapeDtypeStruct((bands, 2 * bands), jnp.float32),
        scratch_shapes=[pltpu.VMEM(first.shape, jnp.float32)],
        compiler_params=pltpu.CompilerParams(vmem_limit_bytes=32 << 20),
        cost_estimate=cost,
    )(own, partner, first)


def on_device(coeffs, neighbour, gshift):
    slab_points, parts, rows, bands = coeffs.shape
    ka_count = lax.axis_size("ka")
    wrapped = lax.axis_index("ka") >= ka_count - SHIFT_DEV
    route = [((i + SHIFT_DEV) % ka_count, i) for i in range(ka_count)]

    def spread(block):
        return lax.all_to_all(block, "pw", split_axis=0, concat_axis=0, tiled=True)

    order = neighbour % slab_points
    own = spread(coeffs)
    arrived = [lax.ppermute(coeffs[:, c], "ka", route) for c in range(parts)]
    waiting = [reordered(plane, order) for plane in arrived]
    own, waiting[0] = lax.optimization_barrier((own, waiting[0]))
    real = spread(waiting[0])
    target = jnp.where(wrapped, gshift, lax.iota(jnp.int32, gshift.shape[0]))
    moved = scattered_rows(own, target)
    real, moved, waiting[1] = lax.optimization_barrier((real, moved, waiting[1]))
    imag = spread(waiting[1])
    first = first_plane(moved, real)
    products = second_plane(moved, imag, first)
    products = spread(products).reshape(slab_points, bands // slab_points, 2, bands)
    return jnp.transpose(products, (1, 0, 2, 3))


def solution(mesh):
    placed = (P("ka", None, "pw", None), P("ka"), P())
    return jax.shard_map(
        on_device, mesh=mesh, in_specs=placed, out_specs=P("pw", "ka", None, None), check_vma=False
    )
```

time: 597 us -> 422 us (0.71)
  Pallas kernels: 247 us -> 77.6 us
  waiting for transfers between devices: 299 us -> 271 us
  local copies, waits for them, and re-layouts: 6.86 us -> 18.1 us
  starting transfers between devices: 20 us -> 29.4 us
    pallas_call x1 -> x2, Pallas kernels: 192 us -> 21 us  [reordered(): pl.pallas_call(reorder_kernel, grid_spec=pltpu.PrefetchScalarGridSpec(num...]
    ppermute x1 -> x2, waiting for transfers between devices: 203 us -> 185 us  [on_device(): arrived = [lax.ppermute(coeffs[:, c], 'ka', route) for c in range(parts)]]
    all_to_all x2 -> x3, waiting for transfers between devices: 95.9 us -> 85.9 us  [spread(): return lax.all_to_all(block, 'pw', split_axis=0, concat_axis=0, tiled=True)]
    all_to_all x2 -> x3, starting transfers between devices: 19.2 us -> 28.2 us  [spread(): return lax.all_to_all(block, 'pw', split_axis=0, concat_axis=0, tiled=True)]
    unnamed x8 -> x16, local copies, waits for them, and re-layouts: 5.46 us -> 11.7 us
  transfers between devices with their start and end apart: 3 -> 5, of which waited for: 2 -> 4; matrix products, arithmetic and copies ran while one was open for 0% -> 1% of each run, Pallas kernels for 40% -> 17%
where the time goes in v2:
time: 422 us; the launch traced here: 419 us
  waiting for transfers between devices  271 us (64%)
  Pallas kernels  77.6 us (18%)
  starting transfers between devices  29.4 us (7%)
  blocking collectives  22.1 us (5%)
  local copies, waits for them, and re-layouts  18.1 us (4%)
    ppermute x2, waiting for transfers between devices, on_device(): arrived = [lax.ppermute(coeffs[:, c], 'ka', route) for c in range(parts)]  185 us
    all_to_all x3, waiting for transfers between devices, spread(): return lax.all_to_all(block, 'pw', split_axis=0, concat_axis=0, tiled=True)  85.9 us
    pallas_call x1, Pallas kernels, scattered_rows(): pl.pallas_call(scatter_rows_kernel, grid=(total // height,), in_specs=[pl...  46.1 us
    all_to_all x3, starting transfers between devices, spread(): return lax.all_to_all(block, 'pw', split_axis=0, concat_axis=0, tiled=True)  28.2 us
    all_to_all x1, blocking collectives, spread(): return lax.all_to_all(block, 'pw', split_axis=0, concat_axis=0, tiled=True)  22.1 us
    pallas_call x2, Pallas kernels, reordered(): pl.pallas_call(reorder_kernel, grid_spec=pltpu.PrefetchScalarGridSpec(num...  21 us
    unnamed x16, local copies, waits for them, and re-layouts  11.7 us
  transfers between devices with their start and end apart: 5, of which 4 were waited for; matrix products, arithmetic and copies ran while one was open for 1% of the time, Pallas kernels for 17%

profile of v2, /device:TPU:26, one launch (start us, length us, event | category | flops | bytes accessed | tf_op | source)
XLA Modules:
  0.0 419.0 jit_solution(7496127645213118467)
XLA Ops:
  0.0 10.2 %all-to-all-start = ((bf16[16,2,384,256]{3,2,1,0:T(8,128)(2,1)}), bf16[16,2,384,256]{3,2,1,0:T(8,128)(2,1)}, u32[]{:S(2)}, u32[]{:S(2)}) async-start(bf16[16,2,384,256]{3,2,1,0:T(8,128)(2,1)} %param.3), calls=%async_computation | async-start | bytes 12582912 | tf_op jit(solution)/shard_map/all_to_all | solution.py:156
  10.2 0.0 copy-start.7
  10.2 5.0 %slice_bitcast_fusion = (bf16[16,384,256]{2,1,0:T(8,128)(2,1)}, bf16[16,384,256]{2,1,0:T(8,128)(2,1)S(1)}) fusion(bf16[16,2,384,256]{3,2,1,0:T(8,128)(2,1)} %param.3), kind=kLoop, calls=%fused_computation | loop fusion | bytes 12582912 | tf_op jit(solution)/shard_map/squeeze | solution.py:160
  15.2 0.7 collective-permute-start
  16.0 0.4 collective-permute-start.1
  16.4 0.0 copy-done.7
  16.4 0.5 and_select_fusion.order
  16.9 106.3 %collective-permute-done.source = bf16[16,384,256]{2,1,0:T(8,128)(2,1)S(1)} collective-permute-done((bf16[16,384,256]{2,1,0:T(8,128)(2,1)S(1)}, bf16[16,384,256]{2,1,0:T(8,128)(2,1)S(1)}, u32[]{:S(2)}, u32[]{:S(2)}) %collective-permute-start) | collective-permute-done | bytes 3145760 | tf_op jit(solution)/shard_map/ppermute | solution.py:160
  123.2 1.6 copy-done.5
  124.9 10.5 %shard_map.37 = bf16[16,384,256]{2,1,0:T(8,128)(2,1)} custom-call(s32[16]{0:T(128)} %and_select_fusion.order, bf16[16,384,256]{2,1,0:T(8,128)(2,1)} %copy-done.5), custom_call_target="tpu_custom_call" | custom-call | bytes 6291456 | tf_op jit(solution)/shard_map/pallas_call | solution.py:17
  135.4 21.6 %all-to-all-done.own_ref = bf16[16,2,384,256]{3,2,1,0:T(8,128)(2,1)} async-done(((bf16[16,2,384,256]{3,2,1,0:T(8,128)(2,1)}), bf16[16,2,384,256]{3,2,1,0:T(8,128)(2,1)}, u32[]{:S(2)}, u32[]{:S(2)}) %all-to-all-start) | async-done | bytes 6291488 | tf_op jit(solution)/shard_map/all_to_all | solution.py:156
  157.0 8.4 %all-to-all-start.1 = ((bf16[16,384,256]{2,1,0:T(8,128)(2,1)}), bf16[16,384,256]{2,1,0:T(8,128)(2,1)S(1)}, u32[]{:S(2)}, u32[]{:S(2)}) async-start(bf16[16,384,256]{2,1,0:T(8,128)(2,1)} %shard_map.37), calls=%async_computation.1 | async-start | bytes 6291456 | tf_op jit(solution)/shard_map/all_to_all | solution.py:156
  165.4 0.0 copy-done.6
  165.4 79.0 %collective-permute-done.1.source = bf16[16,384,256]{2,1,0:T(8,128)(2,1)} collective-permute-done((bf16[16,384,256]{2,1,0:T(8,128)(2,1)}, bf16[16,384,256]{2,1,0:T(8,128)(2,1)}, u32[]{:S(2)}, u32[]{:S(2)}) %collective-permute-start.1) | collective-permute-done | bytes 3145760 | tf_op jit(solution)/shard_map/ppermute | solution.py:160
  244.4 10.5 %shard_map.39 = bf16[16,384,256]{2,1,0:T(8,128)(2,1)} custom-call(s32[16]{0:T(128)} %and_select_fusion.order, bf16[16,384,256]{2,1,0:T(8,128)(2,1)} %collective-permute-done.1.source), custom_call_target="tpu_custom_call" | custom-call | bytes 6291456 | tf_op jit(solution)/shard_map/pallas_call | solution.py:17
  254.9 46.1 %shard_map.38.own_ref = bf16[2,6144,256]{2,1,0:T(8,128)(2,1)S(1)} custom-call(s32[1,6144]{1,0:T(1,128)S(1)} %bitcast.14, bf16[16,2,384,256]{3,2,1,0:T(8,128)(2,1)} %all-to-all-done.own_ref), custom_call_target="tpu_custom_call" | custom-call | flops 38654705664 | bytes 12582912 | tf_op jit(solution)/shard_map/pallas_call | solution.py:50
  301.0 0.0 copy-start
  301.0 2.7 copy-done
  303.6 0.0 all-to-all-done.1.partner_ref
  303.6 9.6 %all-to-all-start.2 = ((bf16[16,384,256]{2,1,0:T(8,128)(2,1)}), bf16[16,384,256]{2,1,0:T(8,128)(2,1)}, u32[]{:S(2)}, u32[]{:S(2)}) async-start(bf16[16,384,256]{2,1,0:T(8,128)(2,1)} %shard_map.39), calls=%async_computation.2 | async-start | bytes 6291456 | tf_op jit(solution)/shard_map/all_to_all | solution.py:156
  313.3 0.0 copy-start.1
  313.3 2.8 copy-done.1
  316.1 3.9 shard_map.40.first_ref
  320.0 0.0 copy-start.3
  320.0 0.8 copy-done.3
  320.8 64.3 %all-to-all-done.2.partner_ref = bf16[16,384,256]{2,1,0:T(8,128)(2,1)} async-done(((bf16[16,384,256]{2,1,0:T(8,128)(2,1)}), bf16[16,384,256]{2,1,0:T(8,128)(2,1)}, u32[]{:S(2)}, u32[]{:S(2)}) %all-to-all-start.2) | async-done | bytes 3145760 | tf_op jit(solution)/shard_map/all_to_all | solution.py:156
  385.1 2.8 copy-done.2
  387.9 1.0 copy-done.4
  388.9 6.5 %shard_map.41 = f32[256,512]{1,0:T(8,128)S(1)} custom-call(bf16[2,6144,256]{2,1,0:T(8,128)(2,1)S(1)} %copy-done.2, bf16[16,384,256]{2,1,0:T(8,128)(2,1)} %all-to-all-done.2.partner_ref, f32[2,256,256]{2,1,0:T(8,128)S(1)} %copy-done.4), custom_call_target="tpu_custom_call" | custom-call | flops 1610612736 | bytes 9437184 | tf_op jit(solution)/shard_map/pallas_call | solution.py:137
  395.5 22.1 %all_to_all.24 = f32[16,16,512]{2,1,0:T(8,128)S(1)} all-to-all(f32[16,16,512]{2,1,0:T(8,128)S(1)} %bitcast.13), channel_id=1, replica_groups=mesh['ka'=16,'pw'=16] {'pw'}, dimensions={0} | all-to-all | bytes 1048576 | tf_op jit(solution)/shard_map/all_to_all | solution.py:156
  417.6 0.3 reshape.11
  417.9 1.1 copy.11
  (5 shorter events, 0.0 us)
Async XLA Ops:
  0.0 157.0 %all-to-all-start = ((bf16[16,2,384,256]{3,2,1,0:T(8,128)(2,1)}), bf16[16,2,384,256]{3,2,1,0:T(8,128)(2,1)}, u32[]{:S(2)}, u32[]{:S(2)}) async-start(bf16[16,2,384,256]{3,2,1,0:T(8,128)(2,1)} %param.3), calls=%async_computation | async-start | bytes 12582912 | tf_op jit(solution)/shard_map/all_to_all | solution.py:156
  10.2 6.2 %copy-start.7 = (s32[16]{0:T(128)S(1)}, s32[16]{0:T(128)}, u32[]{:S(2)}) copy-start(s32[16]{0:T(128)} %param.4) | copy-start | bytes 196
  15.2 108.0 %collective-permute-start = (bf16[16,384,256]{2,1,0:T(8,128)(2,1)S(1)}, bf16[16,384,256]{2,1,0:T(8,128)(2,1)S(1)}, u32[]{:S(2)}, u32[]{:S(2)}) collective-permute-start(bf16[16,384,256]{2,1,0:T(8,128)(2,1)S(1)} %get-tuple-element.16), channel_id=1, source_target_pairs={{32,0},{48,16},{64,32},{80,48},{96,64},{112,80},{128,96},{144,112}... | collective-permute-start | bytes 9437192 | tf_op jit(solution)/shard_map/ppermute | solution.py:160
  16.0 228.4 %collective-permute-start.1 = (bf16[16,384,256]{2,1,0:T(8,128)(2,1)}, bf16[16,384,256]{2,1,0:T(8,128)(2,1)}, u32[]{:S(2)}, u32[]{:S(2)}) collective-permute-start(bf16[16,384,256]{2,1,0:T(8,128)(2,1)} %get-tuple-element.15), channel_id=1, source_target_pairs={{32,0},{48,16},{64,32},{80,48},{96,64},{112,80},{128,96},{144,112}... | collective-permute-start | bytes 9437192 | tf_op jit(solution)/shard_map/ppermute | solution.py:160
  123.2 1.6 copy-start.5
  135.4 29.9 %copy-start.6 = (s32[6144]{0:T(1024)S(1)}, s32[6144]{0:T(1024)}, u32[]{:S(2)}) copy-start(s32[6144]{0:T(1024)} %param.5) | copy-start | bytes 73732
  157.0 146.7 %all-to-all-start.1 = ((bf16[16,384,256]{2,1,0:T(8,128)(2,1)}), bf16[16,384,256]{2,1,0:T(8,128)(2,1)S(1)}, u32[]{:S(2)}, u32[]{:S(2)}) async-start(bf16[16,384,256]{2,1,0:T(8,128)(2,1)} %shard_map.37), calls=%async_computation.1 | async-start | bytes 6291456 | tf_op jit(solution)/shard_map/all_to_all | solution.py:156
  301.0 2.7 copy-start
  303.6 81.5 %all-to-all-start.2 = ((bf16[16,384,256]{2,1,0:T(8,128)(2,1)}), bf16[16,384,256]{2,1,0:T(8,128)(2,1)}, u32[]{:S(2)}, u32[]{:S(2)}) async-start(bf16[16,384,256]{2,1,0:T(8,128)(2,1)} %shard_map.39), calls=%async_computation.2 | async-start | bytes 6291456 | tf_op jit(solution)/shard_map/all_to_all | solution.py:156
  313.3 2.8 copy-start.1
  320.0 0.8 copy-start.3
  385.1 2.8 copy-start.2
  387.9 1.0 copy-start.4

commit v3 on v2

--- a/solution.py
+++ b/solution.py
@@ -8,21 +8,41 @@
 SHIFT_DEV = 2
 
 
-def reorder_kernel(order, source, result):
-    result[...] = source[...]
+def reorder_kernel(order, source, result, held, read, written):
+    count = result.shape[0]
+
+    def fetch(i):
+        return pltpu.make_async_copy(source.at[order[i]], held.at[i], read.at[i])
+
+    def store(i):
+        return pltpu.make_async_copy(held.at[i], result.at[i], written.at[i])
+
+    for i in range(count):
+        fetch(i).start()
+    for i in range(count):
+        fetch(i).wait()
+        store(i).start()
+    for i in range(count):
+        store(i).wait()
 
 
 def reordered(source, order):
-    block = (1,) + source.shape[1:]
+    count = source.shape[0]
     return pl.pallas_call(
         reorder_kernel,
         grid_spec=pltpu.PrefetchScalarGridSpec(
             num_scalar_prefetch=1,
-            grid=(source.shape[0],),
-            in_specs=[pl.BlockSpec(block, lambda i, order: (order[i], 0, 0))],
-            out_specs=pl.BlockSpec(block, lambda i, order: (i, 0, 0)),
+            grid=(),
+            in_specs=[pl.BlockSpec(memory_space=pltpu.HBM)],
+            out_specs=pl.BlockSpec(memory_space=pltpu.HBM),
+            scratch_shapes=[
+                pltpu.VMEM(source.shape, source.dtype),
+                pltpu.SemaphoreType.DMA((count,)),
+                pltpu.SemaphoreType.DMA((count,)),
+            ],
         ),
         out_shape=jax.ShapeDtypeStruct(source.shape, source.dtype),
+        compiler_params=pltpu.CompilerParams(vmem_limit_bytes=32 << 20),
         cost_estimate=pl.CostEstimate(flops=0, bytes_accessed=4 * source.size, transcendentals=0),
     )(order, source)
 
@@ -158,13 +178,15 @@
     order = neighbour % slab_points
     own = spread(coeffs)
     arrived = [lax.ppermute(coeffs[:, c], "ka", route) for c in range(parts)]
-    waiting = [reordered(plane, order) for plane in arrived]
-    own, waiting[0] = lax.optimization_barrier((own, waiting[0]))
-    real = spread(waiting[0])
+    waiting = reordered(arrived[0], order)
+    own, waiting = lax.optimization_barrier((own, waiting))
+    real = spread(waiting)
     target = jnp.where(wrapped, gshift, lax.iota(jnp.int32, gshift.shape[0]))
-    moved = scattered_rows(own, target)
-    real, moved, waiting[1] = lax.optimization_barrier((real, moved, waiting[1]))
-    imag = spread(waiting[1])
+    moved = pltpu.with_memory_space_constraint(scattered_rows(own, target), pltpu.HBM)
+    moved, late = lax.optimization_barrier((moved, arrived[1]))
+    waiting = reordered(late, order)
+    real, waiting = lax.optimization_barrier((real, waiting))
+    imag = spread(waiting)
     first = first_plane(moved, real)
     products = second_plane(moved, imag, first)
     products = spread(products).reshape(slab_points, bands // slab_points, 2, bands)

time: 422 us -> 388 us (0.919)
  waiting for transfers between devices: 271 us -> 248 us
    ppermute x2, waiting for transfers between devices: 185 us -> 159 us  [on_device(): arrived = [lax.ppermute(coeffs[:, c], 'ka', route) for c in range(parts)]]
    pallas_call x2, Pallas kernels: 21 us -> 14.8 us  [reordered(): pl.pallas_call(reorder_kernel, grid_spec=pltpu.PrefetchScalarGridSpec(num...]
    unnamed x16 -> x14, local copies, waits for them, and re-layouts: 11.7 us -> 7.83 us
  transfers between devices with their start and end apart: 5 -> 5, of which waited for: 4 -> 4; matrix products, arithmetic and copies ran while one was open for 1% -> 1% of each run, Pallas kernels for 17% -> 18%
where the time goes in v3:
time: 388 us; the launch traced here: 386 us
  waiting for transfers between devices  248 us (64%)
  Pallas kernels  75.3 us (19%)
  starting transfers between devices  26.8 us (7%)
  blocking collectives  22.1 us (6%)
  local copies, waits for them, and re-layouts  14.3 us (4%)
    ppermute x2, waiting for transfers between devices, on_device(): arrived = [lax.ppermute(coeffs[:, c], 'ka', route) for c in range(parts)]  159 us
    all_to_all x3, waiting for transfers between devices, spread(): return lax.all_to_all(block, 'pw', split_axis=0, concat_axis=0, tiled=True)  89.2 us
    pallas_call x1, Pallas kernels, scattered_rows(): pl.pallas_call(scatter_rows_kernel, grid=(total // height,), in_specs=[pl...  46.1 us
    all_to_all x3, starting transfers between devices, spread(): return lax.all_to_all(block, 'pw', split_axis=0, concat_axis=0, tiled=True)  25.2 us
    all_to_all x1, blocking collectives, spread(): return lax.all_to_all(block, 'pw', split_axis=0, concat_axis=0, tiled=True)  22.1 us
    pallas_call x2, Pallas kernels, reordered(): pl.pallas_call(reorder_kernel, grid_spec=pltpu.PrefetchScalarGridSpec(num...  14.8 us
    unnamed x14, local copies, waits for them, and re-layouts  7.83 us
  transfers between devices with their start and end apart: 5, of which 4 were waited for; matrix products, arithmetic and copies ran while one was open for 1% of the time, Pallas kernels for 18%

profile of v3, /device:TPU:26, one launch (start us, length us, event | category | flops | bytes accessed | tf_op | source)
XLA Modules:
  0.0 386.4 jit_solution(14744782242906575237)
XLA Ops:
  0.0 10.2 %all-to-all-start = ((bf16[16,2,384,256]{3,2,1,0:T(8,128)(2,1)}), bf16[16,2,384,256]{3,2,1,0:T(8,128)(2,1)}, u32[]{:S(2)}, u32[]{:S(2)}) async-start(bf16[16,2,384,256]{3,2,1,0:T(8,128)(2,1)} %param.3), calls=%async_computation | async-start | bytes 12582912 | tf_op jit(solution)/shard_map/all_to_all | solution.py:176
  10.2 0.0 copy-start.6
  10.2 5.0 %slice_bitcast_fusion = (bf16[16,384,256]{2,1,0:T(8,128)(2,1)}, bf16[16,384,256]{2,1,0:T(8,128)(2,1)S(1)}) fusion(bf16[16,2,384,256]{3,2,1,0:T(8,128)(2,1)} %param.3), kind=kLoop, calls=%fused_computation | loop fusion | bytes 12582912 | tf_op jit(solution)/shard_map/squeeze | solution.py:180
  15.2 0.7 collective-permute-start
  16.0 0.0 copy-done.6
  16.0 106.4 %collective-permute-done.source = bf16[16,384,256]{2,1,0:T(8,128)(2,1)S(1)} collective-permute-done((bf16[16,384,256]{2,1,0:T(8,128)(2,1)S(1)}, bf16[16,384,256]{2,1,0:T(8,128)(2,1)S(1)}, u32[]{:S(2)}, u32[]{:S(2)}) %collective-permute-start) | collective-permute-done | bytes 3145760 | tf_op jit(solution)/shard_map/ppermute | solution.py:180
  122.4 9.0 %shard_map.37 = bf16[16,384,256]{2,1,0:T(8,128)(2,1)S(1)} custom-call(s32[16]{0:T(128)S(1)} %and_select_fusion.order, bf16[16,384,256]{2,1,0:T(8,128)(2,1)S(1)} %collective-permute-done.source), custom_call_target="tpu_custom_call" | custom-call | bytes 6291456 | tf_op jit(solution)/shard_map/pallas_call | solution.py:31
  131.5 0.0 copy-start.1
  131.5 1.7 copy-done.1
  133.2 0.0 copy-start.5
  133.2 23.8 %all-to-all-done.own_ref = bf16[16,2,384,256]{3,2,1,0:T(8,128)(2,1)} async-done(((bf16[16,2,384,256]{3,2,1,0:T(8,128)(2,1)}), bf16[16,2,384,256]{3,2,1,0:T(8,128)(2,1)}, u32[]{:S(2)}, u32[]{:S(2)}) %all-to-all-start) | async-done | bytes 6291488 | tf_op jit(solution)/shard_map/all_to_all | solution.py:176
  157.0 5.9 %all-to-all-start.1 = ((bf16[16,384,256]{2,1,0:T(8,128)(2,1)}), bf16[16,384,256]{2,1,0:T(8,128)(2,1)S(1)}, u32[]{:S(2)}, u32[]{:S(2)}) async-start(bf16[16,384,256]{2,1,0:T(8,128)(2,1)} %copy-done.1), calls=%async_computation.1 | async-start | bytes 6291456 | tf_op jit(solution)/shard_map/all_to_all | solution.py:176
  162.9 0.8 collective-permute-start.1
  163.7 0.0 copy-done.5
  163.7 46.1 %shard_map.38.own_ref = bf16[2,6144,256]{2,1,0:T(8,128)(2,1)S(1)} custom-call(s32[1,6144]{1,0:T(1,128)S(1)} %bitcast.14, bf16[16,2,384,256]{3,2,1,0:T(8,128)(2,1)} %all-to-all-done.own_ref), custom_call_target="tpu_custom_call" | custom-call | flops 38654705664 | bytes 12582912 | tf_op jit(solution)/shard_map/pallas_call | solution.py:70
  209.9 0.0 copy-start
  209.9 2.6 copy-done
  212.5 52.2 %collective-permute-done.1.source = bf16[16,384,256]{2,1,0:T(8,128)(2,1)} collective-permute-done((bf16[16,384,256]{2,1,0:T(8,128)(2,1)}, bf16[16,384,256]{2,1,0:T(8,128)(2,1)}, u32[]{:S(2)}, u32[]{:S(2)}) %collective-permute-start.1) | collective-permute-done | bytes 3145760 | tf_op jit(solution)/shard_map/ppermute | solution.py:180
  264.7 5.8 %shard_map.39 = bf16[16,384,256]{2,1,0:T(8,128)(2,1)S(1)} custom-call(s32[16]{0:T(128)S(1)} %and_select_fusion.order, bf16[16,384,256]{2,1,0:T(8,128)(2,1)} %collective-permute-done.1.source), custom_call_target="tpu_custom_call" | custom-call | bytes 6291456 | tf_op jit(solution)/shard_map/pallas_call | solution.py:31
  270.5 0.0 copy-start.2
  270.5 1.6 copy-done.2
  272.2 0.0 all-to-all-done.1.partner_ref
  272.2 9.1 %all-to-all-start.2 = ((bf16[16,384,256]{2,1,0:T(8,128)(2,1)}), bf16[16,384,256]{2,1,0:T(8,128)(2,1)}, u32[]{:S(2)}, u32[]{:S(2)}) async-start(bf16[16,384,256]{2,1,0:T(8,128)(2,1)} %copy-done.2), calls=%async_computation.2 | async-start | bytes 6291456 | tf_op jit(solution)/shard_map/all_to_all | solution.py:176
  281.3 6.9 %shard_map.40.first_ref = f32[2,256,256]{2,1,0:T(8,128)S(1)} custom-call(bf16[2,6144,256]{2,1,0:T(8,128)(2,1)} %copy-done, bf16[16,384,256]{2,1,0:T(8,128)(2,1)S(1)} %all-to-all-done.1.partner_ref), custom_call_target="tpu_custom_call" | custom-call | flops 1610612736 | bytes 9437184 | tf_op jit(solution)/shard_map/pallas_call | solution.py:143
  288.3 0.0 copy-start.3
  288.3 0.8 copy-done.3
  289.0 65.4 %all-to-all-done.2.partner_ref = bf16[16,384,256]{2,1,0:T(8,128)(2,1)} async-done(((bf16[16,384,256]{2,1,0:T(8,128)(2,1)}), bf16[16,384,256]{2,1,0:T(8,128)(2,1)}, u32[]{:S(2)}, u32[]{:S(2)}) %all-to-all-start.2) | async-done | bytes 3145760 | tf_op jit(solution)/shard_map/all_to_all | solution.py:176
  354.5 1.0 copy-done.4
  355.5 7.4 %shard_map.41 = f32[256,512]{1,0:T(8,128)S(1)} custom-call(bf16[2,6144,256]{2,1,0:T(8,128)(2,1)} %copy-done, bf16[16,384,256]{2,1,0:T(8,128)(2,1)} %all-to-all-done.2.partner_ref, f32[2,256,256]{2,1,0:T(8,128)S(1)} %copy-done.4), custom_call_target="tpu_custom_call" | custom-call | flops 1610612736 | bytes 9437184 | tf_op jit(solution)/shard_map/pallas_call | solution.py:157
  363.0 22.1 %all_to_all.24 = f32[16,16,512]{2,1,0:T(8,128)S(1)} all-to-all(f32[16,16,512]{2,1,0:T(8,128)S(1)} %bitcast.13), channel_id=1, replica_groups=mesh['ka'=16,'pw'=16] {'pw'}, dimensions={0} | all-to-all | bytes 1048576 | tf_op jit(solution)/shard_map/all_to_all | solution.py:176
  385.0 0.3 reshape.11
  385.4 1.1 copy.11
  (3 shorter events, 0.0 us)
Async XLA Ops:
  0.0 157.0 %all-to-all-start = ((bf16[16,2,384,256]{3,2,1,0:T(8,128)(2,1)}), bf16[16,2,384,256]{3,2,1,0:T(8,128)(2,1)}, u32[]{:S(2)}, u32[]{:S(2)}) async-start(bf16[16,2,384,256]{3,2,1,0:T(8,128)(2,1)} %param.3), calls=%async_computation | async-start | bytes 12582912 | tf_op jit(solution)/shard_map/all_to_all | solution.py:176
  10.2 5.8 %copy-start.6 = (s32[16]{0:T(128)S(1)}, s32[16]{0:T(128)}, u32[]{:S(2)}) copy-start(s32[16]{0:T(128)} %param.4) | copy-start | bytes 196
  15.2 107.2 %collective-permute-start = (bf16[16,384,256]{2,1,0:T(8,128)(2,1)S(1)}, bf16[16,384,256]{2,1,0:T(8,128)(2,1)S(1)}, u32[]{:S(2)}, u32[]{:S(2)}) collective-permute-start(bf16[16,384,256]{2,1,0:T(8,128)(2,1)S(1)} %get-tuple-element.18), channel_id=1, source_target_pairs={{32,0},{48,16},{64,32},{80,48},{96,64},{112,80},{128,96},{144,112}... | collective-permute-start | bytes 9437192 | tf_op jit(solution)/shard_map/ppermute | solution.py:180
  131.5 1.7 copy-start.1
  133.2 30.5 %copy-start.5 = (s32[6144]{0:T(1024)S(1)}, s32[6144]{0:T(1024)}, u32[]{:S(2)}) copy-start(s32[6144]{0:T(1024)} %param.5) | copy-start | bytes 73732
  157.0 115.2 %all-to-all-start.1 = ((bf16[16,384,256]{2,1,0:T(8,128)(2,1)}), bf16[16,384,256]{2,1,0:T(8,128)(2,1)S(1)}, u32[]{:S(2)}, u32[]{:S(2)}) async-start(bf16[16,384,256]{2,1,0:T(8,128)(2,1)} %copy-done.1), calls=%async_computation.1 | async-start | bytes 6291456 | tf_op jit(solution)/shard_map/all_to_all | solution.py:176
  162.9 101.8 %collective-permute-start.1 = (bf16[16,384,256]{2,1,0:T(8,128)(2,1)}, bf16[16,384,256]{2,1,0:T(8,128)(2,1)}, u32[]{:S(2)}, u32[]{:S(2)}) collective-permute-start(bf16[16,384,256]{2,1,0:T(8,128)(2,1)} %get-tuple-element.17), channel_id=1, source_target_pairs={{32,0},{48,16},{64,32},{80,48},{96,64},{112,80},{128,96},{144,112}... | collective-permute-start | bytes 9437192 | tf_op jit(solution)/shard_map/ppermute | solution.py:180
  209.9 2.7 copy-start
  270.5 1.6 copy-start.2
  272.2 82.3 %all-to-all-start.2 = ((bf16[16,384,256]{2,1,0:T(8,128)(2,1)}), bf16[16,384,256]{2,1,0:T(8,128)(2,1)}, u32[]{:S(2)}, u32[]{:S(2)}) async-start(bf16[16,384,256]{2,1,0:T(8,128)(2,1)} %copy-done.2), calls=%async_computation.2 | async-start | bytes 6291456 | tf_op jit(solution)/shard_map/all_to_all | solution.py:176
  288.3 0.8 copy-start.3
  354.5 1.0 copy-start.4

commit v4 on v3

--- a/solution.py
+++ b/solution.py
@@ -8,43 +8,50 @@
 SHIFT_DEV = 2
 
 
-def reorder_kernel(order, source, result, held, read, written):
+def reorder_kernel(order, relayed, *refs):
+    *sources, result, held, read, written = refs
     count = result.shape[0]
 
-    def fetch(i):
+    def fetch(source, i):
         return pltpu.make_async_copy(source.at[order[i]], held.at[i], read.at[i])
 
     def store(i):
         return pltpu.make_async_copy(held.at[i], result.at[i], written.at[i])
 
-    for i in range(count):
-        fetch(i).start()
-    for i in range(count):
-        fetch(i).wait()
-        store(i).start()
+    for choice, source in enumerate(sources):
+
+        @pl.when(relayed[0] == choice)
+        def _(source=source):
+            for i in range(count):
+                fetch(source, i).start()
+            for i in range(count):
+                fetch(source, i).wait()
+                store(i).start()
+
     for i in range(count):
         store(i).wait()
 
 
-def reordered(source, order):
-    count = source.shape[0]
+def reordered(order, relayed, *sources):
+    shape, dtype = sources[0].shape, sources[0].dtype
+    count = shape[0]
     return pl.pallas_call(
         reorder_kernel,
         grid_spec=pltpu.PrefetchScalarGridSpec(
-            num_scalar_prefetch=1,
+            num_scalar_prefetch=2,
             grid=(),
-            in_specs=[pl.BlockSpec(memory_space=pltpu.HBM)],
+            in_specs=[pl.BlockSpec(memory_space=pltpu.HBM)] * len(sources),
             out_specs=pl.BlockSpec(memory_space=pltpu.HBM),
             scratch_shapes=[
-                pltpu.VMEM(source.shape, source.dtype),
+                pltpu.VMEM(shape, dtype),
                 pltpu.SemaphoreType.DMA((count,)),
                 pltpu.SemaphoreType.DMA((count,)),
             ],
         ),
-        out_shape=jax.ShapeDtypeStruct(source.shape, source.dtype),
-        compiler_params=pltpu.CompilerParams(vmem_limit_bytes=32 << 20),
-        cost_estimate=pl.CostEstimate(flops=0, bytes_accessed=4 * source.size, transcendentals=0),
-    )(order, source)
+        out_shape=jax.ShapeDtypeStruct(shape, dtype),
+        compiler_params=pltpu.CompilerParams(vmem_limit_bytes=56 << 20),
+        cost_estimate=pl.CostEstimate(flops=0, bytes_accessed=4 * sources[0].size, transcendentals=0),
+    )(order, relayed, *sources)
 
 
 def scatter_rows_kernel(target_ref, own_ref, out_ref):
@@ -76,7 +83,7 @@
         ],
         out_specs=pl.BlockSpec((parts, height, bands), lambda i: (0, i, 0)),
         out_shape=jax.ShapeDtypeStruct((parts, total, bands), own.dtype),
-        compiler_params=pltpu.CompilerParams(vmem_limit_bytes=40 << 20),
+        compiler_params=pltpu.CompilerParams(vmem_limit_bytes=56 << 20),
         cost_estimate=pl.CostEstimate(
             flops=2 * total * total * parts * bands, bytes_accessed=4 * own.size, transcendentals=0
         ),
@@ -169,22 +176,29 @@
 def on_device(coeffs, neighbour, gshift):
     slab_points, parts, rows, bands = coeffs.shape
     ka_count = lax.axis_size("ka")
-    wrapped = lax.axis_index("ka") >= ka_count - SHIFT_DEV
-    route = [((i + SHIFT_DEV) % ka_count, i) for i in range(ka_count)]
+    here = lax.axis_index("ka")
+    wrapped = here >= ka_count - SHIFT_DEV
+    half = ka_count // 2
+    crosses = here % half >= half - SHIFT_DEV
 
     def spread(block):
         return lax.all_to_all(block, "pw", split_axis=0, concat_axis=0, tiled=True)
 
     order = neighbour % slab_points
     own = spread(coeffs)
-    arrived = [lax.ppermute(coeffs[:, c], "ka", route) for c in range(parts)]
-    waiting = reordered(arrived[0], order)
-    own, waiting = lax.optimization_barrier((own, waiting))
+    straight = [((i + SHIFT_DEV) % ka_count, i) for i in range(ka_count)]
+    around = [(i // half * half + (i + SHIFT_DEV) % half, i) for i in range(ka_count)]
+    swap = [((i + half) % ka_count, i) for i in range(ka_count) if i % half >= half - SHIFT_DEV]
+    direct = lax.ppermute(coeffs[:, 0], "ka", straight)
+    turned = lax.ppermute(coeffs[:, 1], "ka", around)
+    waiting = reordered(order, jnp.zeros((1,), jnp.int32), direct)
+    own, waiting, turned = lax.optimization_barrier((own, waiting, turned))
+    swapped = lax.ppermute(turned, "ka", swap)
     real = spread(waiting)
     target = jnp.where(wrapped, gshift, lax.iota(jnp.int32, gshift.shape[0]))
     moved = pltpu.with_memory_space_constraint(scattered_rows(own, target), pltpu.HBM)
-    moved, late = lax.optimization_barrier((moved, arrived[1]))
-    waiting = reordered(late, order)
+    moved, swapped = lax.optimization_barrier((moved, swapped))
+    waiting = reordered(order, crosses.astype(jnp.int32).reshape(1), turned, swapped)
     real, waiting = lax.optimization_barrier((real, waiting))
     imag = spread(waiting)
     first = first_plane(moved, real)

time: 388 us -> 387 us (level)
  Pallas kernels: 75.3 us -> 68.9 us
  waiting for transfers between devices: 248 us -> 253 us
  local copies, waits for them, and re-layouts: 14.3 us -> 9.92 us
    ppermute x2 -> x3, waiting for transfers between devices: 159 us -> 183 us  [the longest x1 107 us: on_device(): direct = lax.ppermute(coeffs[:, 0], 'ka', straight)]
    all_to_all x3, waiting for transfers between devices: 89.2 us -> 69.6 us  [spread(): return lax.all_to_all(block, 'pw', split_axis=0, concat_axis=0, tiled=True)]
    pallas_call x2, Pallas kernels: 14.8 us -> 7.7 us  [reordered(): pl.pallas_call(reorder_kernel, grid_spec=pltpu.PrefetchScalarGridSpec(num...]
    unnamed x14 -> x12, local copies, waits for them, and re-layouts: 7.83 us -> 5.13 us
  transfers between devices with their start and end apart: 5 -> 6, of which waited for: 4 -> 5; matrix products, arithmetic and copies ran while one was open for 1% -> 1% of each run, Pallas kernels for 18% -> 16%
where the time goes in v4:
time: 387 us; the launch traced here: 385 us
  waiting for transfers between devices  253 us (65%)
  Pallas kernels  68.9 us (18%)
  starting transfers between devices  29.8 us (8%)
  blocking collectives  22.1 us (6%)
  local copies, waits for them, and re-layouts  9.92 us (3%)
    ppermute x1, waiting for transfers between devices, on_device(): direct = lax.ppermute(coeffs[:, 0], 'ka', straight)  107 us
    all_to_all x3, waiting for transfers between devices, spread(): return lax.all_to_all(block, 'pw', split_axis=0, concat_axis=0, tiled=True)  69.6 us
    ppermute x1, waiting for transfers between devices, on_device(): swapped = lax.ppermute(turned, 'ka', swap)  51.3 us
    pallas_call x1, Pallas kernels, scattered_rows(): pl.pallas_call(scatter_rows_kernel, grid=(total // height,), in_specs=[pl...  46.8 us
    all_to_all x3, starting transfers between devices, spread(): return lax.all_to_all(block, 'pw', split_axis=0, concat_axis=0, tiled=True)  25.2 us
    ppermute x1, waiting for transfers between devices, on_device(): turned = lax.ppermute(coeffs[:, 1], 'ka', around)  24.8 us
    all_to_all x1, blocking collectives, spread(): return lax.all_to_all(block, 'pw', split_axis=0, concat_axis=0, tiled=True)  22.1 us
  transfers between devices with their start and end apart: 6, of which 5 were waited for; matrix products, arithmetic and copies ran while one was open for 1% of the time, Pallas kernels for 16%

profile of v4, /device:TPU:26, one launch (start us, length us, event | category | flops | bytes accessed | tf_op | source)
XLA Modules:
  0.0 384.8 jit_solution(13154674953419642886)
XLA Ops:
  0.0 10.2 %all-to-all-start = ((bf16[16,2,384,256]{3,2,1,0:T(8,128)(2,1)}), bf16[16,2,384,256]{3,2,1,0:T(8,128)(2,1)}, u32[]{:S(2)}, u32[]{:S(2)}) async-start(bf16[16,2,384,256]{3,2,1,0:T(8,128)(2,1)} %param.3), calls=%async_computation | async-start | bytes 12582912 | tf_op jit(solution)/shard_map/all_to_all | solution.py:185
  10.2 0.0 copy-start.5
  10.2 3.4 slice_bitcast_fusion
  13.6 0.8 collective-permute-start
  14.4 0.4 collective-permute-start.1
  14.9 0.0 copy-done.5
  14.9 0.5 and_select_fusion.order
  15.4 107.1 %collective-permute-done.refs_0_ = bf16[16,384,256]{2,1,0:T(8,128)(2,1)S(1)} collective-permute-done((bf16[16,384,256]{2,1,0:T(8,128)(2,1)S(1)}, bf16[16,384,256]{2,1,0:T(8,128)(2,1)S(1)}, u32[]{:S(2)}, u32[]{:S(2)}) %collective-permute-start) | collective-permute-done | bytes 3145760 | tf_op jit(solution)/shard_map/ppermute | solution.py:192
  122.5 1.6 copy-done.3
  124.2 3.8 %shard_map.37 = bf16[16,384,256]{2,1,0:T(8,128)(2,1)} custom-call(s32[16]{0:T(128)} %and_select_fusion.order, s32[1]{0:T(128)} %constant.34.clone.1.relayed, bf16[16,384,256]{2,1,0:T(8,128)(2,1)} %copy-done.3), custom_call_target="tpu_custom_call" | custom-call | bytes 6291456 | tf_op jit(solution)/shard_map/pallas_call | solution.py:38
  128.0 0.0 copy-start.4
  128.0 24.8 %collective-permute-done.1.refs_0_ = bf16[16,384,256]{2,1,0:T(8,128)(2,1)} collective-permute-done((bf16[16,384,256]{2,1,0:T(8,128)(2,1)S(1)}, bf16[16,384,256]{2,1,0:T(8,128)(2,1)}, u32[]{:S(2)}, u32[]{:S(2)}) %collective-permute-start.1) | collective-permute-done | bytes 3145760 | tf_op jit(solution)/shard_map/ppermute | solution.py:193
  152.8 4.2 %all-to-all-done.own_ref = bf16[16,2,384,256]{3,2,1,0:T(8,128)(2,1)} async-done(((bf16[16,2,384,256]{3,2,1,0:T(8,128)(2,1)}), bf16[16,2,384,256]{3,2,1,0:T(8,128)(2,1)}, u32[]{:S(2)}, u32[]{:S(2)}) %all-to-all-start) | async-done | bytes 6291488 | tf_op jit(solution)/shard_map/all_to_all | solution.py:185
  157.0 5.9 %all-to-all-start.1 = ((bf16[16,384,256]{2,1,0:T(8,128)(2,1)}), bf16[16,384,256]{2,1,0:T(8,128)(2,1)S(1)}, u32[]{:S(2)}, u32[]{:S(2)}) async-start(bf16[16,384,256]{2,1,0:T(8,128)(2,1)} %shard_map.37), calls=%async_computation.1 | async-start | bytes 6291456 | tf_op jit(solution)/shard_map/all_to_all | solution.py:185
  162.9 0.0 copy-done.4
  162.9 0.6 iota_select_fusion
  163.5 3.3 collective-permute-start.2
  166.9 46.8 %shard_map.38.own_ref = bf16[2,6144,256]{2,1,0:T(8,128)(2,1)} custom-call(s32[1,6144]{1,0:T(1,128)} %bitcast.15, bf16[16,2,384,256]{3,2,1,0:T(8,128)(2,1)} %all-to-all-done.own_ref), custom_call_target="tpu_custom_call" | custom-call | flops 38654705664 | bytes 12582912 | tf_op jit(solution)/shard_map/pallas_call | solution.py:77
  213.7 51.3 %collective-permute-done.2.refs_1_ = bf16[16,384,256]{2,1,0:T(8,128)(2,1)S(1)} collective-permute-done((bf16[16,384,256]{2,1,0:T(8,128)(2,1)}, bf16[16,384,256]{2,1,0:T(8,128)(2,1)S(1)}, u32[]{:S(2)}, u32[]{:S(2)}) %collective-permute-start.2) | collective-permute-done | bytes 3145760 | tf_op jit(solution)/shard_map/ppermute | solution.py:196
  265.0 1.6 copy-done.2
  266.7 3.8 shard_map.39
  270.5 0.0 all-to-all-done.1.partner_ref
  270.5 9.1 %all-to-all-start.2 = ((bf16[16,384,256]{2,1,0:T(8,128)(2,1)}), bf16[16,384,256]{2,1,0:T(8,128)(2,1)}, u32[]{:S(2)}, u32[]{:S(2)}) async-start(bf16[16,384,256]{2,1,0:T(8,128)(2,1)} %shard_map.39), calls=%async_computation.2 | async-start | bytes 6291456 | tf_op jit(solution)/shard_map/all_to_all | solution.py:185
  279.7 6.9 %shard_map.40.first_ref = f32[2,256,256]{2,1,0:T(8,128)S(1)} custom-call(bf16[2,6144,256]{2,1,0:T(8,128)(2,1)} %shard_map.38.own_ref, bf16[16,384,256]{2,1,0:T(8,128)(2,1)S(1)} %all-to-all-done.1.partner_ref), custom_call_target="tpu_custom_call" | custom-call | flops 1610612736 | bytes 9437184 | tf_op jit(solution)/shard_map/pallas_call | solution.py:150
  286.6 0.0 copy-start
  286.6 0.8 copy-done
  287.4 65.5 %all-to-all-done.2.partner_ref = bf16[16,384,256]{2,1,0:T(8,128)(2,1)} async-done(((bf16[16,384,256]{2,1,0:T(8,128)(2,1)}), bf16[16,384,256]{2,1,0:T(8,128)(2,1)}, u32[]{:S(2)}, u32[]{:S(2)}) %all-to-all-start.2) | async-done | bytes 3145760 | tf_op jit(solution)/shard_map/all_to_all | solution.py:185
  352.9 1.0 copy-done.1
  353.9 7.4 %shard_map.41 = f32[256,512]{1,0:T(8,128)S(1)} custom-call(bf16[2,6144,256]{2,1,0:T(8,128)(2,1)} %shard_map.38.own_ref, bf16[16,384,256]{2,1,0:T(8,128)(2,1)} %all-to-all-done.2.partner_ref, f32[2,256,256]{2,1,0:T(8,128)S(1)} %copy-done.1), custom_call_target="tpu_custom_call" | custom-call | flops 1610612736 | bytes 9437184 | tf_op jit(solution)/shard_map/pallas_call | solution.py:164
  361.4 22.1 %all_to_all.24 = f32[16,16,512]{2,1,0:T(8,128)S(1)} all-to-all(f32[16,16,512]{2,1,0:T(8,128)S(1)} %bitcast.14), channel_id=1, replica_groups=mesh['ka'=16,'pw'=16] {'pw'}, dimensions={0} | all-to-all | bytes 1048576 | tf_op jit(solution)/shard_map/all_to_all | solution.py:185
  383.4 0.3 reshape.20
  383.8 1.1 copy.11
  (3 shorter events, 0.0 us)
Async XLA Ops:
  0.0 157.0 %all-to-all-start = ((bf16[16,2,384,256]{3,2,1,0:T(8,128)(2,1)}), bf16[16,2,384,256]{3,2,1,0:T(8,128)(2,1)}, u32[]{:S(2)}, u32[]{:S(2)}) async-start(bf16[16,2,384,256]{3,2,1,0:T(8,128)(2,1)} %param.3), calls=%async_computation | async-start | bytes 12582912 | tf_op jit(solution)/shard_map/all_to_all | solution.py:185
  10.2 4.7 %copy-start.5 = (s32[16]{0:T(128)S(1)}, s32[16]{0:T(128)}, u32[]{:S(2)}) copy-start(s32[16]{0:T(128)} %param.4) | copy-start | bytes 196
  13.6 108.9 %collective-permute-start = (bf16[16,384,256]{2,1,0:T(8,128)(2,1)S(1)}, bf16[16,384,256]{2,1,0:T(8,128)(2,1)S(1)}, u32[]{:S(2)}, u32[]{:S(2)}) collective-permute-start(bf16[16,384,256]{2,1,0:T(8,128)(2,1)S(1)} %get-tuple-element.20), channel_id=1, source_target_pairs={{32,0},{48,16},{64,32},{80,48},{96,64},{112,80},{128,96},{144,112}... | collective-permute-start | bytes 9437192 | tf_op jit(solution)/shard_map/ppermute | solution.py:192
  14.4 138.4 %collective-permute-start.1 = (bf16[16,384,256]{2,1,0:T(8,128)(2,1)S(1)}, bf16[16,384,256]{2,1,0:T(8,128)(2,1)}, u32[]{:S(2)}, u32[]{:S(2)}) collective-permute-start(bf16[16,384,256]{2,1,0:T(8,128)(2,1)S(1)} %get-tuple-element.19), channel_id=1, source_target_pairs={{32,0},{48,16},{64,32},{80,48},{96,64},{112,80},{0,96},{16,112},{1... | collective-permute-start | bytes 9437192 | tf_op jit(solution)/shard_map/ppermute | solution.py:193
  122.5 1.6 copy-start.3
  128.0 34.9 %copy-start.4 = (s32[6144]{0:T(1024)S(1)}, s32[6144]{0:T(1024)}, u32[]{:S(2)}) copy-start(s32[6144]{0:T(1024)} %param.5) | copy-start | bytes 73732
  157.0 113.6 %all-to-all-start.1 = ((bf16[16,384,256]{2,1,0:T(8,128)(2,1)}), bf16[16,384,256]{2,1,0:T(8,128)(2,1)S(1)}, u32[]{:S(2)}, u32[]{:S(2)}) async-start(bf16[16,384,256]{2,1,0:T(8,128)(2,1)} %shard_map.37), calls=%async_computation.1 | async-start | bytes 6291456 | tf_op jit(solution)/shard_map/all_to_all | solution.py:185
  163.5 101.5 %collective-permute-start.2 = (bf16[16,384,256]{2,1,0:T(8,128)(2,1)}, bf16[16,384,256]{2,1,0:T(8,128)(2,1)S(1)}, u32[]{:S(2)}, u32[]{:S(2)}) collective-permute-start(bf16[16,384,256]{2,1,0:T(8,128)(2,1)} %collective-permute-done.1.refs_0_), channel_id=1, source_target_pairs={{224,96},{240,112},{96,224},{112,240},{225,97},{241,113},{97,225},... | collective-permute-start | bytes 9437192 | tf_op jit(solution)/shard_map/ppermute | solution.py:196
  265.0 1.6 copy-start.2
  270.5 82.3 %all-to-all-start.2 = ((bf16[16,384,256]{2,1,0:T(8,128)(2,1)}), bf16[16,384,256]{2,1,0:T(8,128)(2,1)}, u32[]{:S(2)}, u32[]{:S(2)}) async-start(bf16[16,384,256]{2,1,0:T(8,128)(2,1)} %shard_map.39), calls=%async_computation.2 | async-start | bytes 6291456 | tf_op jit(solution)/shard_map/all_to_all | solution.py:185
  286.6 0.8 copy-start
  352.9 1.0 copy-start.1

commit v5 on v4

--- a/solution.py
+++ b/solution.py
@@ -8,35 +8,49 @@
 SHIFT_DEV = 2
 
 
-def reorder_kernel(order, relayed, *refs):
-    *sources, result, held, read, written = refs
-    count = result.shape[0]
-
-    def fetch(source, i):
-        return pltpu.make_async_copy(source.at[order[i]], held.at[i], read.at[i])
-
-    def store(i):
-        return pltpu.make_async_copy(held.at[i], result.at[i], written.at[i])
-
-    for choice, source in enumerate(sources):
-
-        @pl.when(relayed[0] == choice)
-        def _(source=source):
-            for i in range(count):
-                fetch(source, i).start()
-            for i in range(count):
-                fetch(source, i).wait()
-                store(i).start()
-
-    for i in range(count):
-        store(i).wait()
-
-
-def reordered(order, relayed, *sources):
-    shape, dtype = sources[0].shape, sources[0].dtype
-    count = shape[0]
-    return pl.pallas_call(
-        reorder_kernel,
+def reordered(order, relayed, *pieces):
+    sources = [source for piece in pieces for source in piece]
+    count, _, bands = sources[0].shape
+    rows = sum(piece[0].shape[1] for piece in pieces)
+    shape, dtype = (count, rows, bands), sources[0].dtype
+
+    def kernel(order, relayed, *refs):
+        *given, result, held, read, written = refs
+
+        def fetches(choice):
+            at, first, copies = 0, 0, []
+            for p, piece in enumerate(pieces):
+                source = given[at + min(choice, len(piece) - 1)]
+                height = piece[0].shape[1]
+                copies += [
+                    pltpu.make_async_copy(
+                        source.at[order[i]], held.at[i, pl.ds(first, height)], read.at[p, i]
+                    )
+                    for i in range(count)
+                ]
+                at, first = at + len(piece), first + height
+            return copies
+
+        stores = [
+            pltpu.make_async_copy(held.at[i], result.at[i], written.at[i]) for i in range(count)
+        ]
+        for choice in range(max(len(piece) for piece in pieces)):
+
+            @pl.when(relayed[0] == choice)
+            def _(choice=choice):
+                copies = fetches(choice)
+                for copy in copies:
+                    copy.start()
+                for i in range(count):
+                    for copy in copies[i::count]:
+                        copy.wait()
+                    stores[i].start()
+
+        for store in stores:
+            store.wait()
+
+    return pl.pallas_call(
+        kernel,
         grid_spec=pltpu.PrefetchScalarGridSpec(
             num_scalar_prefetch=2,
             grid=(),
@@ -44,19 +58,21 @@
             out_specs=pl.BlockSpec(memory_space=pltpu.HBM),
             scratch_shapes=[
                 pltpu.VMEM(shape, dtype),
-                pltpu.SemaphoreType.DMA((count,)),
+                pltpu.SemaphoreType.DMA((len(pieces), count)),
                 pltpu.SemaphoreType.DMA((count,)),
             ],
         ),
         out_shape=jax.ShapeDtypeStruct(shape, dtype),
         compiler_params=pltpu.CompilerParams(vmem_limit_bytes=56 << 20),
-        cost_estimate=pl.CostEstimate(flops=0, bytes_accessed=4 * sources[0].size, transcendentals=0),
+        cost_estimate=pl.CostEstimate(
+            flops=0, bytes_accessed=4 * count * rows * bands, transcendentals=0
+        ),
     )(order, relayed, *sources)
 
 
 def scatter_rows_kernel(target_ref, own_ref, out_ref):
     sources, parts, rows, bands = own_ref.shape
-    height = out_ref.shape[1]
+    height = out_ref.shape[2]
     first = pl.program_id(0) * height
     pair = 2
     wanted = first + lax.broadcasted_iota(jnp.int32, (height, pair * rows), 0)
@@ -67,7 +83,7 @@
             block = own_ref[s : s + pair, c].reshape(pair * rows, bands)
             totals[c] += jnp.dot(hot, block, preferred_element_type=jnp.float32)
     for c in range(parts):
-        out_ref[c] = totals[c].astype(out_ref.dtype)
+        out_ref[c] = totals[c].T.astype(out_ref.dtype)
 
 
 def scattered_rows(own, target):
@@ -81,8 +97,8 @@
             pl.BlockSpec((1, total), lambda i: (0, 0)),
             pl.BlockSpec(own.shape, lambda i: (0, 0, 0, 0), pipeline_mode=pl.Buffered(1)),
         ],
-        out_specs=pl.BlockSpec((parts, height, bands), lambda i: (0, i, 0)),
-        out_shape=jax.ShapeDtypeStruct((parts, total, bands), own.dtype),
+        out_specs=pl.BlockSpec((parts, bands, height), lambda i: (0, 0, i)),
+        out_shape=jax.ShapeDtypeStruct((parts, bands, total), own.dtype),
         compiler_params=pltpu.CompilerParams(vmem_limit_bytes=56 << 20),
         cost_estimate=pl.CostEstimate(
             flops=2 * total * total * parts * bands, bytes_accessed=4 * own.size, transcendentals=0
@@ -93,12 +109,9 @@
 def plane_products(own_ref, partner_ref):
     sources, rows, bands = partner_ref.shape
     partner = partner_ref[...].reshape(sources * rows, bands)
-    return [
-        lax.dot_general(
-            own_ref[c], partner, (((0,), (0,)), ((), ())), preferred_element_type=jnp.float32
-        )
-        for c in range(2)
-    ]
+    own = own_ref[...].reshape(-1, sources * rows)
+    both = jnp.dot(own, partner, preferred_element_type=jnp.float32)
+    return both[:bands], both[bands:]
 
 
 def first_plane_kernel(own_ref, partner_ref, out_ref):
@@ -135,7 +148,7 @@
 def pair_specs(own, partner):
     sources, rows, bands = partner.shape
     specs = [
-        pl.BlockSpec((own.shape[0], TAKE * rows, bands), lambda i: (0, i, 0)),
+        pl.BlockSpec((own.shape[0], bands, TAKE * rows), lambda i: (0, 0, i)),
         pl.BlockSpec((TAKE, rows, bands), lambda i: (i, 0, 0)),
     ]
     cost = pl.CostEstimate(
@@ -146,21 +159,21 @@
 
 def first_plane(own, partner):
     grid, specs, cost = pair_specs(own, partner)
-    bands = own.shape[-1]
+    bands = own.shape[1]
     return pl.pallas_call(
         first_plane_kernel,
         grid=grid,
         in_specs=specs,
         out_specs=pl.BlockSpec((2, bands, bands), lambda i: (0, 0, 0)),
         out_shape=jax.ShapeDtypeStruct((2, bands, bands), jnp.float32),
-        compiler_params=pltpu.CompilerParams(vmem_limit_bytes=32 << 20),
+        compiler_params=pltpu.CompilerParams(vmem_limit_bytes=56 << 20),
         cost_estimate=cost,
     )(own, partner)
 
 
 def second_plane(own, partner, first):
     grid, specs, cost = pair_specs(own, partner)
-    bands = own.shape[-1]
+    bands = own.shape[1]
     return pl.pallas_call(
         second_plane_kernel,
         grid=grid,
@@ -168,7 +181,7 @@
         out_specs=pl.BlockSpec((bands, 2 * bands), lambda i: (0, 0)),
         out_shape=jax.ShapeDtypeStruct((bands, 2 * bands), jnp.float32),
         scratch_shapes=[pltpu.VMEM(first.shape, jnp.float32)],
-        compiler_params=pltpu.CompilerParams(vmem_limit_bytes=32 << 20),
+        compiler_params=pltpu.CompilerParams(vmem_limit_bytes=56 << 20),
         cost_estimate=cost,
     )(own, partner, first)
 
@@ -189,16 +202,18 @@
     straight = [((i + SHIFT_DEV) % ka_count, i) for i in range(ka_count)]
     around = [(i // half * half + (i + SHIFT_DEV) % half, i) for i in range(ka_count)]
     swap = [((i + half) % ka_count, i) for i in range(ka_count) if i % half >= half - SHIFT_DEV]
+    cut = rows // 2
     direct = lax.ppermute(coeffs[:, 0], "ka", straight)
-    turned = lax.ppermute(coeffs[:, 1], "ka", around)
-    waiting = reordered(order, jnp.zeros((1,), jnp.int32), direct)
+    turned = lax.ppermute(coeffs[:, 1, cut:], "ka", around)
+    later = lax.ppermute(coeffs[:, 1, :cut], "ka", straight)
+    waiting = reordered(order, jnp.zeros((1,), jnp.int32), [direct])
     own, waiting, turned = lax.optimization_barrier((own, waiting, turned))
     swapped = lax.ppermute(turned, "ka", swap)
     real = spread(waiting)
     target = jnp.where(wrapped, gshift, lax.iota(jnp.int32, gshift.shape[0]))
     moved = pltpu.with_memory_space_constraint(scattered_rows(own, target), pltpu.HBM)
-    moved, swapped = lax.optimization_barrier((moved, swapped))
-    waiting = reordered(order, crosses.astype(jnp.int32).reshape(1), turned, swapped)
+    moved, swapped, later = lax.optimization_barrier((moved, swapped, later))
+    waiting = reordered(order, crosses.astype(jnp.int32).reshape(1), [later], [turned, swapped])
     real, waiting = lax.optimization_barrier((real, waiting))
     imag = spread(waiting)
     first = first_plane(moved, real)

time: 387 us -> 350 us (0.904)
  waiting for transfers between devices: 253 us -> 209 us
  Pallas kernels: 68.9 us -> 73.5 us
    ppermute x1, waiting for transfers between devices: 51.3 us -> 0.01 us  [on_device(): swapped = lax.ppermute(turned, 'ka', swap)]
    all_to_all x3, waiting for transfers between devices: 69.6 us -> 103 us  [spread(): return lax.all_to_all(block, 'pw', split_axis=0, concat_axis=0, tiled=True)]
    ppermute x1 -> x2, waiting for transfers between devices: 24.8 us -> 0.01 us  [the longest x1 0.01 us: on_device(): turned = lax.ppermute(coeffs[:, 1, cut:], 'ka', around)]
  transfers between devices with their start and end apart: 6 -> 7, of which waited for: 5 -> 4; matrix products, arithmetic and copies ran while one was open for 1% -> 1% of each run, Pallas kernels for 16% -> 19%
where the time goes in v5:
time: 350 us; the launch traced here: 347 us
  waiting for transfers between devices  209 us (60%)
  Pallas kernels  73.5 us (21%)
  starting transfers between devices  31.5 us (9%)
  blocking collectives  22 us (6%)
  local copies, waits for them, and re-layouts  10.3 us (3%)
    ppermute x1, waiting for transfers between devices, on_device(): direct = lax.ppermute(coeffs[:, 0], 'ka', straight)  106 us
    all_to_all x3, waiting for transfers between devices, spread(): return lax.all_to_all(block, 'pw', split_axis=0, concat_axis=0, tiled=True)  103 us
    pallas_call x1, Pallas kernels, scattered_rows(): pl.pallas_call(scatter_rows_kernel, grid=(total // height,), in_specs=[pl...  49.2 us
    all_to_all x3, starting transfers between devices, spread(): return lax.all_to_all(block, 'pw', split_axis=0, concat_axis=0, tiled=True)  25.7 us
    all_to_all x1, blocking collectives, spread(): return lax.all_to_all(block, 'pw', split_axis=0, concat_axis=0, tiled=True)  22 us
    pallas_call x1, Pallas kernels, second_plane(): pl.pallas_call(second_plane_kernel, grid=grid, in_specs=specs + [pl.Block...  8.18 us
    pallas_call x2, Pallas kernels, reordered(): pl.pallas_call(kernel, grid_spec=pltpu.PrefetchScalarGridSpec(num_scalar_...  8.13 us
    pallas_call x1, Pallas kernels, first_plane(): pl.pallas_call(first_plane_kernel, grid=grid, in_specs=specs, out_specs=p...  7.97 us
  transfers between devices with their start and end apart: 7, of which 4 were waited for; matrix products, arithmetic and copies ran while one was open for 1% of the time, Pallas kernels for 19%

profile of v5, /device:TPU:26, one launch (start us, length us, event | category | flops | bytes accessed | tf_op | source)
XLA Modules:
  0.0 347.3 jit_solution(17447570863636473448)
XLA Ops:
  0.0 10.2 %all-to-all-start = ((bf16[16,2,384,256]{3,2,1,0:T(8,128)(2,1)}), bf16[16,2,384,256]{3,2,1,0:T(8,128)(2,1)}, u32[]{:S(2)}, u32[]{:S(2)}) async-start(bf16[16,2,384,256]{3,2,1,0:T(8,128)(2,1)} %param.3), calls=%async_computation | async-start | bytes 12582912 | tf_op jit(solution)/shard_map/all_to_all | solution.py:198
  10.2 0.0 copy-start
  10.2 2.3 slice_bitcast_fusion
  12.5 0.0 copy-start.5
  12.5 0.8 collective-permute-start
  13.4 0.6 copy-done
  13.9 1.5 slice_bitcast_fusion.1
  15.4 0.7 collective-permute-start.1
  16.2 0.5 and_select_fusion.order
  16.7 105.8 %collective-permute-done.refs_0_ = bf16[16,384,256]{2,1,0:T(8,128)(2,1)S(1)} collective-permute-done((bf16[16,384,256]{2,1,0:T(8,128)(2,1)S(1)}, bf16[16,384,256]{2,1,0:T(8,128)(2,1)S(1)}, u32[]{:S(2)}, u32[]{:S(2)}) %collective-permute-start) | collective-permute-done | bytes 3145760 | tf_op jit(solution)/shard_map/ppermute | solution.py:206
  122.5 1.7 copy-done.2
  124.1 3.8 %shard_map.37 = bf16[16,384,256]{2,1,0:T(8,128)(2,1)} custom-call(s32[16]{0:T(128)} %and_select_fusion.order, s32[1]{0:T(128)} %constant.34.clone.1.relayed, bf16[16,384,256]{2,1,0:T(8,128)(2,1)} %copy-done.2), custom_call_target="tpu_custom_call" | custom-call | bytes 6291456 | tf_op jit(solution)/shard_map/pallas_call | solution.py:52
  128.0 0.0 copy-start.4
  128.0 0.0 collective-permute-done.1.refs_1_
  128.0 29.0 %all-to-all-done.own_ref = bf16[16,2,384,256]{3,2,1,0:T(8,128)(2,1)} async-done(((bf16[16,2,384,256]{3,2,1,0:T(8,128)(2,1)}), bf16[16,2,384,256]{3,2,1,0:T(8,128)(2,1)}, u32[]{:S(2)}, u32[]{:S(2)}) %all-to-all-start) | async-done | bytes 6291488 | tf_op jit(solution)/shard_map/all_to_all | solution.py:198
  157.0 5.9 %all-to-all-start.1 = ((bf16[16,384,256]{2,1,0:T(8,128)(2,1)}), bf16[16,384,256]{2,1,0:T(8,128)(2,1)S(1)}, u32[]{:S(2)}, u32[]{:S(2)}) async-start(bf16[16,384,256]{2,1,0:T(8,128)(2,1)} %shard_map.37), calls=%async_computation.1 | async-start | bytes 6291456 | tf_op jit(solution)/shard_map/all_to_all | solution.py:198
  162.9 0.8 collective-permute-start.3
  163.7 0.6 iota_select_fusion
  164.3 3.3 collective-permute-start.2
  167.7 49.2 %shard_map.38.own_ref = bf16[2,256,6144]{2,1,0:T(8,128)(2,1)} custom-call(s32[1,6144]{1,0:T(1,128)} %bitcast.19, bf16[16,2,384,256]{3,2,1,0:T(8,128)(2,1)} %all-to-all-done.own_ref), custom_call_target="tpu_custom_call" | custom-call | flops 38654705664 | bytes 12582912 | tf_op jit(solution)/shard_map/pallas_call | solution.py:93
  216.9 0.0 collective-permute-done.3.refs_0_
  216.9 1.2 copy-done.3
  218.1 4.3 %shard_map.39 = bf16[16,384,256]{2,1,0:T(8,128)(2,1)} custom-call(s32[16]{0:T(128)} %and_select_fusion.order, s32[1]{0:T(128)} %bitcast.4.relayed, bf16[16,192,256]{2,1,0:T(8,128)(2,1)} %collective-permute-done.3.refs_0_, bf16[16,192,256]{2,1,0:T(8,128)(2,1)} %collective-permute-done.1.refs_1_, bf16[16,192,256]{2,1,0:T(8,128)(2,1)} %copy-done.3), custom_call_target="tpu_custom_call" | custom-call | bytes 6291456 | tf_op jit(solution)/shard_map/pallas_call | solution.py:52
  222.4 13.9 %all-to-all-done.1.partner_ref = bf16[16,384,256]{2,1,0:T(8,128)(2,1)S(1)} async-done(((bf16[16,384,256]{2,1,0:T(8,128)(2,1)}), bf16[16,384,256]{2,1,0:T(8,128)(2,1)S(1)}, u32[]{:S(2)}, u32[]{:S(2)}) %all-to-all-start.1) | async-done | bytes 3145760 | tf_op jit(solution)/shard_map/all_to_all | solution.py:198
  236.3 1.6 copy-done.1
  237.9 9.6 %all-to-all-start.2 = ((bf16[16,384,256]{2,1,0:T(8,128)(2,1)}), bf16[16,384,256]{2,1,0:T(8,128)(2,1)}, u32[]{:S(2)}, u32[]{:S(2)}) async-start(bf16[16,384,256]{2,1,0:T(8,128)(2,1)} %shard_map.39), calls=%async_computation.2 | async-start | bytes 6291456 | tf_op jit(solution)/shard_map/all_to_all | solution.py:198
  247.6 8.0 %shard_map.40.first_ref = f32[2,256,256]{2,1,0:T(8,128)} custom-call(bf16[2,256,6144]{2,1,0:T(8,128)(2,1)} %shard_map.38.own_ref, bf16[16,384,256]{2,1,0:T(8,128)(2,1)} %copy-done.1), custom_call_target="tpu_custom_call" | custom-call | flops 1610612736 | bytes 9437184 | tf_op jit(solution)/shard_map/pallas_call | solution.py:163
  255.6 60.2 %all-to-all-done.2.partner_ref = bf16[16,384,256]{2,1,0:T(8,128)(2,1)} async-done(((bf16[16,384,256]{2,1,0:T(8,128)(2,1)}), bf16[16,384,256]{2,1,0:T(8,128)(2,1)}, u32[]{:S(2)}, u32[]{:S(2)}) %all-to-all-start.2) | async-done | bytes 3145760 | tf_op jit(solution)/shard_map/all_to_all | solution.py:198
  315.7 8.2 %shard_map.41 = f32[256,512]{1,0:T(8,128)} custom-call(bf16[2,256,6144]{2,1,0:T(8,128)(2,1)} %shard_map.38.own_ref, bf16[16,384,256]{2,1,0:T(8,128)(2,1)} %all-to-all-done.2.partner_ref, f32[2,256,256]{2,1,0:T(8,128)} %shard_map.40.first_ref), custom_call_target="tpu_custom_call" | custom-call | flops 1610612736 | bytes 9437184 | tf_op jit(solution)/shard_map/pallas_call | solution.py:177
  323.9 22.0 %all_to_all.24 = f32[16,16,512]{2,1,0:T(8,128)S(1)} all-to-all(f32[16,16,512]{2,1,0:T(8,128)} %bitcast.18), channel_id=1, replica_groups=mesh['ka'=16,'pw'=16] {'pw'}, dimensions={0} | all-to-all | bytes 1048576 | tf_op jit(solution)/shard_map/all_to_all | solution.py:198
  345.9 0.3 reshape.20
  346.2 1.1 copy.13
  (6 shorter events, 0.0 us)
Async XLA Ops:
  0.0 157.0 %all-to-all-start = ((bf16[16,2,384,256]{3,2,1,0:T(8,128)(2,1)}), bf16[16,2,384,256]{3,2,1,0:T(8,128)(2,1)}, u32[]{:S(2)}, u32[]{:S(2)}) async-start(bf16[16,2,384,256]{3,2,1,0:T(8,128)(2,1)} %param.3), calls=%async_computation | async-start | bytes 12582912 | tf_op jit(solution)/shard_map/all_to_all | solution.py:198
  10.2 3.7 %copy-start = (bf16[16,2,384,256]{3,2,1,0:T(8,128)(2,1)S(1)}, bf16[16,2,384,256]{3,2,1,0:T(8,128)(2,1)}, u32[]{:S(2)}) copy-start(bf16[16,2,384,256]{3,2,1,0:T(8,128)(2,1)} %param.3) | copy-start | bytes 18874372
  12.5 3.6 %copy-start.5 = (s32[16]{0:T(128)S(1)}, s32[16]{0:T(128)}, u32[]{:S(2)}) copy-start(s32[16]{0:T(128)} %param.4) | copy-start | bytes 196
  12.5 110.0 %collective-permute-start = (bf16[16,384,256]{2,1,0:T(8,128)(2,1)S(1)}, bf16[16,384,256]{2,1,0:T(8,128)(2,1)S(1)}, u32[]{:S(2)}, u32[]{:S(2)}) collective-permute-start(bf16[16,384,256]{2,1,0:T(8,128)(2,1)S(1)} %slice_bitcast_fusion), channel_id=1, source_target_pairs={{32,0},{48,16},{64,32},{80,48},{96,64},{112,80},{128,96},{144,112}... | collective-permute-start | bytes 9437192 | tf_op jit(solution)/shard_map/ppermute | solution.py:206
  15.4 112.6 %collective-permute-start.1 = (bf16[16,192,256]{2,1,0:T(8,128)(2,1)S(1)}, bf16[16,192,256]{2,1,0:T(8,128)(2,1)}, u32[]{:S(2)}, u32[]{:S(2)}) collective-permute-start(bf16[16,192,256]{2,1,0:T(8,128)(2,1)S(1)} %get-tuple-element.22), channel_id=1, source_target_pairs={{32,0},{48,16},{64,32},{80,48},{96,64},{112,80},{0,96},{16,112},{1... | collective-permute-start | bytes 4718600 | tf_op jit(solution)/shard_map/ppermute | solution.py:207
  122.5 1.7 copy-start.2
  128.0 35.7 %copy-start.4 = (s32[6144]{0:T(1024)S(1)}, s32[6144]{0:T(1024)}, u32[]{:S(2)}) copy-start(s32[6144]{0:T(1024)} %param.5) | copy-start | bytes 73732
  157.0 79.3 %all-to-all-start.1 = ((bf16[16,384,256]{2,1,0:T(8,128)(2,1)}), bf16[16,384,256]{2,1,0:T(8,128)(2,1)S(1)}, u32[]{:S(2)}, u32[]{:S(2)}) async-start(bf16[16,384,256]{2,1,0:T(8,128)(2,1)} %shard_map.37), calls=%async_computation.1 | async-start | bytes 6291456 | tf_op jit(solution)/shard_map/all_to_all | solution.py:198
  162.9 54.0 %collective-permute-start.3 = (bf16[16,192,256]{2,1,0:T(8,128)(2,1)}, bf16[16,192,256]{2,1,0:T(8,128)(2,1)}, u32[]{:S(2)}, u32[]{:S(2)}) collective-permute-start(bf16[16,192,256]{2,1,0:T(8,128)(2,1)} %get-tuple-element.21), channel_id=1, source_target_pairs={{32,0},{48,16},{64,32},{80,48},{96,64},{112,80},{128,96},{144,112}... | collective-permute-start | bytes 4718600 | tf_op jit(solution)/shard_map/ppermute | solution.py:208
  164.3 52.6 %collective-permute-start.2 = (bf16[16,192,256]{2,1,0:T(8,128)(2,1)}, bf16[16,192,256]{2,1,0:T(8,128)(2,1)S(1)}, u32[]{:S(2)}, u32[]{:S(2)}) collective-permute-start(bf16[16,192,256]{2,1,0:T(8,128)(2,1)} %collective-permute-done.1.refs_1_), channel_id=1, source_target_pairs={{224,96},{240,112},{96,224},{112,240},{225,97},{241,113},{97,225},... | collective-permute-start | bytes 4718600 | tf_op jit(solution)/shard_map/ppermute | solution.py:211
  216.9 1.2 copy-start.3
  236.3 1.6 copy-start.1
  237.9 77.8 %all-to-all-start.2 = ((bf16[16,384,256]{2,1,0:T(8,128)(2,1)}), bf16[16,384,256]{2,1,0:T(8,128)(2,1)}, u32[]{:S(2)}, u32[]{:S(2)}) async-start(bf16[16,384,256]{2,1,0:T(8,128)(2,1)} %shard_map.39), calls=%async_computation.2 | async-start | bytes 6291456 | tf_op jit(solution)/shard_map/all_to_all | solution.py:198

commit v6 on v5

--- a/solution.py
+++ b/solution.py
@@ -65,45 +65,126 @@
         out_shape=jax.ShapeDtypeStruct(shape, dtype),
         compiler_params=pltpu.CompilerParams(vmem_limit_bytes=56 << 20),
         cost_estimate=pl.CostEstimate(
-            flops=0, bytes_accessed=4 * count * rows * bands, transcendentals=0
+            flops=0, bytes_accessed=2 * count * rows * bands * dtype.itemsize, transcendentals=0
         ),
     )(order, relayed, *sources)
 
 
-def scatter_rows_kernel(target_ref, own_ref, out_ref):
-    sources, parts, rows, bands = own_ref.shape
+def scatter_rows_kernel(target_ref, real_ref, imag_ref, out_ref):
+    sources, rows, bands = real_ref.shape
     height = out_ref.shape[2]
     first = pl.program_id(0) * height
     pair = 2
     wanted = first + lax.broadcasted_iota(jnp.int32, (height, pair * rows), 0)
-    totals = [jnp.zeros((height, bands), jnp.float32) for _ in range(parts)]
+    totals = [jnp.zeros((height, bands), jnp.float32) for _ in range(2)]
     for s in range(0, sources, pair):
         hot = (target_ref[:, s * rows : (s + pair) * rows] == wanted).astype(jnp.bfloat16)
-        for c in range(parts):
-            block = own_ref[s : s + pair, c].reshape(pair * rows, bands)
+        for c, plane in enumerate((real_ref, imag_ref)):
+            block = plane[s : s + pair].reshape(pair * rows, bands)
             totals[c] += jnp.dot(hot, block, preferred_element_type=jnp.float32)
-    for c in range(parts):
+    for c in range(2):
         out_ref[c] = totals[c].T.astype(out_ref.dtype)
 
 
-def scattered_rows(own, target):
-    sources, parts, rows, bands = own.shape
+def scattered_rows(planes, target):
+    sources, rows, bands = planes[0].shape
     total = sources * rows
     height = 256
+    whole = pl.BlockSpec(planes[0].shape, lambda i: (0, 0, 0), pipeline_mode=pl.Buffered(1))
     return pl.pallas_call(
         scatter_rows_kernel,
         grid=(total // height,),
-        in_specs=[
-            pl.BlockSpec((1, total), lambda i: (0, 0)),
-            pl.BlockSpec(own.shape, lambda i: (0, 0, 0, 0), pipeline_mode=pl.Buffered(1)),
-        ],
-        out_specs=pl.BlockSpec((parts, bands, height), lambda i: (0, 0, i)),
-        out_shape=jax.ShapeDtypeStruct((parts, bands, total), own.dtype),
+        in_specs=[pl.BlockSpec((1, total), lambda i: (0, 0)), whole, whole],
+        out_specs=pl.BlockSpec((2, bands, height), lambda i: (0, 0, i)),
+        out_shape=jax.ShapeDtypeStruct((2, bands, total), planes[0].dtype),
         compiler_params=pltpu.CompilerParams(vmem_limit_bytes=56 << 20),
         cost_estimate=pl.CostEstimate(
-            flops=2 * total * total * parts * bands, bytes_accessed=4 * own.size, transcendentals=0
-        ),
-    )(target.reshape(1, total), own)
+            flops=4 * total * total * bands, bytes_accessed=8 * planes[0].size, transcendentals=0
+        ),
+    )(target.reshape(1, total), *planes)
+
+
+def ordered_planes_kernel(order, source, real, imag, held, read, written):
+    count = real.shape[0]
+    fetches, stores = [], []
+    for c, result in enumerate((real, imag)):
+        for i in range(count):
+            fetches.append(
+                pltpu.make_async_copy(source.at[order[i], c], held.at[c, i], read.at[c, i])
+            )
+            stores.append(pltpu.make_async_copy(held.at[c, i], result.at[i], written.at[c, i]))
+    for copy in fetches:
+        copy.start()
+    for fetch, store in zip(fetches, stores):
+        fetch.wait()
+        store.start()
+    for store in stores:
+        store.wait()
+
+
+def ordered_planes(source, order):
+    count, parts, rows, bands = source.shape
+    plane = jax.ShapeDtypeStruct((count, rows, bands), source.dtype)
+    return pl.pallas_call(
+        ordered_planes_kernel,
+        grid_spec=pltpu.PrefetchScalarGridSpec(
+            num_scalar_prefetch=1,
+            grid=(),
+            in_specs=[pl.BlockSpec(memory_space=pltpu.HBM)],
+            out_specs=[pl.BlockSpec(memory_space=pltpu.HBM)] * 2,
+            scratch_shapes=[
+                pltpu.VMEM((parts, count, rows, bands), source.dtype),
+                pltpu.SemaphoreType.DMA((parts, count)),
+                pltpu.SemaphoreType.DMA((parts, count)),
+            ],
+        ),
+        out_shape=[plane, plane],
+        compiler_params=pltpu.CompilerParams(vmem_limit_bytes=56 << 20),
+        cost_estimate=pl.CostEstimate(flops=0, bytes_accessed=4 * source.size, transcendentals=0),
+    )(order, source)
+
+
+def slab_kernel(own_of, own_ref, partner_ref, out_ref):
+    own = [own_ref[0, c] for c in range(2)]
+    partner = [partner_ref[0, d] for d in range(2)]
+
+    def product(c, d):
+        return lax.dot_general(
+            own[c], partner[d], (((0,), (0,)), ((), ())), preferred_element_type=jnp.float32
+        )
+
+    groups, _, height, width = out_ref.shape
+    bands = width // 2
+    real = product(0, 0) + product(1, 1)
+    imag = product(0, 1) - product(1, 0)
+    out_ref[:, 0, :, :bands] = real.reshape(groups, height, bands)
+    out_ref[:, 0, :, bands:] = imag.reshape(groups, height, bands)
+
+
+def slab_products(coeffs, partner, own_of, groups):
+    count, parts, rows, bands = partner.shape
+    block = (1, parts, rows, bands)
+    return pl.pallas_call(
+        slab_kernel,
+        grid_spec=pltpu.PrefetchScalarGridSpec(
+            num_scalar_prefetch=1,
+            grid=(count,),
+            in_specs=[
+                pl.BlockSpec(block, lambda j, own_of: (own_of[j], 0, 0, 0)),
+                pl.BlockSpec(block, lambda j, own_of: (j, 0, 0, 0)),
+            ],
+            out_specs=pl.BlockSpec(
+                (groups, 1, bands // groups, 2 * bands), lambda j, own_of: (0, j, 0, 0)
+            ),
+        ),
+        out_shape=jax.ShapeDtypeStruct((groups, count, bands // groups, 2 * bands), jnp.float32),
+        compiler_params=pltpu.CompilerParams(vmem_limit_bytes=56 << 20),
+        cost_estimate=pl.CostEstimate(
+            flops=8 * count * rows * bands * bands,
+            bytes_accessed=4 * partner.size + 8 * count * bands * bands,
+            transcendentals=0,
+        ),
+    )(own_of, coeffs, partner)
 
 
 def plane_products(own_ref, partner_ref):
@@ -142,7 +223,7 @@
             out_ref[:, d * bands : (d + 1) * bands] = acc_ref[d]
 
 
-TAKE = 2
+TAKE = 8
 
 
 def pair_specs(own, partner):
@@ -186,40 +267,74 @@
     )(own, partner, first)
 
 
+SIDES = 2
+
+
 def on_device(coeffs, neighbour, gshift):
     slab_points, parts, rows, bands = coeffs.shape
-    ka_count = lax.axis_size("ka")
-    here = lax.axis_index("ka")
-    wrapped = here >= ka_count - SHIFT_DEV
-    half = ka_count // 2
-    crosses = here % half >= half - SHIFT_DEV
+    ka_count, pw_count = lax.axis_size("ka"), lax.axis_size("pw")
+    wrapped = lax.axis_index("ka") >= ka_count - SHIFT_DEV
+    side = lax.axis_index("pw") % SIDES
+    points = lax.iota(jnp.int32, slab_points)
 
     def spread(block):
         return lax.all_to_all(block, "pw", split_axis=0, concat_axis=0, tiled=True)
 
     order = neighbour % slab_points
-    own = spread(coeffs)
-    straight = [((i + SHIFT_DEV) % ka_count, i) for i in range(ka_count)]
-    around = [(i // half * half + (i + SHIFT_DEV) % half, i) for i in range(ka_count)]
-    swap = [((i + half) % ka_count, i) for i in range(ka_count) if i % half >= half - SHIFT_DEV]
-    cut = rows // 2
-    direct = lax.ppermute(coeffs[:, 0], "ka", straight)
-    turned = lax.ppermute(coeffs[:, 1, cut:], "ka", around)
-    later = lax.ppermute(coeffs[:, 1, :cut], "ka", straight)
-    waiting = reordered(order, jnp.zeros((1,), jnp.int32), [direct])
-    own, waiting, turned = lax.optimization_barrier((own, waiting, turned))
-    swapped = lax.ppermute(turned, "ka", swap)
-    real = spread(waiting)
-    target = jnp.where(wrapped, gshift, lax.iota(jnp.int32, gshift.shape[0]))
-    moved = pltpu.with_memory_space_constraint(scattered_rows(own, target), pltpu.HBM)
-    moved, swapped, later = lax.optimization_barrier((moved, swapped, later))
-    waiting = reordered(order, crosses.astype(jnp.int32).reshape(1), [later], [turned, swapped])
-    real, waiting = lax.optimization_barrier((real, waiting))
-    imag = spread(waiting)
-    first = first_plane(moved, real)
-    products = second_plane(moved, imag, first)
-    products = spread(products).reshape(slab_points, bands // slab_points, 2, bands)
-    return jnp.transpose(products, (1, 0, 2, 3))
+    own_of = jnp.sum(jnp.where(order[None, :] == points[:, None], points[None, :], 0), axis=1)
+    inside = [(i + SHIFT_DEV, i) for i in range(ka_count - SHIFT_DEV)]
+    outside = [((i + SHIFT_DEV) % ka_count, i) for i in range(ka_count - SHIFT_DEV, ka_count)]
+
+    planes = ordered_planes(coeffs, jnp.where(wrapped, own_of, points))
+    levels = pw_count // SIDES
+    columns = [[z * SIDES + x for z in range(levels)] for x in range(SIDES)]
+    swap = [(i, i + 1 - 2 * (i % SIDES)) for i in range(pw_count)]
+    height = slab_points // 2
+    half = ka_count // 2
+    crossing = range(half - SHIFT_DEV, half)
+    relayed = (lax.axis_index("ka") >= crossing[0]) & (lax.axis_index("ka") <= crossing[-1])
+    first_leg = [(s, d + half if d in crossing else d) for s, d in inside]
+    second_leg = [(d + half, d) for d in crossing]
+
+    def part(i, block):
+        own = own_of[i * height : (i + 1) * height]
+        return slab_products(coeffs, block, own, levels)
+
+    def summed(block):
+        block = lax.psum_scatter(
+            block, "pw", scatter_dimension=0, axis_index_groups=columns, tiled=True
+        ).reshape(height, SIDES, bands // pw_count, 2 * bands)
+        keep = lax.dynamic_index_in_dim(block, side, 1, keepdims=False)
+        give = lax.dynamic_index_in_dim(block, 1 - side, 1, keepdims=False)
+        return keep + lax.ppermute(give, "pw", swap)
+
+    quarter = slab_points // 4
+    early = lax.ppermute(coeffs[: 2 * quarter], "ka", inside)
+    real = spread(planes[0])
+    real, later, early, middle, turned = lax.optimization_barrier(
+        (real, planes[1], early, coeffs[2 * quarter : 3 * quarter], coeffs[3 * quarter :])
+    )
+    imag = spread(later)
+    turned = lax.ppermute(turned, "ka", first_leg)
+    middle = lax.ppermute(middle, "ka", inside)
+    real_over = lax.ppermute(real, "ka", outside)
+    upper = part(0, early)
+    _, turned = lax.optimization_barrier((upper, turned))
+    swapped = lax.ppermute(turned, "ka", second_leg)
+    imag, middle, turned, swapped, real_over = lax.optimization_barrier(
+        (imag, middle, turned, swapped, real_over)
+    )
+    imag_over = lax.ppermute(imag, "ka", outside)
+    lower = part(1, jnp.concatenate([middle, jnp.where(relayed, swapped, turned)]))
+    within = jnp.concatenate([summed(upper), summed(lower)])
+    real, imag, _ = lax.optimization_barrier((real, imag, lower))
+    moved = scattered_rows([real, imag], gshift)
+    products = second_plane(moved, imag_over, first_plane(moved, real_over))
+    across = spread(products).reshape(slab_points, bands // pw_count, 2 * bands)
+
+    result = reordered(order, wrapped.astype(jnp.int32).reshape(1), [within, across])
+    result = result.reshape(slab_points, bands // pw_count, 2, bands)
+    return jnp.transpose(result, (1, 0, 2, 3))
 
 
 def solution(mesh):

time: 350 us -> 400 us (1.14)
  blocking collectives: 22 us -> 0 us
  waiting for transfers between devices: 209 us -> 230 us
  Pallas kernels: 73.5 us -> 88.4 us
  between operations: 0.11 us -> 13.6 us
  starting transfers between devices: 31.5 us -> 44.4 us
  other arithmetic: 1.16 us -> 10.2 us
    ppermute x4 -> x8, waiting for transfers between devices: 106 us -> 227 us  [the longest x1 103 us: on_device(): turned = lax.ppermute(turned, 'ka', first_leg)]
    all_to_all x3, waiting for transfers between devices: 103 us -> 2.69 us  [spread(): return lax.all_to_all(block, 'pw', split_axis=0, concat_axis=0, tiled=True)]
    pallas_call x0 -> x3, Pallas kernels: none -> 25.3 us  [the longest x2 19 us: slab_products(): pl.pallas_call(slab_kernel, grid_spec=pltpu.PrefetchScalarGridSpec(num_sc...]
    all_to_all x1 -> x0, blocking collectives: 22 us -> none  [spread(): return lax.all_to_all(block, 'pw', split_axis=0, concat_axis=0, tiled=True)]
    ppermute x4 -> x8, starting transfers between devices: 5.71 us -> 20.8 us  [the longest x1 4.5 us: on_device(): turned = lax.ppermute(turned, 'ka', first_leg)]
    pallas_call x2 -> x1, Pallas kernels: 8.13 us -> 2.57 us  [reordered(): pl.pallas_call(kernel, grid_spec=pltpu.PrefetchScalarGridSpec(num_scalar_...]
    slice x0 -> x3, local copies, waits for them, and re-layouts: none -> 4.85 us  [the longest x1 2.31 us: on_device(): early = lax.ppermute(coeffs[:2 * quarter], 'ka', inside)]
    concatenate x0 -> x2, other arithmetic: none -> 4.18 us  [the longest x1 3.34 us: on_device(): jnp.concatenate([middle, jnp.where(relayed, swapped, turned)])]
  transfers between devices with their start and end apart: 7 -> 13, of which waited for: 4 -> 7; matrix products, arithmetic and copies ran while one was open for 1% -> 4% of each run, Pallas kernels for 19% -> 18%
where the time goes in v6:
time: 400 us; the launch traced here: 398 us
  waiting for transfers between devices  230 us (58%)
  Pallas kernels  88.4 us (22%)
  starting transfers between devices  44.4 us (11%)
  between operations  13.6 us (3%)
  local copies, waits for them, and re-layouts  11.7 us (3%)
  other arithmetic  10.2 us (3%)
    ppermute x1, waiting for transfers between devices, on_device(): turned = lax.ppermute(turned, 'ka', first_leg)  103 us
    ppermute x1, waiting for transfers between devices, on_device(): early = lax.ppermute(coeffs[:2 * quarter], 'ka', inside)  62.9 us
    pallas_call x1, Pallas kernels, scattered_rows(): pl.pallas_call(scatter_rows_kernel, grid=(total // height,), in_specs=[pl...  49.3 us
    ppermute x1, waiting for transfers between devices, on_device(): swapped = lax.ppermute(turned, 'ka', second_leg)  32.6 us
    all_to_all x3, starting transfers between devices, spread(): return lax.all_to_all(block, 'pw', split_axis=0, concat_axis=0, tiled=True)  23.5 us
    pallas_call x2, Pallas kernels, slab_products(): pl.pallas_call(slab_kernel, grid_spec=pltpu.PrefetchScalarGridSpec(num_sc...  19 us
    ppermute x1, waiting for transfers between devices, on_device(): imag_over = lax.ppermute(imag, 'ka', outside)  16.9 us
    ppermute x2, waiting for transfers between devices, summed(): return keep + lax.ppermute(give, 'pw', swap)  11.8 us
  transfers between devices with their start and end apart: 13, of which 7 were waited for; matrix products, arithmetic and copies ran while one was open for 4% of the time, Pallas kernels for 18%

profile of v6, /device:TPU:26, one launch (start us, length us, event | category | flops | bytes accessed | tf_op | source)
XLA Modules:
  0.0 398.4 jit_solution(2469141534352580092)
XLA Ops:
  7.8 6.3 %shard_map.37 = (bf16[16,384,256]{2,1,0:T(8,128)(2,1)}, bf16[16,384,256]{2,1,0:T(8,128)(2,1)}) custom-call(s32[16]{0:T(128)} %broadcast_select_fusion.1.order, bf16[16,2,384,256]{3,2,1,0:T(8,128)(2,1)} %own_ref.3), custom_call_target="tpu_custom_call" | custom-call | bytes 12582912 | tf_op jit(solution)/shard_map/pallas_call | solution.py:128
  14.1 10.1 %all-to-all-start = ((bf16[16,384,256]{2,1,0:T(8,128)(2,1)}), bf16[16,384,256]{2,1,0:T(8,128)(2,1)S(1)}, u32[]{:S(2)}, u32[]{:S(2)}) async-start(bf16[16,384,256]{2,1,0:T(8,128)(2,1)} %get-tuple-element.20), calls=%async_computation | async-start | bytes 6291456 | tf_op jit(solution)/shard_map/all_to_all | solution.py:281
  24.4 2.3 slice.16
  26.7 4.4 %collective-permute-start = (bf16[8,2,384,256]{3,2,1,0:T(8,128)(2,1)S(1)}, bf16[8,2,384,256]{3,2,1,0:T(8,128)(2,1)}, u32[]{:S(2)}, u32[]{:S(2)}) collective-permute-start(bf16[8,2,384,256]{3,2,1,0:T(8,128)(2,1)S(1)} %slice.16), channel_id=1, source_target_pairs={{32,0},{48,16},{64,32},{80,48},{96,64},{112,80},{128,96},{144,112}... | collective-permute-start | bytes 9437192 | tf_op jit(solution)/shard_map/ppermute | solution.py:312
  31.7 1.9 fusion.1
  33.7 62.9 %collective-permute-done.partner_ref = bf16[8,2,384,256]{3,2,1,0:T(8,128)(2,1)} collective-permute-done((bf16[8,2,384,256]{3,2,1,0:T(8,128)(2,1)S(1)}, bf16[8,2,384,256]{3,2,1,0:T(8,128)(2,1)}, u32[]{:S(2)}, u32[]{:S(2)}) %collective-permute-start) | collective-permute-done | bytes 3145760 | tf_op jit(solution)/shard_map/ppermute | solution.py:312
  96.5 2.7 all-to-all-done.real_ref
  99.2 9.7 %shard_map.38 = f32[8,8,32,512]{3,2,1,0:T(8,128)} custom-call(s32[8]{0:T(128)} %get-tuple-element.37.own_of, bf16[16,2,384,256]{3,2,1,0:T(8,128)(2,1)} %own_ref.3, bf16[8,2,384,256]{3,2,1,0:T(8,128)(2,1)} %collective-permute-done.partner_ref), custom_call_target="tpu_custom_call" | custom-call | flops 1610612736 | bytes 10485760 | tf_op jit(solution)/shard_map/pallas_call | solution.py:167
  108.9 6.7 %all-to-all-start.1 = ((bf16[16,384,256]{2,1,0:T(8,128)(2,1)}), bf16[16,384,256]{2,1,0:T(8,128)(2,1)}, u32[]{:S(2)}, u32[]{:S(2)}) async-start(bf16[16,384,256]{2,1,0:T(8,128)(2,1)} %get-tuple-element.23), calls=%async_computation.2 | async-start | bytes 6291456 | tf_op jit(solution)/shard_map/all_to_all | solution.py:281
  115.7 4.5 %collective-permute-start.3 = (bf16[4,2,384,256]{3,2,1,0:T(8,128)(2,1)}, bf16[4,2,384,256]{3,2,1,0:T(8,128)(2,1)}, u32[]{:S(2)}, u32[]{:S(2)}) collective-permute-start(bf16[4,2,384,256]{3,2,1,0:T(8,128)(2,1)} %get-tuple-element.25), channel_id=1, source_target_pairs={{32,0},{48,16},{64,32},{80,48},{96,64},{112,80},{128,224},{144,240... | collective-permute-start | bytes 4718600 | tf_op jit(solution)/shard_map/ppermute | solution.py:318
  120.2 1.3 collective-permute-start.5
  121.5 3.1 collective-permute-start.2
  124.6 103.3 %collective-permute-done.3 = bf16[4,2,384,256]{3,2,1,0:T(8,128)(2,1)} collective-permute-done((bf16[4,2,384,256]{3,2,1,0:T(8,128)(2,1)}, bf16[4,2,384,256]{3,2,1,0:T(8,128)(2,1)}, u32[]{:S(2)}, u32[]{:S(2)}) %collective-permute-start.3) | collective-permute-done | bytes 1572896 | tf_op jit(solution)/shard_map/ppermute | solution.py:318
  227.9 2.5 collective-permute-start.4
  230.4 32.6 %collective-permute-done.4 = bf16[4,2,384,256]{3,2,1,0:T(8,128)(2,1)} collective-permute-done((bf16[4,2,384,256]{3,2,1,0:T(8,128)(2,1)}, bf16[4,2,384,256]{3,2,1,0:T(8,128)(2,1)}, u32[]{:S(2)}, u32[]{:S(2)}) %collective-permute-start.4) | collective-permute-done | bytes 1572896 | tf_op jit(solution)/shard_map/ppermute | solution.py:323
  263.0 2.7 broadcast_select_fusion
  265.7 3.3 pad_maximum_fusion.partner_ref
  269.1 9.3 %shard_map.39 = f32[8,8,32,512]{3,2,1,0:T(8,128)} custom-call(s32[8]{0:T(128)} %get-tuple-element.38.own_of, bf16[16,2,384,256]{3,2,1,0:T(8,128)(2,1)} %own_ref.3, bf16[8,2,384,256]{3,2,1,0:T(8,128)(2,1)} %pad_maximum_fusion.partner_ref), custom_call_target="tpu_custom_call" | custom-call | flops 1610612736 | bytes 10485760 | tf_op jit(solution)/shard_map/pallas_call | solution.py:167
  278.3 1.3 collective-permute-start.7
  279.6 49.3 %shard_map.40.own_ref = bf16[2,256,6144]{2,1,0:T(8,128)(2,1)} custom-call(s32[1,6144]{1,0:T(1,128)} %bitcast.29, bf16[16,384,256]{2,1,0:T(8,128)(2,1)} %copy-done.2, bf16[16,384,256]{2,1,0:T(8,128)(2,1)} %all-to-all-done.1.imag_ref), custom_call_target="tpu_custom_call" | custom-call | flops 38654705664 | bytes 12582912 | tf_op jit(solution)/shard_map/pallas_call | solution.py:94
  328.9 5.5 %shard_map.41.first_ref = f32[2,256,256]{2,1,0:T(8,128)} custom-call(bf16[2,256,6144]{2,1,0:T(8,128)(2,1)} %shard_map.40.own_ref, bf16[16,384,256]{2,1,0:T(8,128)(2,1)} %copy-done.1), custom_call_target="tpu_custom_call" | custom-call | flops 1610612736 | bytes 9437184 | tf_op jit(solution)/shard_map/pallas_call | solution.py:244
  334.5 16.9 %collective-permute-done.7.partner_ref = bf16[16,384,256]{2,1,0:T(8,128)(2,1)S(1)} collective-permute-done((bf16[16,384,256]{2,1,0:T(8,128)(2,1)}, bf16[16,384,256]{2,1,0:T(8,128)(2,1)S(1)}, u32[]{:S(2)}, u32[]{:S(2)}) %collective-permute-start.7) | collective-permute-done | bytes 3145760 | tf_op jit(solution)/shard_map/ppermute | solution.py:327
  351.3 1.6 copy-done.3
  353.0 5.7 %shard_map.42 = f32[256,512]{1,0:T(8,128)} custom-call(bf16[2,256,6144]{2,1,0:T(8,128)(2,1)} %shard_map.40.own_ref, bf16[16,384,256]{2,1,0:T(8,128)(2,1)} %copy-done.3, f32[2,256,256]{2,1,0:T(8,128)} %shard_map.41.first_ref), custom_call_target="tpu_custom_call" | custom-call | flops 1610612736 | bytes 9437184 | tf_op jit(solution)/shard_map/pallas_call | solution.py:258
  358.7 6.7 %all-to-all-start.2 = ((f32[16,16,512]{2,1,0:T(8,128)}), f32[16,16,512]{2,1,0:T(8,128)S(1)}, u32[]{:S(2)}, u32[]{:S(2)}) async-start(f32[16,16,512]{2,1,0:T(8,128)} %bitcast.24), calls=%async_computation.4 | async-start | bytes 1048576 | tf_op jit(solution)/shard_map/all_to_all | solution.py:281
  366.4 3.5 collective-permute-start.1
  371.1 9.6 %collective-permute-done.1 = f32[8,16,512]{2,1,0:T(8,128)S(1)} collective-permute-done((f32[8,16,512]{2,1,0:T(8,128)S(1)}, f32[8,16,512]{2,1,0:T(8,128)S(1)}, u32[]{:S(2)}, u32[]{:S(2)}) %collective-permute-start.1) | collective-permute-done | bytes 262176 | tf_op jit(solution)/shard_map/ppermute | solution.py:309
  380.7 1.0 bitcast_add_fusion.1
  381.7 2.2 collective-permute-done.6
  386.5 2.6 shard_map.43
  389.1 1.4 reshape.27
  390.5 1.1 copy.19
  (30 shorter events, 6.8 us)
Async XLA Ops:
  7.2 6.9 %copy-start.5 = (s32[16]{0:T(128)}, s32[16]{0:T(128)S(1)}, u32[]{:S(2)}) copy-start(s32[16]{0:T(128)S(1)} %and_select_fusion.order) | copy-start | bytes 196
  14.1 85.1 %all-to-all-start = ((bf16[16,384,256]{2,1,0:T(8,128)(2,1)}), bf16[16,384,256]{2,1,0:T(8,128)(2,1)S(1)}, u32[]{:S(2)}, u32[]{:S(2)}) async-start(bf16[16,384,256]{2,1,0:T(8,128)(2,1)} %get-tuple-element.20), calls=%async_computation | async-start | bytes 6291456 | tf_op jit(solution)/shard_map/all_to_all | solution.py:281
  24.3 341.1 %reduce-scatter.3.cloned.1.call-start = ((), (), s32[]{:S(2)}) async-start(), calls=%async_computation.5 | async-start | bytes 4718592 | tf_op jit(solution)/shard_map/reduce_scatter | solution.py:304
  24.3 7.4 %copy-start = (bf16[16,2,384,256]{3,2,1,0:T(8,128)(2,1)S(1)}, bf16[16,2,384,256]{3,2,1,0:T(8,128)(2,1)}, u32[]{:S(2)}) copy-start(bf16[16,2,384,256]{3,2,1,0:T(8,128)(2,1)} %own_ref.3) | copy-start | bytes 18874372
  26.7 69.8 %collective-permute-start = (bf16[8,2,384,256]{3,2,1,0:T(8,128)(2,1)S(1)}, bf16[8,2,384,256]{3,2,1,0:T(8,128)(2,1)}, u32[]{:S(2)}, u32[]{:S(2)}) collective-permute-start(bf16[8,2,384,256]{3,2,1,0:T(8,128)(2,1)S(1)} %slice.16), channel_id=1, source_target_pairs={{32,0},{48,16},{64,32},{80,48},{96,64},{112,80},{128,96},{144,112}... | collective-permute-start | bytes 9437192 | tf_op jit(solution)/shard_map/ppermute | solution.py:312
  99.2 9.7 %copy-start.2 = (bf16[16,384,256]{2,1,0:T(8,128)(2,1)}, bf16[16,384,256]{2,1,0:T(8,128)(2,1)S(1)}, u32[]{:S(2)}) copy-start(bf16[16,384,256]{2,1,0:T(8,128)(2,1)S(1)} %all-to-all-done.real_ref) | copy-start | bytes 9437188
  108.9 154.1 %all-to-all-start.1 = ((bf16[16,384,256]{2,1,0:T(8,128)(2,1)}), bf16[16,384,256]{2,1,0:T(8,128)(2,1)}, u32[]{:S(2)}, u32[]{:S(2)}) async-start(bf16[16,384,256]{2,1,0:T(8,128)(2,1)} %get-tuple-element.23), calls=%async_computation.2 | async-start | bytes 6291456 | tf_op jit(solution)/shard_map/all_to_all | solution.py:281
  115.7 254.2 %reduce-scatter.5.cloned.1.call-start = ((), (), s32[]{:S(2)}) async-start(), calls=%async_computation.6 | async-start | bytes 4718592 | tf_op jit(solution)/shard_map/reduce_scatter | solution.py:304
  115.7 112.2 %collective-permute-start.3 = (bf16[4,2,384,256]{3,2,1,0:T(8,128)(2,1)}, bf16[4,2,384,256]{3,2,1,0:T(8,128)(2,1)}, u32[]{:S(2)}, u32[]{:S(2)}) collective-permute-start(bf16[4,2,384,256]{3,2,1,0:T(8,128)(2,1)} %get-tuple-element.25), channel_id=1, source_target_pairs={{32,0},{48,16},{64,32},{80,48},{96,64},{112,80},{128,224},{144,240... | collective-permute-start | bytes 4718600 | tf_op jit(solution)/shard_map/ppermute | solution.py:318
  120.2 142.8 %collective-permute-start.5 = (bf16[16,384,256]{2,1,0:T(8,128)(2,1)}, bf16[16,384,256]{2,1,0:T(8,128)(2,1)S(1)}, u32[]{:S(2)}, u32[]{:S(2)}) collective-permute-start(bf16[16,384,256]{2,1,0:T(8,128)(2,1)} %copy-done.2), channel_id=1, source_target_pairs={{0,224},{16,240},{1,225},{17,241},{2,226},{18,242},{3,227},{19,243... | collective-permute-start | bytes 9437192 | tf_op jit(solution)/shard_map/ppermute | solution.py:320
  121.5 108.9 %collective-permute-start.2 = (bf16[4,2,384,256]{3,2,1,0:T(8,128)(2,1)}, bf16[4,2,384,256]{3,2,1,0:T(8,128)(2,1)}, u32[]{:S(2)}, u32[]{:S(2)}) collective-permute-start(bf16[4,2,384,256]{3,2,1,0:T(8,128)(2,1)} %get-tuple-element.24), channel_id=1, source_target_pairs={{32,0},{48,16},{64,32},{80,48},{96,64},{112,80},{128,96},{144,112}... | collective-permute-start | bytes 4718600 | tf_op jit(solution)/shard_map/ppermute | solution.py:319
  227.9 35.1 %collective-permute-start.4 = (bf16[4,2,384,256]{3,2,1,0:T(8,128)(2,1)}, bf16[4,2,384,256]{3,2,1,0:T(8,128)(2,1)}, u32[]{:S(2)}, u32[]{:S(2)}) collective-permute-start(bf16[4,2,384,256]{3,2,1,0:T(8,128)(2,1)} %collective-permute-done.3), channel_id=1, source_target_pairs={{224,96},{240,112},{225,97},{241,113},{226,98},{242,114},{227,99},... | collective-permute-start | bytes 4718600 | tf_op jit(solution)/shard_map/ppermute | solution.py:323
  263.0 6.1 %copy-start.1 = (bf16[16,384,256]{2,1,0:T(8,128)(2,1)}, bf16[16,384,256]{2,1,0:T(8,128)(2,1)S(1)}, u32[]{:S(2)}) copy-start(bf16[16,384,256]{2,1,0:T(8,128)(2,1)S(1)} %collective-permute-done.5.partner_ref) | copy-start | bytes 9437188
  278.3 73.0 %collective-permute-start.7 = (bf16[16,384,256]{2,1,0:T(8,128)(2,1)}, bf16[16,384,256]{2,1,0:T(8,128)(2,1)S(1)}, u32[]{:S(2)}, u32[]{:S(2)}) collective-permute-start(bf16[16,384,256]{2,1,0:T(8,128)(2,1)} %all-to-all-done.1.imag_ref), channel_id=1, source_target_pairs={{0,224},{16,240},{1,225},{17,241},{2,226},{18,242},{3,227},{19,243... | collective-permute-start | bytes 9437192 | tf_op jit(solution)/shard_map/ppermute | solution.py:327
  351.3 1.6 copy-start.3
  358.7 27.0 %all-to-all-start.2 = ((f32[16,16,512]{2,1,0:T(8,128)}), f32[16,16,512]{2,1,0:T(8,128)S(1)}, u32[]{:S(2)}, u32[]{:S(2)}) async-start(f32[16,16,512]{2,1,0:T(8,128)} %bitcast.24), calls=%async_computation.4 | async-start | bytes 1048576 | tf_op jit(solution)/shard_map/all_to_all | solution.py:281
  366.4 14.3 %collective-permute-start.1 = (f32[8,16,512]{2,1,0:T(8,128)S(1)}, f32[8,16,512]{2,1,0:T(8,128)S(1)}, u32[]{:S(2)}, u32[]{:S(2)}) collective-permute-start(f32[8,16,512]{2,1,0:T(8,128)S(1)} %dynamic-slice_bitcast_fusion.1), channel_id=1, source_target_pairs={{0,1},{1,0},{2,3},{3,2},{4,5},{5,4},{6,7},{7,6},{8,9},{9,8},{10,11... | collective-permute-start | bytes 786440 | tf_op jit(solution)/shard_map/ppermute | solution.py:309
  370.9 13.0 %collective-permute-start.6 = (f32[8,16,512]{2,1,0:T(8,128)S(1)}, f32[8,16,512]{2,1,0:T(8,128)S(1)}, u32[]{:S(2)}, u32[]{:S(2)}) collective-permute-start(f32[8,16,512]{2,1,0:T(8,128)S(1)} %dynamic-slice_bitcast_fusion), channel_id=1, source_target_pairs={{0,1},{1,0},{2,3},{3,2},{4,5},{5,4},{6,7},{7,6},{8,9},{9,8},{10,11... | collective-permute-start | bytes 786440 | tf_op jit(solution)/shard_map/ppermute | solution.py:309
  385.7 0.8 copy-start.4
Sparse Core Ops, SparseCore 0:
  109.1 116.3 reduce-scatter.2
  278.5 56.8 reduce-scatter.4

commit v7 on v6

--- a/solution.py
+++ b/solution.py
@@ -290,12 +290,6 @@
     columns = [[z * SIDES + x for z in range(levels)] for x in range(SIDES)]
     swap = [(i, i + 1 - 2 * (i % SIDES)) for i in range(pw_count)]
     height = slab_points // 2
-    half = ka_count // 2
-    crossing = range(half - SHIFT_DEV, half)
-    relayed = (lax.axis_index("ka") >= crossing[0]) & (lax.axis_index("ka") <= crossing[-1])
-    first_leg = [(s, d + half if d in crossing else d) for s, d in inside]
-    second_leg = [(d + half, d) for d in crossing]
-
     def part(i, block):
         own = own_of[i * height : (i + 1) * height]
         return slab_products(coeffs, block, own, levels)
@@ -308,24 +302,16 @@
         give = lax.dynamic_index_in_dim(block, 1 - side, 1, keepdims=False)
         return keep + lax.ppermute(give, "pw", swap)
 
-    quarter = slab_points // 4
-    early = lax.ppermute(coeffs[: 2 * quarter], "ka", inside)
+    early = lax.ppermute(coeffs[:height], "ka", inside)
     real = spread(planes[0])
-    real, later, early, middle, turned = lax.optimization_barrier(
-        (real, planes[1], early, coeffs[2 * quarter : 3 * quarter], coeffs[3 * quarter :])
-    )
+    real, later, early, late = lax.optimization_barrier((real, planes[1], early, coeffs[height:]))
     imag = spread(later)
-    turned = lax.ppermute(turned, "ka", first_leg)
-    middle = lax.ppermute(middle, "ka", inside)
+    late = lax.ppermute(late, "ka", inside)
     real_over = lax.ppermute(real, "ka", outside)
     upper = part(0, early)
-    _, turned = lax.optimization_barrier((upper, turned))
-    swapped = lax.ppermute(turned, "ka", second_leg)
-    imag, middle, turned, swapped, real_over = lax.optimization_barrier(
-        (imag, middle, turned, swapped, real_over)
-    )
+    imag, _, late, real_over = lax.optimization_barrier((imag, upper, late, real_over))
     imag_over = lax.ppermute(imag, "ka", outside)
-    lower = part(1, jnp.concatenate([middle, jnp.where(relayed, swapped, turned)]))
+    lower = part(1, late)
     within = jnp.concatenate([summed(upper), summed(lower)])
     real, imag, _ = lax.optimization_barrier((real, imag, lower))
     moved = scattered_rows([real, imag], gshift)

time: 400 us -> 370 us (0.925)
  the two profiles are of different devices: /device:TPU:26 before, /device:TPU:24 now
where the time goes in v7:
time: 370 us; the launch traced here: 369 us
  waiting for transfers between devices  212 us (57%)
  Pallas kernels  88.3 us (24%)
  starting transfers between devices  39 us (11%)
  between operations  13.5 us (4%)
  local copies, waits for them, and re-layouts  12.5 us (3%)
  other arithmetic  4.11 us (1%)
    ppermute x1, waiting for transfers between devices, on_device(): early = lax.ppermute(coeffs[:height], 'ka', inside)  99.9 us
    ppermute x1, waiting for transfers between devices, on_device(): late = lax.ppermute(late, 'ka', inside)  99.1 us
    pallas_call x1, Pallas kernels, scattered_rows(): pl.pallas_call(scatter_rows_kernel, grid=(total // height,), in_specs=[pl...  49.3 us
    all_to_all x3, starting transfers between devices, spread(): return lax.all_to_all(block, 'pw', split_axis=0, concat_axis=0, tiled=True)  28.9 us
    pallas_call x2, Pallas kernels, slab_products(): pl.pallas_call(slab_kernel, grid_spec=pltpu.PrefetchScalarGridSpec(num_sc...  18.9 us
    ppermute x2, waiting for transfers between devices, summed(): return keep + lax.ppermute(give, 'pw', swap)  11.7 us
  transfers between devices with their start and end apart: 11, of which 5 were waited for; matrix products, arithmetic and copies ran while one was open for 3% of the time, Pallas kernels for 19%

profile of v7, /device:TPU:24, one launch (start us, length us, event | category | flops | bytes accessed | tf_op | source)
XLA Modules:
  0.0 369.4 jit_solution(11878726001678727957)
XLA Ops:
  6.5 0.7 and_select_fusion.order
  7.8 6.3 %shard_map.37 = (bf16[16,384,256]{2,1,0:T(8,128)(2,1)}, bf16[16,384,256]{2,1,0:T(8,128)(2,1)}) custom-call(s32[16]{0:T(128)} %broadcast_select_fusion.order, bf16[16,2,384,256]{3,2,1,0:T(8,128)(2,1)} %own_ref.3), custom_call_target="tpu_custom_call" | custom-call | bytes 12582912 | tf_op jit(solution)/shard_map/pallas_call | solution.py:128
  14.1 11.0 %all-to-all-start = ((bf16[16,384,256]{2,1,0:T(8,128)(2,1)}), bf16[16,384,256]{2,1,0:T(8,128)(2,1)S(1)}, u32[]{:S(2)}, u32[]{:S(2)}) async-start(bf16[16,384,256]{2,1,0:T(8,128)(2,1)} %get-tuple-element.16), calls=%async_computation | async-start | bytes 6291456 | tf_op jit(solution)/shard_map/all_to_all | solution.py:281
  25.2 5.0 %fusion.1 = (bf16[8,2,384,256]{3,2,1,0:T(8,128)(2,1)}, bf16[8,2,384,256]{3,2,1,0:T(8,128)(2,1)S(1)}) fusion(bf16[16,2,384,256]{3,2,1,0:T(8,128)(2,1)} %own_ref.3), kind=kLoop, calls=%fused_computation.13 | loop fusion | bytes 12582912 | tf_op jit(solution)/shard_map/slice | solution.py:307
  30.3 2.6 collective-permute-start
  32.9 0.6 fusion.2
  33.5 99.9 %collective-permute-done.partner_ref = bf16[8,2,384,256]{3,2,1,0:T(8,128)(2,1)} collective-permute-done((bf16[8,2,384,256]{3,2,1,0:T(8,128)(2,1)S(1)}, bf16[8,2,384,256]{3,2,1,0:T(8,128)(2,1)}, u32[]{:S(2)}, u32[]{:S(2)}) %collective-permute-start) | collective-permute-done | bytes 3145760 | tf_op jit(solution)/shard_map/ppermute | solution.py:305
  133.4 9.6 %shard_map.38 = f32[8,8,32,512]{3,2,1,0:T(8,128)} custom-call(s32[8]{0:T(128)} %get-tuple-element.29.own_of, bf16[16,2,384,256]{3,2,1,0:T(8,128)(2,1)} %own_ref.3, bf16[8,2,384,256]{3,2,1,0:T(8,128)(2,1)} %collective-permute-done.partner_ref), custom_call_target="tpu_custom_call" | custom-call | flops 1610612736 | bytes 10485760 | tf_op jit(solution)/shard_map/pallas_call | solution.py:167
  143.1 9.4 %all-to-all-start.1 = ((bf16[16,384,256]{2,1,0:T(8,128)(2,1)}), bf16[16,384,256]{2,1,0:T(8,128)(2,1)}, u32[]{:S(2)}, u32[]{:S(2)}) async-start(bf16[16,384,256]{2,1,0:T(8,128)(2,1)} %get-tuple-element.19), calls=%async_computation.2 | async-start | bytes 6291456 | tf_op jit(solution)/shard_map/all_to_all | solution.py:281
  152.6 1.9 collective-permute-start.2
  154.5 0.9 collective-permute-start.3
  155.4 99.1 %collective-permute-done.2.partner_ref = bf16[8,2,384,256]{3,2,1,0:T(8,128)(2,1)} collective-permute-done((bf16[8,2,384,256]{3,2,1,0:T(8,128)(2,1)}, bf16[8,2,384,256]{3,2,1,0:T(8,128)(2,1)}, u32[]{:S(2)}, u32[]{:S(2)}) %collective-permute-start.2) | collective-permute-done | bytes 3145760 | tf_op jit(solution)/shard_map/ppermute | solution.py:309
  254.5 1.3 all-to-all-done.1.imag_ref
  255.7 9.2 %shard_map.39 = f32[8,8,32,512]{3,2,1,0:T(8,128)} custom-call(s32[8]{0:T(128)} %get-tuple-element.30.own_of, bf16[16,2,384,256]{3,2,1,0:T(8,128)(2,1)} %own_ref.3, bf16[8,2,384,256]{3,2,1,0:T(8,128)(2,1)} %collective-permute-done.2.partner_ref), custom_call_target="tpu_custom_call" | custom-call | flops 1610612736 | bytes 10485760 | tf_op jit(solution)/shard_map/pallas_call | solution.py:167
  265.0 0.9 collective-permute-start.5
  265.9 49.3 %shard_map.40.own_ref = bf16[2,256,6144]{2,1,0:T(8,128)(2,1)} custom-call(s32[1,6144]{1,0:T(1,128)} %bitcast.29, bf16[16,384,256]{2,1,0:T(8,128)(2,1)} %copy-done.1, bf16[16,384,256]{2,1,0:T(8,128)(2,1)} %all-to-all-done.1.imag_ref), custom_call_target="tpu_custom_call" | custom-call | flops 38654705664 | bytes 12582912 | tf_op jit(solution)/shard_map/pallas_call | solution.py:94
  315.1 5.6 %shard_map.41.first_ref = f32[2,256,256]{2,1,0:T(8,128)} custom-call(bf16[2,256,6144]{2,1,0:T(8,128)(2,1)} %shard_map.40.own_ref, bf16[16,384,256]{2,1,0:T(8,128)(2,1)} %copy-done), custom_call_target="tpu_custom_call" | custom-call | flops 1610612736 | bytes 9437184 | tf_op jit(solution)/shard_map/pallas_call | solution.py:244
  320.7 1.6 copy-done.2
  322.4 5.7 %shard_map.42 = f32[256,512]{1,0:T(8,128)} custom-call(bf16[2,256,6144]{2,1,0:T(8,128)(2,1)} %shard_map.40.own_ref, bf16[16,384,256]{2,1,0:T(8,128)(2,1)} %copy-done.2, f32[2,256,256]{2,1,0:T(8,128)} %shard_map.41.first_ref), custom_call_target="tpu_custom_call" | custom-call | flops 1610612736 | bytes 9437184 | tf_op jit(solution)/shard_map/pallas_call | solution.py:258
  328.1 8.4 %all-to-all-start.2 = ((f32[16,16,512]{2,1,0:T(8,128)}), f32[16,16,512]{2,1,0:T(8,128)S(1)}, u32[]{:S(2)}, u32[]{:S(2)}) async-start(f32[16,16,512]{2,1,0:T(8,128)} %bitcast.24), calls=%async_computation.4 | async-start | bytes 1048576 | tf_op jit(solution)/shard_map/all_to_all | solution.py:281
  336.6 1.0 dynamic-slice_bitcast_fusion.1
  337.6 3.5 collective-permute-start.1
  341.1 1.0 dynamic-slice_bitcast_fusion
  342.3 9.5 %collective-permute-done.1 = f32[8,16,512]{2,1,0:T(8,128)S(1)} collective-permute-done((f32[8,16,512]{2,1,0:T(8,128)S(1)}, f32[8,16,512]{2,1,0:T(8,128)S(1)}, u32[]{:S(2)}, u32[]{:S(2)}) %collective-permute-start.1) | collective-permute-done | bytes 262176 | tf_op jit(solution)/shard_map/ppermute | solution.py:303
  351.8 1.0 bitcast_add_fusion.1
  352.8 2.2 collective-permute-done.4
  354.9 1.0 bitcast_add_fusion
  355.9 0.8 pad_maximum_fusion.refs_0_
  356.8 0.8 copy-done.3
  357.6 2.6 shard_map.43
  360.1 1.4 reshape.27
  361.5 1.1 copy.19
  (21 shorter events, 1.0 us)
Async XLA Ops:
  7.2 6.9 %copy-start.4 = (s32[16]{0:T(128)}, s32[16]{0:T(128)S(1)}, u32[]{:S(2)}) copy-start(s32[16]{0:T(128)S(1)} %and_select_fusion.order) | copy-start | bytes 196
  14.1 119.3 %all-to-all-start = ((bf16[16,384,256]{2,1,0:T(8,128)(2,1)}), bf16[16,384,256]{2,1,0:T(8,128)(2,1)S(1)}, u32[]{:S(2)}, u32[]{:S(2)}) async-start(bf16[16,384,256]{2,1,0:T(8,128)(2,1)} %get-tuple-element.16), calls=%async_computation | async-start | bytes 6291456 | tf_op jit(solution)/shard_map/all_to_all | solution.py:281
  25.2 311.4 %reduce-scatter.3.cloned.1.call-start = ((), (), s32[]{:S(2)}) async-start(), calls=%async_computation.5 | async-start | bytes 4718592 | tf_op jit(solution)/shard_map/reduce_scatter | solution.py:298
  30.3 103.2 %collective-permute-start = (bf16[8,2,384,256]{3,2,1,0:T(8,128)(2,1)S(1)}, bf16[8,2,384,256]{3,2,1,0:T(8,128)(2,1)}, u32[]{:S(2)}, u32[]{:S(2)}) collective-permute-start(bf16[8,2,384,256]{3,2,1,0:T(8,128)(2,1)S(1)} %get-tuple-element.28), channel_id=1, source_target_pairs={{32,0},{48,16},{64,32},{80,48},{96,64},{112,80},{128,96},{144,112}... | collective-permute-start | bytes 9437192 | tf_op jit(solution)/shard_map/ppermute | solution.py:305
  133.4 9.6 %copy-start.1 = (bf16[16,384,256]{2,1,0:T(8,128)(2,1)}, bf16[16,384,256]{2,1,0:T(8,128)(2,1)S(1)}, u32[]{:S(2)}) copy-start(bf16[16,384,256]{2,1,0:T(8,128)(2,1)S(1)} %all-to-all-done.real_ref) | copy-start | bytes 9437188
  143.1 112.6 %all-to-all-start.1 = ((bf16[16,384,256]{2,1,0:T(8,128)(2,1)}), bf16[16,384,256]{2,1,0:T(8,128)(2,1)}, u32[]{:S(2)}, u32[]{:S(2)}) async-start(bf16[16,384,256]{2,1,0:T(8,128)(2,1)} %get-tuple-element.19), calls=%async_computation.2 | async-start | bytes 6291456 | tf_op jit(solution)/shard_map/all_to_all | solution.py:281
  152.5 188.6 %reduce-scatter.5.cloned.1.call-start = ((), (), s32[]{:S(2)}) async-start(), calls=%async_computation.6 | async-start | bytes 4718592 | tf_op jit(solution)/shard_map/reduce_scatter | solution.py:298
  152.6 101.9 %collective-permute-start.2 = (bf16[8,2,384,256]{3,2,1,0:T(8,128)(2,1)}, bf16[8,2,384,256]{3,2,1,0:T(8,128)(2,1)}, u32[]{:S(2)}, u32[]{:S(2)}) collective-permute-start(bf16[8,2,384,256]{3,2,1,0:T(8,128)(2,1)} %get-tuple-element.20), channel_id=1, source_target_pairs={{32,0},{48,16},{64,32},{80,48},{96,64},{112,80},{128,96},{144,112}... | collective-permute-start | bytes 9437192 | tf_op jit(solution)/shard_map/ppermute | solution.py:309
  154.5 100.0 %collective-permute-start.3 = (bf16[16,384,256]{2,1,0:T(8,128)(2,1)}, bf16[16,384,256]{2,1,0:T(8,128)(2,1)S(1)}, u32[]{:S(2)}, u32[]{:S(2)}) collective-permute-start(bf16[16,384,256]{2,1,0:T(8,128)(2,1)} %copy-done.1), channel_id=1, source_target_pairs={{0,224},{16,240},{1,225},{17,241},{2,226},{18,242},{3,227},{19,243... | collective-permute-start | bytes 9437192 | tf_op jit(solution)/shard_map/ppermute | solution.py:310
  254.5 10.5 %copy-start = (bf16[16,384,256]{2,1,0:T(8,128)(2,1)}, bf16[16,384,256]{2,1,0:T(8,128)(2,1)S(1)}, u32[]{:S(2)}) copy-start(bf16[16,384,256]{2,1,0:T(8,128)(2,1)S(1)} %collective-permute-done.3.partner_ref) | copy-start | bytes 9437188
  265.0 55.8 %collective-permute-start.5 = (bf16[16,384,256]{2,1,0:T(8,128)(2,1)}, bf16[16,384,256]{2,1,0:T(8,128)(2,1)S(1)}, u32[]{:S(2)}, u32[]{:S(2)}) collective-permute-start(bf16[16,384,256]{2,1,0:T(8,128)(2,1)} %all-to-all-done.1.imag_ref), channel_id=1, source_target_pairs={{0,224},{16,240},{1,225},{17,241},{2,226},{18,242},{3,227},{19,243... | collective-permute-start | bytes 9437192 | tf_op jit(solution)/shard_map/ppermute | solution.py:313
  320.7 1.7 copy-start.2
  328.1 28.7 %all-to-all-start.2 = ((f32[16,16,512]{2,1,0:T(8,128)}), f32[16,16,512]{2,1,0:T(8,128)S(1)}, u32[]{:S(2)}, u32[]{:S(2)}) async-start(f32[16,16,512]{2,1,0:T(8,128)} %bitcast.24), calls=%async_computation.4 | async-start | bytes 1048576 | tf_op jit(solution)/shard_map/all_to_all | solution.py:281
  337.6 14.2 %collective-permute-start.1 = (f32[8,16,512]{2,1,0:T(8,128)S(1)}, f32[8,16,512]{2,1,0:T(8,128)S(1)}, u32[]{:S(2)}, u32[]{:S(2)}) collective-permute-start(f32[8,16,512]{2,1,0:T(8,128)S(1)} %dynamic-slice_bitcast_fusion.1), channel_id=1, source_target_pairs={{0,1},{1,0},{2,3},{3,2},{4,5},{5,4},{6,7},{7,6},{8,9},{9,8},{10,11... | collective-permute-start | bytes 786440 | tf_op jit(solution)/shard_map/ppermute | solution.py:303
  342.1 12.9 %collective-permute-start.4 = (f32[8,16,512]{2,1,0:T(8,128)S(1)}, f32[8,16,512]{2,1,0:T(8,128)S(1)}, u32[]{:S(2)}, u32[]{:S(2)}) collective-permute-start(f32[8,16,512]{2,1,0:T(8,128)S(1)} %dynamic-slice_bitcast_fusion), channel_id=1, source_target_pairs={{0,1},{1,0},{2,3},{3,2},{4,5},{5,4},{6,7},{7,6},{8,9},{9,8},{10,11... | collective-permute-start | bytes 786440 | tf_op jit(solution)/shard_map/ppermute | solution.py:303
  356.8 0.8 copy-start.3
Sparse Core Ops, SparseCore 0:
  143.2 118.9 reduce-scatter.2
  265.1 55.2 reduce-scatter.4

commit v8 on v7

--- a/solution.py
+++ b/solution.py
@@ -290,33 +290,59 @@
     columns = [[z * SIDES + x for z in range(levels)] for x in range(SIDES)]
     swap = [(i, i + 1 - 2 * (i % SIDES)) for i in range(pw_count)]
     height = slab_points // 2
+    here = lax.axis_index("ka")
+    engaged = wrapped | (here < SHIFT_DEV)
+
+    def spread_there(block):
+        return lax.cond(engaged, spread, lambda block: block, block)
+
     def part(i, block):
         own = own_of[i * height : (i + 1) * height]
         return slab_products(coeffs, block, own, levels)
 
+    def summed_over_z(block):
+        return lax.psum_scatter(
+            block, "pw", scatter_dimension=0, axis_index_groups=columns, tiled=True
+        )
+
     def summed(block):
-        block = lax.psum_scatter(
-            block, "pw", scatter_dimension=0, axis_index_groups=columns, tiled=True
-        ).reshape(height, SIDES, bands // pw_count, 2 * bands)
+        block = block.reshape(height, SIDES, bands // pw_count, 2 * bands)
         keep = lax.dynamic_index_in_dim(block, side, 1, keepdims=False)
         give = lax.dynamic_index_in_dim(block, 1 - side, 1, keepdims=False)
         return keep + lax.ppermute(give, "pw", swap)
 
     early = lax.ppermute(coeffs[:height], "ka", inside)
-    real = spread(planes[0])
+    real = spread_there(planes[0])
     real, later, early, late = lax.optimization_barrier((real, planes[1], early, coeffs[height:]))
-    imag = spread(later)
+    imag = spread_there(later)
     late = lax.ppermute(late, "ka", inside)
     real_over = lax.ppermute(real, "ka", outside)
     upper = part(0, early)
     imag, _, late, real_over = lax.optimization_barrier((imag, upper, late, real_over))
     imag_over = lax.ppermute(imag, "ka", outside)
     lower = part(1, late)
-    within = jnp.concatenate([summed(upper), summed(lower)])
+    sums = [summed_over_z(upper), summed_over_z(lower)]
     real, imag, _ = lax.optimization_barrier((real, imag, lower))
-    moved = scattered_rows([real, imag], gshift)
-    products = second_plane(moved, imag_over, first_plane(moved, real_over))
-    across = spread(products).reshape(slab_points, bands // pw_count, 2 * bands)
+    rows_all = gshift.shape[0]
+    moved = lax.cond(
+        wrapped,
+        lambda real, imag: scattered_rows([real, imag], gshift),
+        lambda real, imag: jnp.zeros((2, bands, rows_all), real.dtype),
+        real,
+        imag,
+    )
+
+    moved, *sums = lax.optimization_barrier((moved, *sums))
+    within = jnp.concatenate([summed(block) for block in sums])
+
+    def finished(moved, real, imag):
+        return spread(second_plane(moved, imag, first_plane(moved, real)))
+
+    def empty(moved, real, imag):
+        return jnp.zeros((bands, 2 * bands), jnp.float32)
+
+    across = lax.cond(wrapped, finished, empty, moved, real_over, imag_over)
+    across = across.reshape(slab_points, bands // pw_count, 2 * bands)
 
     result = reordered(order, wrapped.astype(jnp.int32).reshape(1), [within, across])
     result = result.reshape(slab_points, bands // pw_count, 2, bands)

time: 370 us -> 369 us (level)
  the two profiles are of different devices: /device:TPU:24 before, /device:TPU:26 now
where the time goes in v8:
time: 369 us; the launch traced here: 368 us
  blocking collectives  215 us (58%)
  Pallas kernels  88.3 us (24%)
  waiting for transfers between devices  18.6 us (5%)
  local copies, waits for them, and re-layouts  15.7 us (4%)
  starting transfers between devices  13.5 us (4%)
  between operations  13.5 us (4%)
    all_to_all x3, blocking collectives, spread(): return lax.all_to_all(block, 'pw', split_axis=0, concat_axis=0, tiled=True)  215 us
    pallas_call x1, Pallas kernels, scattered_rows(): pl.pallas_call(scatter_rows_kernel, grid=(total // height,), in_specs=[pl...  49.2 us
    pallas_call x2, Pallas kernels, slab_products(): pl.pallas_call(slab_kernel, grid_spec=pltpu.PrefetchScalarGridSpec(num_sc...  18.5 us
    ppermute x1, waiting for transfers between devices, on_device(): imag_over = lax.ppermute(imag, 'ka', outside)  18.3 us
    pallas_call x1, Pallas kernels, ordered_planes(): pl.pallas_call(ordered_planes_kernel, grid_spec=pltpu.PrefetchScalarGridS...  7.88 us
  transfers between devices with their start and end apart: 8, of which 2 were waited for; matrix products, arithmetic and copies ran while one was open for 2% of the time, Pallas kernels for 21%

profile of v8, /device:TPU:26, one launch (start us, length us, event | category | flops | bytes accessed | tf_op | source)
XLA Modules:
  0.0 368.4 jit_solution(12130920443817702591)
XLA Ops:
  6.5 6.1 %fusion.1 = (bf16[8,2,384,256]{3,2,1,0:T(8,128)(2,1)}, bf16[8,2,384,256]{3,2,1,0:T(8,128)(2,1)}) fusion(bf16[16,2,384,256]{3,2,1,0:T(8,128)(2,1)} %own_ref.3), kind=kLoop, calls=%fused_computation.13 | loop fusion | bytes 12582912 | tf_op jit(solution)/shard_map/slice | solution.py:316
  12.7 4.3 %collective-permute-start = (bf16[8,2,384,256]{3,2,1,0:T(8,128)(2,1)}, bf16[8,2,384,256]{3,2,1,0:T(8,128)(2,1)}, u32[]{:S(2)}, u32[]{:S(2)}) collective-permute-start(bf16[8,2,384,256]{3,2,1,0:T(8,128)(2,1)} %get-tuple-element.71), channel_id=1, source_target_pairs={{32,0},{48,16},{64,32},{80,48},{96,64},{112,80},{128,96},{144,112}... | collective-permute-start | bytes 9437192 | tf_op jit(solution)/shard_map/ppermute | solution.py:314
  17.6 7.9 %shard_map.38 = (bf16[16,384,256]{2,1,0:T(8,128)(2,1)S(1)}, bf16[16,384,256]{2,1,0:T(8,128)(2,1)}) custom-call(s32[16]{0:T(128)} %broadcast_select_fusion.order, bf16[16,2,384,256]{3,2,1,0:T(8,128)(2,1)} %own_ref.3), custom_call_target="tpu_custom_call" | custom-call | bytes 12582912 | tf_op jit(solution)/shard_map/pallas_call | solution.py:128
  25.5 84.8 %conditional.4 = (bf16[16,384,256]{2,1,0:T(8,128)(2,1)S(1)}) conditional(s32[]{:T(128)} %convert_element_type.10, bf16[16,384,256]{2,1,0:T(8,128)(2,1)S(1)} %get-tuple-element.54, bf16[16,384,256]{2,1,0:T(8,128)(2,1)S(1)} %get-tuple-element.54), branch_computations={%region_1.2_spmd, %region_2.3_spmd} | conditional | bytes 12582920 | solution.py:297
  25.7 84.5 %all_to_all.15 = bf16[16,384,256]{2,1,0:T(8,128)(2,1)S(1)} all-to-all(bf16[16,384,256]{2,1,0:T(8,128)(2,1)S(1)} %copy.29), channel_id=1, replica_groups=mesh['ka'=16,'pw'=16] {'pw'}, dimensions={0} | all-to-all | bytes 6291456 | tf_op jit(solution)/shard_map/cond/branch_1_fun/all_to_all | solution.py:281
  110.3 0.7 fusion.2
  110.9 9.3 %shard_map.39 = f32[8,8,32,512]{3,2,1,0:T(8,128)} custom-call(s32[8]{0:T(128)} %get-tuple-element.73.own_of, bf16[16,2,384,256]{3,2,1,0:T(8,128)(2,1)} %own_ref.3, bf16[8,2,384,256]{3,2,1,0:T(8,128)(2,1)} %collective-permute-done.partner_ref), custom_call_target="tpu_custom_call" | custom-call | flops 1610612736 | bytes 10485760 | tf_op jit(solution)/shard_map/pallas_call | solution.py:167
  120.3 2.9 collective-permute-start.1
  123.2 1.3 collective-permute-start.2
  124.5 114.3 %conditional.5 = (bf16[16,384,256]{2,1,0:T(8,128)(2,1)}) conditional(s32[]{:T(128)} %convert_element_type.10, bf16[16,384,256]{2,1,0:T(8,128)(2,1)} %get-tuple-element.57, bf16[16,384,256]{2,1,0:T(8,128)(2,1)} %get-tuple-element.57), branch_computations={%region_3.4_spmd, %region_4.5_spmd} | conditional | bytes 12582920 | solution.py:297
  124.5 1.9 copy.30
  126.4 112.4 %all_to_all.16 = bf16[16,384,256]{2,1,0:T(8,128)(2,1)} all-to-all(bf16[16,384,256]{2,1,0:T(8,128)(2,1)S(1)} %copy.30), channel_id=1, replica_groups=mesh['ka'=16,'pw'=16] {'pw'}, dimensions={0} | all-to-all | bytes 6291456 | tf_op jit(solution)/shard_map/cond/branch_1_fun/all_to_all | solution.py:281
  238.8 9.2 %shard_map.40 = f32[8,8,32,512]{3,2,1,0:T(8,128)} custom-call(s32[8]{0:T(128)} %get-tuple-element.72.own_of, bf16[16,2,384,256]{3,2,1,0:T(8,128)(2,1)} %own_ref.3, bf16[8,2,384,256]{3,2,1,0:T(8,128)(2,1)} %collective-permute-done.1.partner_ref), custom_call_target="tpu_custom_call" | custom-call | flops 1610612736 | bytes 10485760 | tf_op jit(solution)/shard_map/pallas_call | solution.py:167
  248.1 1.3 collective-permute-start.5
  249.5 49.2 %conditional.6 = (bf16[2,256,6144]{2,1,0:T(8,128)(2,1)}) conditional(s32[]{:T(128)} %convert_element_type.4, () %tuple.35, (s32[6144]{0:T(1024)S(1)}, bf16[16,384,256]{2,1,0:T(8,128)(2,1)}, bf16[16,384,256]{2,1,0:T(8,128)(2,1)}) %tuple.58), branch_computations={%region_5.6_spmd, %region_6.7_spmd} | conditional | flops 38654705664 | bytes 12582920 | solution.py:327
  249.5 49.2 %branch_1_fun.3 = bf16[2,256,6144]{2,1,0:T(8,128)(2,1)} custom-call(s32[1,6144]{1,0:T(1,128)S(1)} %bitcast.29, bf16[16,384,256]{2,1,0:T(8,128)(2,1)} %get-tuple-element.35.real_ref, bf16[16,384,256]{2,1,0:T(8,128)(2,1)} %get-tuple-element.36.imag_ref), custom_call_target="tpu_custom_call" | custom-call | flops 38654705664 | bytes 12582912 | tf_op jit(solution)/shard_map/cond/branch_1_fun/pallas_call | solution.py:94
  299.0 1.7 dynamic-slice_bitcast_fusion.1
  300.6 2.0 collective-permute-start.3
  302.7 1.0 dynamic-slice_bitcast_fusion
  303.6 1.6 collective-permute-start.4
  305.2 18.3 %collective-permute-done.5 = bf16[16,384,256]{2,1,0:T(8,128)(2,1)} collective-permute-done((bf16[16,384,256]{2,1,0:T(8,128)(2,1)}, bf16[16,384,256]{2,1,0:T(8,128)(2,1)}, u32[]{:S(2)}, u32[]{:S(2)}) %collective-permute-start.5) | collective-permute-done | bytes 3145760 | tf_op jit(solution)/shard_map/ppermute | solution.py:322
  323.5 30.2 %conditional.7 = (f32[16,16,512]{2,1,0:T(8,128)S(1)}) conditional(s32[]{:T(128)} %convert_element_type.4, () %tuple.41, (bf16[2,256,6144]{2,1,0:T(8,128)(2,1)}, bf16[16,384,256]{2,1,0:T(8,128)(2,1)S(1)}, bf16[16,384,256]{2,1,0:T(8,128)(2,1)}) %tuple.42), branch_computations={%region_9.10_spmd, %region_10.11_spmd} | conditional | flops 3221225472 | bytes 57671744 | solution.py:344
  323.5 1.7 copy-done.1
  325.2 5.6 %branch_1_fun.4.first_ref = f32[2,256,256]{2,1,0:T(8,128)} custom-call(bf16[2,256,6144]{2,1,0:T(8,128)(2,1)} %get-tuple-element.37.own_ref, bf16[16,384,256]{2,1,0:T(8,128)(2,1)} %copy-done.1), custom_call_target="tpu_custom_call" | custom-call | flops 1610612736 | bytes 9437184 | tf_op jit(solution)/shard_map/cond/branch_1_fun/pallas_call | solution.py:244
  330.8 4.6 %branch_1_fun.5 = f32[256,512]{1,0:T(8,128)} custom-call(bf16[2,256,6144]{2,1,0:T(8,128)(2,1)S(1)} %copy-done, bf16[16,384,256]{2,1,0:T(8,128)(2,1)} %get-tuple-element.38.partner_ref, f32[2,256,256]{2,1,0:T(8,128)} %branch_1_fun.4.first_ref), custom_call_target="tpu_custom_call" | custom-call | flops 1610612736 | bytes 9437184 | tf_op jit(solution)/shard_map/cond/branch_1_fun/pallas_call | solution.py:258
  335.4 18.3 %all_to_all.17 = f32[16,16,512]{2,1,0:T(8,128)S(1)} all-to-all(f32[16,16,512]{2,1,0:T(8,128)} %bitcast.24), channel_id=1, replica_groups=mesh['ka'=16,'pw'=16] {'pw'}, dimensions={0} | all-to-all | bytes 1048576 | tf_op jit(solution)/shard_map/cond/branch_1_fun/all_to_all | solution.py:281
  353.7 1.1 bitcast_add_fusion.1
  354.7 1.1 bitcast_add_fusion
  355.8 0.8 pad_maximum_fusion.refs_0_
  356.7 2.5 shard_map.41
  359.1 1.4 reshape.25
  360.5 1.1 copy.20
  (26 shorter events, 1.2 us)
Async XLA Ops:
  6.5 10.4 %copy-start.5 = (s32[16]{0:T(128)S(1)}, s32[16]{0:T(128)}, u32[]{:S(2)}) copy-start(s32[16]{0:T(128)} %param.12) | copy-start | bytes 196
  6.5 292.2 %reduce-scatter.3.cloned.1.call-start = ((), (), s32[]{:S(2)}) async-start(), calls=%async_computation.5 | async-start | bytes 4718592 | tf_op jit(solution)/shard_map/reduce_scatter | solution.py:304
  12.7 98.3 %collective-permute-start = (bf16[8,2,384,256]{3,2,1,0:T(8,128)(2,1)}, bf16[8,2,384,256]{3,2,1,0:T(8,128)(2,1)}, u32[]{:S(2)}, u32[]{:S(2)}) collective-permute-start(bf16[8,2,384,256]{3,2,1,0:T(8,128)(2,1)} %get-tuple-element.71), channel_id=1, source_target_pairs={{32,0},{48,16},{64,32},{80,48},{96,64},{112,80},{128,96},{144,112}... | collective-permute-start | bytes 9437192 | tf_op jit(solution)/shard_map/ppermute | solution.py:314
  17.0 8.5 %copy-start.3 = (s32[16]{0:T(128)}, s32[16]{0:T(128)S(1)}, u32[]{:S(2)}) copy-start(s32[16]{0:T(128)S(1)} %and_select_fusion.order) | copy-start | bytes 196
  110.3 10.0 %copy-start.2 = (bf16[16,384,256]{2,1,0:T(8,128)(2,1)}, bf16[16,384,256]{2,1,0:T(8,128)(2,1)S(1)}, u32[]{:S(2)}) copy-start(bf16[16,384,256]{2,1,0:T(8,128)(2,1)S(1)} %get-tuple-element.74) | copy-start | bytes 9437188
  120.2 178.7 %reduce-scatter.5.cloned.1.call-start = ((), (), s32[]{:S(2)}) async-start(), calls=%async_computation.6 | async-start | bytes 4718592 | tf_op jit(solution)/shard_map/reduce_scatter | solution.py:304
  120.3 118.6 %collective-permute-start.1 = (bf16[8,2,384,256]{3,2,1,0:T(8,128)(2,1)}, bf16[8,2,384,256]{3,2,1,0:T(8,128)(2,1)}, u32[]{:S(2)}, u32[]{:S(2)}) collective-permute-start(bf16[8,2,384,256]{3,2,1,0:T(8,128)(2,1)} %get-tuple-element.59), channel_id=1, source_target_pairs={{32,0},{48,16},{64,32},{80,48},{96,64},{112,80},{128,96},{144,112}... | collective-permute-start | bytes 9437192 | tf_op jit(solution)/shard_map/ppermute | solution.py:318
  123.2 115.6 %collective-permute-start.2 = (bf16[16,384,256]{2,1,0:T(8,128)(2,1)}, bf16[16,384,256]{2,1,0:T(8,128)(2,1)S(1)}, u32[]{:S(2)}, u32[]{:S(2)}) collective-permute-start(bf16[16,384,256]{2,1,0:T(8,128)(2,1)} %copy-done.2), channel_id=1, source_target_pairs={{0,224},{16,240},{1,225},{17,241},{2,226},{18,242},{3,227},{19,243... | collective-permute-start | bytes 9437192 | tf_op jit(solution)/shard_map/ppermute | solution.py:319
  248.1 1.3 copy-start.4
  248.1 75.4 %collective-permute-start.5 = (bf16[16,384,256]{2,1,0:T(8,128)(2,1)}, bf16[16,384,256]{2,1,0:T(8,128)(2,1)}, u32[]{:S(2)}, u32[]{:S(2)}) collective-permute-start(bf16[16,384,256]{2,1,0:T(8,128)(2,1)} %get-tuple-element.75), channel_id=1, source_target_pairs={{0,224},{16,240},{1,225},{17,241},{2,226},{18,242},{3,227},{19,243... | collective-permute-start | bytes 9437192 | tf_op jit(solution)/shard_map/ppermute | solution.py:322
  300.6 53.0 %collective-permute-start.3 = (f32[8,16,512]{2,1,0:T(8,128)}, f32[8,16,512]{2,1,0:T(8,128)}, u32[]{:S(2)}, u32[]{:S(2)}) collective-permute-start(f32[8,16,512]{2,1,0:T(8,128)} %dynamic-slice_bitcast_fusion.1), channel_id=1, source_target_pairs={{0,1},{1,0},{2,3},{3,2},{4,5},{5,4},{6,7},{7,6},{8,9},{9,8},{10,11... | collective-permute-start | bytes 786440 | tf_op jit(solution)/shard_map/ppermute | solution.py:312
  303.6 51.1 %collective-permute-start.4 = (f32[8,16,512]{2,1,0:T(8,128)S(1)}, f32[8,16,512]{2,1,0:T(8,128)}, u32[]{:S(2)}, u32[]{:S(2)}) collective-permute-start(f32[8,16,512]{2,1,0:T(8,128)S(1)} %dynamic-slice_bitcast_fusion), channel_id=1, source_target_pairs={{0,1},{1,0},{2,3},{3,2},{4,5},{5,4},{6,7},{7,6},{8,9},{9,8},{10,11... | collective-permute-start | bytes 786440 | tf_op jit(solution)/shard_map/ppermute | solution.py:312
  323.5 1.7 copy-start.1
  325.2 5.7 %copy-start = (bf16[2,256,6144]{2,1,0:T(8,128)(2,1)S(1)}, bf16[2,256,6144]{2,1,0:T(8,128)(2,1)}, u32[]{:S(2)}) copy-start(bf16[2,256,6144]{2,1,0:T(8,128)(2,1)} %get-tuple-element.37.own_ref) | copy-start | bytes 18874372 | tf_op jit(solution)/shard_map/cond
Sparse Core Ops, SparseCore 0:
  120.4 118.1 reduce-scatter.2
  248.2 50.6 reduce-scatter.4

commit v9 on v8

--- a/solution.py
+++ b/solution.py
@@ -317,9 +317,10 @@
     imag = spread_there(later)
     late = lax.ppermute(late, "ka", inside)
     real_over = lax.ppermute(real, "ka", outside)
+    imag, early, late, real_over = lax.optimization_barrier((imag, early, late, real_over))
+    imag_over = lax.ppermute(imag, "ka", outside)
     upper = part(0, early)
-    imag, _, late, real_over = lax.optimization_barrier((imag, upper, late, real_over))
-    imag_over = lax.ppermute(imag, "ka", outside)
+    _, late = lax.optimization_barrier((upper, late))
     lower = part(1, late)
     sums = [summed_over_z(upper), summed_over_z(lower)]
     real, imag, _ = lax.optimization_barrier((real, imag, lower))

time: 369 us -> 397 us (1.076)
  waiting for transfers between devices: 18.6 us -> 72.8 us
  blocking collectives: 215 us -> 187 us
    reduce_scatter x2, waiting for transfers between devices: 0.27 us -> 50.6 us  [summed_over_z(): lax.psum_scatter(block, 'pw', scatter_dimension=0, axis_index_groups=colu...]
    all_to_all x3, blocking collectives: 215 us -> 187 us  [spread(): return lax.all_to_all(block, 'pw', split_axis=0, concat_axis=0, tiled=True)]
    ppermute x1, waiting for transfers between devices: 0.01 us -> 22.2 us  [on_device(): real_over = lax.ppermute(real, 'ka', outside)]
    ppermute x1, waiting for transfers between devices: 18.3 us -> 0.01 us  [on_device(): imag_over = lax.ppermute(imag, 'ka', outside)]
  transfers between devices with their start and end apart: 8 -> 8, of which waited for: 2 -> 2; matrix products, arithmetic and copies ran while one was open for 2% -> 2% of each run, Pallas kernels for 21% -> 19%
where the time goes in v9:
time: 397 us; the launch traced here: 396 us
  blocking collectives  187 us (47%)
  Pallas kernels  88.3 us (22%)
  waiting for transfers between devices  72.8 us (18%)
  local copies, waits for them, and re-layouts  17.3 us (4%)
  starting transfers between devices  13.6 us (3%)
  between operations  13.5 us (3%)
    all_to_all x3, blocking collectives, spread(): return lax.all_to_all(block, 'pw', split_axis=0, concat_axis=0, tiled=True)  187 us
    reduce_scatter x2, waiting for transfers between devices, summed_over_z(): lax.psum_scatter(block, 'pw', scatter_dimension=0, axis_index_groups=colu...  50.6 us
    pallas_call x1, Pallas kernels, scattered_rows(): pl.pallas_call(scatter_rows_kernel, grid=(total // height,), in_specs=[pl...  49.2 us
    ppermute x1, waiting for transfers between devices, on_device(): real_over = lax.ppermute(real, 'ka', outside)  22.2 us
    pallas_call x2, Pallas kernels, slab_products(): pl.pallas_call(slab_kernel, grid_spec=pltpu.PrefetchScalarGridSpec(num_sc...  18.5 us
  transfers between devices with their start and end apart: 8, of which 2 were waited for; matrix products, arithmetic and copies ran while one was open for 2% of the time, Pallas kernels for 19%

profile of v9, /device:TPU:26, one launch (start us, length us, event | category | flops | bytes accessed | tf_op | source)
XLA Modules:
  0.0 395.9 jit_solution(12255099361309573074)
XLA Ops:
  6.5 6.2 %fusion.1 = (bf16[8,2,384,256]{3,2,1,0:T(8,128)(2,1)}, bf16[8,2,384,256]{3,2,1,0:T(8,128)(2,1)}) fusion(bf16[16,2,384,256]{3,2,1,0:T(8,128)(2,1)} %own_ref.3), kind=kLoop, calls=%fused_computation.13 | loop fusion | bytes 12582912 | tf_op jit(solution)/shard_map/slice | solution.py:316
  12.7 4.4 %collective-permute-start = (bf16[8,2,384,256]{3,2,1,0:T(8,128)(2,1)}, bf16[8,2,384,256]{3,2,1,0:T(8,128)(2,1)}, u32[]{:S(2)}, u32[]{:S(2)}) collective-permute-start(bf16[8,2,384,256]{3,2,1,0:T(8,128)(2,1)} %get-tuple-element.75), channel_id=1, source_target_pairs={{32,0},{48,16},{64,32},{80,48},{96,64},{112,80},{128,96},{144,112}... | collective-permute-start | bytes 9437192 | tf_op jit(solution)/shard_map/ppermute | solution.py:314
  17.8 7.9 %shard_map.38 = (bf16[16,384,256]{2,1,0:T(8,128)(2,1)S(1)}, bf16[16,384,256]{2,1,0:T(8,128)(2,1)}) custom-call(s32[16]{0:T(128)} %broadcast_select_fusion.order, bf16[16,2,384,256]{3,2,1,0:T(8,128)(2,1)} %own_ref.3), custom_call_target="tpu_custom_call" | custom-call | bytes 12582912 | tf_op jit(solution)/shard_map/pallas_call | solution.py:128
  25.7 84.8 %conditional.4 = (bf16[16,384,256]{2,1,0:T(8,128)(2,1)S(1)}) conditional(s32[]{:T(128)} %convert_element_type.10, bf16[16,384,256]{2,1,0:T(8,128)(2,1)S(1)} %get-tuple-element.56, bf16[16,384,256]{2,1,0:T(8,128)(2,1)S(1)} %get-tuple-element.56), branch_computations={%region_1.2_spmd, %region_2.3_spmd} | conditional | bytes 12582920 | solution.py:297
  25.9 84.5 %all_to_all.15 = bf16[16,384,256]{2,1,0:T(8,128)(2,1)S(1)} all-to-all(bf16[16,384,256]{2,1,0:T(8,128)(2,1)S(1)} %copy.29), channel_id=1, replica_groups=mesh['ka'=16,'pw'=16] {'pw'}, dimensions={0} | all-to-all | bytes 6291456 | tf_op jit(solution)/shard_map/cond/branch_1_fun/all_to_all | solution.py:281
  110.5 1.6 copy-done.2
  112.1 3.0 collective-permute-start.1
  115.1 1.3 collective-permute-start.2
  117.0 79.8 %conditional.5 = (bf16[16,384,256]{2,1,0:T(8,128)(2,1)}) conditional(s32[]{:T(128)} %convert_element_type.10, bf16[16,384,256]{2,1,0:T(8,128)(2,1)} %get-tuple-element.59, bf16[16,384,256]{2,1,0:T(8,128)(2,1)} %get-tuple-element.59), branch_computations={%region_3.4_spmd, %region_4.5_spmd} | conditional | bytes 12582920 | solution.py:297
  117.0 1.9 copy.30
  118.9 77.9 %all_to_all.16 = bf16[16,384,256]{2,1,0:T(8,128)(2,1)} all-to-all(bf16[16,384,256]{2,1,0:T(8,128)(2,1)S(1)} %copy.30), channel_id=1, replica_groups=mesh['ka'=16,'pw'=16] {'pw'}, dimensions={0} | all-to-all | bytes 6291456 | tf_op jit(solution)/shard_map/cond/branch_1_fun/all_to_all | solution.py:281
  196.8 22.2 %collective-permute-done.2 = bf16[16,384,256]{2,1,0:T(8,128)(2,1)S(1)} collective-permute-done((bf16[16,384,256]{2,1,0:T(8,128)(2,1)}, bf16[16,384,256]{2,1,0:T(8,128)(2,1)S(1)}, u32[]{:S(2)}, u32[]{:S(2)}) %collective-permute-start.2) | collective-permute-done | bytes 3145760 | tf_op jit(solution)/shard_map/ppermute | solution.py:319
  219.0 9.3 %shard_map.39 = f32[8,8,32,512]{3,2,1,0:T(8,128)} custom-call(s32[8]{0:T(128)} %get-tuple-element.76.own_of, bf16[16,2,384,256]{3,2,1,0:T(8,128)(2,1)} %own_ref.3, bf16[8,2,384,256]{3,2,1,0:T(8,128)(2,1)} %collective-permute-done.partner_ref), custom_call_target="tpu_custom_call" | custom-call | flops 1610612736 | bytes 10485760 | tf_op jit(solution)/shard_map/pallas_call | solution.py:167
  228.3 9.2 %shard_map.40 = f32[8,8,32,512]{3,2,1,0:T(8,128)} custom-call(s32[8]{0:T(128)} %get-tuple-element.77.own_of, bf16[16,2,384,256]{3,2,1,0:T(8,128)(2,1)} %own_ref.3, bf16[8,2,384,256]{3,2,1,0:T(8,128)(2,1)} %collective-permute-done.1.partner_ref), custom_call_target="tpu_custom_call" | custom-call | flops 1610612736 | bytes 10485760 | tf_op jit(solution)/shard_map/pallas_call | solution.py:167
  237.6 1.3 collective-permute-start.5
  238.9 49.2 %conditional.6 = (bf16[2,256,6144]{2,1,0:T(8,128)(2,1)}) conditional(s32[]{:T(128)} %convert_element_type.4, () %tuple.36, (s32[6144]{0:T(1024)S(1)}, bf16[16,384,256]{2,1,0:T(8,128)(2,1)}, bf16[16,384,256]{2,1,0:T(8,128)(2,1)}) %tuple.60), branch_computations={%region_5.6_spmd, %region_6.7_spmd} | conditional | flops 38654705664 | bytes 12582920 | solution.py:328
  238.9 49.2 %branch_1_fun.3 = bf16[2,256,6144]{2,1,0:T(8,128)(2,1)} custom-call(s32[1,6144]{1,0:T(1,128)S(1)} %bitcast.29, bf16[16,384,256]{2,1,0:T(8,128)(2,1)} %get-tuple-element.35.real_ref, bf16[16,384,256]{2,1,0:T(8,128)(2,1)} %get-tuple-element.36.imag_ref), custom_call_target="tpu_custom_call" | custom-call | flops 38654705664 | bytes 12582912 | tf_op jit(solution)/shard_map/cond/branch_1_fun/pallas_call | solution.py:94
  288.2 50.6 %reduce-scatter.5.cloned.1.call-done = f32[1,8,32,512]{3,2,1,0:T(8,128)} async-done(((f32[8,8,32,512]{3,2,1,0:T(8,128)}), f32[1,8,32,512]{3,2,1,0:T(8,128)}) %reduce-scatter.5.cloned.1.call-update) | async-done | bytes 524304 | tf_op jit(solution)/shard_map/reduce_scatter | solution.py:304
  338.8 1.7 dynamic-slice_bitcast_fusion.1
  340.4 2.1 collective-permute-start.3
  342.5 1.0 dynamic-slice_bitcast_fusion
  343.5 1.5 collective-permute-start.4
  345.0 36.1 %conditional.7 = (f32[16,16,512]{2,1,0:T(8,128)S(1)}) conditional(s32[]{:T(128)} %convert_element_type.4, () %tuple.43, (bf16[2,256,6144]{2,1,0:T(8,128)(2,1)}, bf16[16,384,256]{2,1,0:T(8,128)(2,1)S(1)}, bf16[16,384,256]{2,1,0:T(8,128)(2,1)}) %tuple.44), branch_computations={%region_9.10_spmd, %region_10.11_spmd} | conditional | flops 3221225472 | bytes 57671744 | solution.py:345
  345.0 1.7 copy-done.1
  346.7 5.6 %branch_1_fun.4.first_ref = f32[2,256,256]{2,1,0:T(8,128)} custom-call(bf16[2,256,6144]{2,1,0:T(8,128)(2,1)} %get-tuple-element.37.own_ref, bf16[16,384,256]{2,1,0:T(8,128)(2,1)} %copy-done.1), custom_call_target="tpu_custom_call" | custom-call | flops 1610612736 | bytes 9437184 | tf_op jit(solution)/shard_map/cond/branch_1_fun/pallas_call | solution.py:244
  352.4 4.6 %branch_1_fun.5 = f32[256,512]{1,0:T(8,128)} custom-call(bf16[2,256,6144]{2,1,0:T(8,128)(2,1)S(1)} %copy-done, bf16[16,384,256]{2,1,0:T(8,128)(2,1)} %get-tuple-element.38.partner_ref, f32[2,256,256]{2,1,0:T(8,128)} %branch_1_fun.4.first_ref), custom_call_target="tpu_custom_call" | custom-call | flops 1610612736 | bytes 9437184 | tf_op jit(solution)/shard_map/cond/branch_1_fun/pallas_call | solution.py:258
  356.9 24.2 %all_to_all.17 = f32[16,16,512]{2,1,0:T(8,128)S(1)} all-to-all(f32[16,16,512]{2,1,0:T(8,128)} %bitcast.24), channel_id=1, replica_groups=mesh['ka'=16,'pw'=16] {'pw'}, dimensions={0} | all-to-all | bytes 1048576 | tf_op jit(solution)/shard_map/cond/branch_1_fun/all_to_all | solution.py:281
  381.1 1.1 bitcast_add_fusion.1
  382.2 1.1 bitcast_add_fusion
  384.1 2.5 shard_map.41
  386.6 1.4 reshape.25
  388.0 1.1 copy.20
  (26 shorter events, 2.5 us)
Async XLA Ops:
  6.5 10.6 %copy-start.5 = (s32[16]{0:T(128)S(1)}, s32[16]{0:T(128)}, u32[]{:S(2)}) copy-start(s32[16]{0:T(128)} %param.12) | copy-start | bytes 196
  6.5 281.6 %reduce-scatter.3.cloned.1.call-start = ((), (), s32[]{:S(2)}) async-start(), calls=%async_computation.5 | async-start | bytes 4718592 | tf_op jit(solution)/shard_map/reduce_scatter | solution.py:304
  12.7 97.7 %collective-permute-start = (bf16[8,2,384,256]{3,2,1,0:T(8,128)(2,1)}, bf16[8,2,384,256]{3,2,1,0:T(8,128)(2,1)}, u32[]{:S(2)}, u32[]{:S(2)}) collective-permute-start(bf16[8,2,384,256]{3,2,1,0:T(8,128)(2,1)} %get-tuple-element.75), channel_id=1, source_target_pairs={{32,0},{48,16},{64,32},{80,48},{96,64},{112,80},{128,96},{144,112}... | collective-permute-start | bytes 9437192 | tf_op jit(solution)/shard_map/ppermute | solution.py:314
  17.1 8.5 %copy-start.3 = (s32[16]{0:T(128)}, s32[16]{0:T(128)S(1)}, u32[]{:S(2)}) copy-start(s32[16]{0:T(128)S(1)} %and_select_fusion.order) | copy-start | bytes 196
  110.5 1.6 copy-start.2
  112.1 84.7 %collective-permute-start.1 = (bf16[8,2,384,256]{3,2,1,0:T(8,128)(2,1)}, bf16[8,2,384,256]{3,2,1,0:T(8,128)(2,1)}, u32[]{:S(2)}, u32[]{:S(2)}) collective-permute-start(bf16[8,2,384,256]{3,2,1,0:T(8,128)(2,1)} %get-tuple-element.61), channel_id=1, source_target_pairs={{32,0},{48,16},{64,32},{80,48},{96,64},{112,80},{128,96},{144,112}... | collective-permute-start | bytes 9437192 | tf_op jit(solution)/shard_map/ppermute | solution.py:318
  115.1 103.9 %collective-permute-start.2 = (bf16[16,384,256]{2,1,0:T(8,128)(2,1)}, bf16[16,384,256]{2,1,0:T(8,128)(2,1)S(1)}, u32[]{:S(2)}, u32[]{:S(2)}) collective-permute-start(bf16[16,384,256]{2,1,0:T(8,128)(2,1)} %copy-done.2), channel_id=1, source_target_pairs={{0,224},{16,240},{1,225},{17,241},{2,226},{18,242},{3,227},{19,243... | collective-permute-start | bytes 9437192 | tf_op jit(solution)/shard_map/ppermute | solution.py:319
  228.3 110.5 %reduce-scatter.5.cloned.1.call-start = ((), (), s32[]{:S(2)}) async-start(), calls=%async_computation.6 | async-start | bytes 4718592 | tf_op jit(solution)/shard_map/reduce_scatter | solution.py:304
  237.6 1.3 copy-start.4
  237.6 107.5 %collective-permute-start.5 = (bf16[16,384,256]{2,1,0:T(8,128)(2,1)}, bf16[16,384,256]{2,1,0:T(8,128)(2,1)}, u32[]{:S(2)}, u32[]{:S(2)}) collective-permute-start(bf16[16,384,256]{2,1,0:T(8,128)(2,1)} %get-tuple-element.79), channel_id=1, source_target_pairs={{0,224},{16,240},{1,225},{17,241},{2,226},{18,242},{3,227},{19,243... | collective-permute-start | bytes 9437192 | tf_op jit(solution)/shard_map/ppermute | solution.py:321
  340.4 40.7 %collective-permute-start.3 = (f32[8,16,512]{2,1,0:T(8,128)}, f32[8,16,512]{2,1,0:T(8,128)}, u32[]{:S(2)}, u32[]{:S(2)}) collective-permute-start(f32[8,16,512]{2,1,0:T(8,128)} %dynamic-slice_bitcast_fusion.1), channel_id=1, source_target_pairs={{0,1},{1,0},{2,3},{3,2},{4,5},{5,4},{6,7},{7,6},{8,9},{9,8},{10,11... | collective-permute-start | bytes 786440 | tf_op jit(solution)/shard_map/ppermute | solution.py:312
  343.5 38.7 %collective-permute-start.4 = (f32[8,16,512]{2,1,0:T(8,128)S(1)}, f32[8,16,512]{2,1,0:T(8,128)}, u32[]{:S(2)}, u32[]{:S(2)}) collective-permute-start(f32[8,16,512]{2,1,0:T(8,128)S(1)} %dynamic-slice_bitcast_fusion), channel_id=1, source_target_pairs={{0,1},{1,0},{2,3},{3,2},{4,5},{5,4},{6,7},{7,6},{8,9},{9,8},{10,11... | collective-permute-start | bytes 786440 | tf_op jit(solution)/shard_map/ppermute | solution.py:312
  345.0 1.7 copy-start.1
  346.7 5.6 %copy-start = (bf16[2,256,6144]{2,1,0:T(8,128)(2,1)S(1)}, bf16[2,256,6144]{2,1,0:T(8,128)(2,1)}, u32[]{:S(2)}) copy-start(bf16[2,256,6144]{2,1,0:T(8,128)(2,1)} %get-tuple-element.37.own_ref) | copy-start | bytes 18874372 | tf_op jit(solution)/shard_map/cond
Sparse Core Ops, SparseCore 0:
  228.4 53.8 reduce-scatter.2
  284.8 53.9 reduce-scatter.4

commit v10 on v5

--- a/solution.py
+++ b/solution.py
@@ -142,7 +142,7 @@
             out_ref[:, d * bands : (d + 1) * bands] = acc_ref[d]
 
 
-TAKE = 2
+TAKE = 8
 
 
 def pair_specs(own, partner):
@@ -166,7 +166,7 @@
         in_specs=specs,
         out_specs=pl.BlockSpec((2, bands, bands), lambda i: (0, 0, 0)),
         out_shape=jax.ShapeDtypeStruct((2, bands, bands), jnp.float32),
-        compiler_params=pltpu.CompilerParams(vmem_limit_bytes=56 << 20),
+        compiler_params=pltpu.CompilerParams(vmem_limit_bytes=24 << 20),
         cost_estimate=cost,
     )(own, partner)
 
@@ -181,7 +181,7 @@
         out_specs=pl.BlockSpec((bands, 2 * bands), lambda i: (0, 0)),
         out_shape=jax.ShapeDtypeStruct((bands, 2 * bands), jnp.float32),
         scratch_shapes=[pltpu.VMEM(first.shape, jnp.float32)],
-        compiler_params=pltpu.CompilerParams(vmem_limit_bytes=56 << 20),
+        compiler_params=pltpu.CompilerParams(vmem_limit_bytes=24 << 20),
         cost_estimate=cost,
     )(own, partner, first)
 
@@ -216,7 +216,7 @@
     waiting = reordered(order, crosses.astype(jnp.int32).reshape(1), [later], [turned, swapped])
     real, waiting = lax.optimization_barrier((real, waiting))
     imag = spread(waiting)
-    first = first_plane(moved, real)
+    first = pltpu.with_memory_space_constraint(first_plane(moved, real), pltpu.HBM)
     products = second_plane(moved, imag, first)
     products = spread(products).reshape(slab_points, bands // slab_points, 2, bands)
     return jnp.transpose(products, (1, 0, 2, 3))

time: 350 us -> 344 us (0.983)
  Pallas kernels: 73.5 us -> 66.2 us
    pallas_call x1, Pallas kernels: 7.97 us -> 3.93 us  [first_plane(): pl.pallas_call(first_plane_kernel, grid=grid, in_specs=specs, out_specs=p...]
  transfers between devices with their start and end apart: 7 -> 7, of which waited for: 4 -> 4; matrix products, arithmetic and copies ran while one was open for 1% -> 1% of each run, Pallas kernels for 19% -> 18%
where the time goes in v10:
time: 344 us; the launch traced here: 342 us
  waiting for transfers between devices  212 us (62%)
  Pallas kernels  66.2 us (19%)
  starting transfers between devices  31.5 us (9%)
  blocking collectives  21.8 us (6%)
  local copies, waits for them, and re-layouts  9.41 us (3%)
    all_to_all x3, waiting for transfers between devices, spread(): return lax.all_to_all(block, 'pw', split_axis=0, concat_axis=0, tiled=True)  106 us
    ppermute x1, waiting for transfers between devices, on_device(): direct = lax.ppermute(coeffs[:, 0], 'ka', straight)  106 us
    pallas_call x1, Pallas kernels, scattered_rows(): pl.pallas_call(scatter_rows_kernel, grid=(total // height,), in_specs=[pl...  49.2 us
    all_to_all x3, starting transfers between devices, spread(): return lax.all_to_all(block, 'pw', split_axis=0, concat_axis=0, tiled=True)  25.8 us
    all_to_all x1, blocking collectives, spread(): return lax.all_to_all(block, 'pw', split_axis=0, concat_axis=0, tiled=True)  21.8 us
    pallas_call x2, Pallas kernels, reordered(): pl.pallas_call(kernel, grid_spec=pltpu.PrefetchScalarGridSpec(num_scalar_...  8.13 us
  transfers between devices with their start and end apart: 7, of which 4 were waited for; matrix products, arithmetic and copies ran while one was open for 1% of the time, Pallas kernels for 18%

profile of v10, /device:TPU:26, one launch (start us, length us, event | category | flops | bytes accessed | tf_op | source)
XLA Modules:
  0.0 342.2 jit_solution(5383204595836305743)
XLA Ops:
  0.0 10.2 %all-to-all-start = ((bf16[16,2,384,256]{3,2,1,0:T(8,128)(2,1)}), bf16[16,2,384,256]{3,2,1,0:T(8,128)(2,1)}, u32[]{:S(2)}, u32[]{:S(2)}) async-start(bf16[16,2,384,256]{3,2,1,0:T(8,128)(2,1)} %param.3), calls=%async_computation | async-start | bytes 12582912 | tf_op jit(solution)/shard_map/all_to_all | solution.py:198
  10.2 0.0 copy-start.1
  10.2 2.3 slice_bitcast_fusion
  12.5 0.0 copy-start.5
  12.5 0.8 collective-permute-start
  13.4 0.6 copy-done.1
  13.9 1.5 slice_bitcast_fusion.1
  15.4 0.7 collective-permute-start.1
  16.2 0.5 and_select_fusion.order
  16.7 105.8 %collective-permute-done.refs_0_ = bf16[16,384,256]{2,1,0:T(8,128)(2,1)S(1)} collective-permute-done((bf16[16,384,256]{2,1,0:T(8,128)(2,1)S(1)}, bf16[16,384,256]{2,1,0:T(8,128)(2,1)S(1)}, u32[]{:S(2)}, u32[]{:S(2)}) %collective-permute-start) | collective-permute-done | bytes 3145760 | tf_op jit(solution)/shard_map/ppermute | solution.py:206
  122.5 1.7 copy-done.2
  124.1 3.8 %shard_map.37 = bf16[16,384,256]{2,1,0:T(8,128)(2,1)} custom-call(s32[16]{0:T(128)} %and_select_fusion.order, s32[1]{0:T(128)} %constant.34.clone.1.relayed, bf16[16,384,256]{2,1,0:T(8,128)(2,1)} %copy-done.2), custom_call_target="tpu_custom_call" | custom-call | bytes 6291456 | tf_op jit(solution)/shard_map/pallas_call | solution.py:52
  128.0 0.0 copy-start.4
  128.0 29.0 %all-to-all-done.own_ref = bf16[16,2,384,256]{3,2,1,0:T(8,128)(2,1)} async-done(((bf16[16,2,384,256]{3,2,1,0:T(8,128)(2,1)}), bf16[16,2,384,256]{3,2,1,0:T(8,128)(2,1)}, u32[]{:S(2)}, u32[]{:S(2)}) %all-to-all-start) | async-done | bytes 6291488 | tf_op jit(solution)/shard_map/all_to_all | solution.py:198
  157.0 5.9 %all-to-all-start.1 = ((bf16[16,384,256]{2,1,0:T(8,128)(2,1)}), bf16[16,384,256]{2,1,0:T(8,128)(2,1)S(1)}, u32[]{:S(2)}, u32[]{:S(2)}) async-start(bf16[16,384,256]{2,1,0:T(8,128)(2,1)} %shard_map.37), calls=%async_computation.1 | async-start | bytes 6291456 | tf_op jit(solution)/shard_map/all_to_all | solution.py:198
  162.9 0.8 collective-permute-start.3
  163.7 0.6 iota_select_fusion
  164.3 3.3 collective-permute-start.2
  167.7 49.2 %shard_map.38.own_ref = bf16[2,256,6144]{2,1,0:T(8,128)(2,1)} custom-call(s32[1,6144]{1,0:T(1,128)} %bitcast.19, bf16[16,2,384,256]{3,2,1,0:T(8,128)(2,1)} %all-to-all-done.own_ref), custom_call_target="tpu_custom_call" | custom-call | flops 38654705664 | bytes 12582912 | tf_op jit(solution)/shard_map/pallas_call | solution.py:93
  216.9 0.0 collective-permute-done.2.refs_2_
  216.9 1.2 copy-done.3
  218.1 4.3 %shard_map.39 = bf16[16,384,256]{2,1,0:T(8,128)(2,1)} custom-call(s32[16]{0:T(128)} %and_select_fusion.order, s32[1]{0:T(128)} %bitcast.4.relayed, bf16[16,192,256]{2,1,0:T(8,128)(2,1)} %collective-permute-done.3.refs_0_, bf16[16,192,256]{2,1,0:T(8,128)(2,1)} %collective-permute-done.1.refs_1_, bf16[16,192,256]{2,1,0:T(8,128)(2,1)} %copy-done.3), custom_call_target="tpu_custom_call" | custom-call | bytes 6291456 | tf_op jit(solution)/shard_map/pallas_call | solution.py:52
  222.4 13.9 %all-to-all-done.1.partner_ref = bf16[16,384,256]{2,1,0:T(8,128)(2,1)S(1)} async-done(((bf16[16,384,256]{2,1,0:T(8,128)(2,1)}), bf16[16,384,256]{2,1,0:T(8,128)(2,1)S(1)}, u32[]{:S(2)}, u32[]{:S(2)}) %all-to-all-start.1) | async-done | bytes 3145760 | tf_op jit(solution)/shard_map/all_to_all | solution.py:198
  236.3 9.7 %all-to-all-start.2 = ((bf16[16,384,256]{2,1,0:T(8,128)(2,1)}), bf16[16,384,256]{2,1,0:T(8,128)(2,1)}, u32[]{:S(2)}, u32[]{:S(2)}) async-start(bf16[16,384,256]{2,1,0:T(8,128)(2,1)} %shard_map.39), calls=%async_computation.2 | async-start | bytes 6291456 | tf_op jit(solution)/shard_map/all_to_all | solution.py:198
  246.0 3.9 %shard_map.40.first_ref = f32[2,256,256]{2,1,0:T(8,128)S(1)} custom-call(bf16[2,256,6144]{2,1,0:T(8,128)(2,1)} %shard_map.38.own_ref, bf16[16,384,256]{2,1,0:T(8,128)(2,1)S(1)} %all-to-all-done.1.partner_ref), custom_call_target="tpu_custom_call" | custom-call | flops 1610612736 | bytes 9437184 | tf_op jit(solution)/shard_map/pallas_call | solution.py:163
  249.9 0.0 copy-start
  249.9 0.8 copy-done
  250.7 63.4 %all-to-all-done.2.partner_ref = bf16[16,384,256]{2,1,0:T(8,128)(2,1)} async-done(((bf16[16,384,256]{2,1,0:T(8,128)(2,1)}), bf16[16,384,256]{2,1,0:T(8,128)(2,1)}, u32[]{:S(2)}, u32[]{:S(2)}) %all-to-all-start.2) | async-done | bytes 3145760 | tf_op jit(solution)/shard_map/all_to_all | solution.py:198
  314.1 4.9 %shard_map.41 = f32[256,512]{1,0:T(8,128)S(1)} custom-call(bf16[2,256,6144]{2,1,0:T(8,128)(2,1)} %shard_map.38.own_ref, bf16[16,384,256]{2,1,0:T(8,128)(2,1)} %all-to-all-done.2.partner_ref, f32[2,256,256]{2,1,0:T(8,128)} %copy-done), custom_call_target="tpu_custom_call" | custom-call | flops 1610612736 | bytes 9437184 | tf_op jit(solution)/shard_map/pallas_call | solution.py:177
  319.0 21.8 %all_to_all.24 = f32[16,16,512]{2,1,0:T(8,128)S(1)} all-to-all(f32[16,16,512]{2,1,0:T(8,128)S(1)} %bitcast.18), channel_id=1, replica_groups=mesh['ka'=16,'pw'=16] {'pw'}, dimensions={0} | all-to-all | bytes 1048576 | tf_op jit(solution)/shard_map/all_to_all | solution.py:198
  340.8 0.3 reshape.20
  341.1 1.1 copy.13
  (6 shorter events, 0.0 us)
Async XLA Ops:
  0.0 157.0 %all-to-all-start = ((bf16[16,2,384,256]{3,2,1,0:T(8,128)(2,1)}), bf16[16,2,384,256]{3,2,1,0:T(8,128)(2,1)}, u32[]{:S(2)}, u32[]{:S(2)}) async-start(bf16[16,2,384,256]{3,2,1,0:T(8,128)(2,1)} %param.3), calls=%async_computation | async-start | bytes 12582912 | tf_op jit(solution)/shard_map/all_to_all | solution.py:198
  10.2 3.7 %copy-start.1 = (bf16[16,2,384,256]{3,2,1,0:T(8,128)(2,1)S(1)}, bf16[16,2,384,256]{3,2,1,0:T(8,128)(2,1)}, u32[]{:S(2)}) copy-start(bf16[16,2,384,256]{3,2,1,0:T(8,128)(2,1)} %param.3) | copy-start | bytes 18874372
  12.5 3.6 %copy-start.5 = (s32[16]{0:T(128)S(1)}, s32[16]{0:T(128)}, u32[]{:S(2)}) copy-start(s32[16]{0:T(128)} %param.4) | copy-start | bytes 196
  12.5 110.0 %collective-permute-start = (bf16[16,384,256]{2,1,0:T(8,128)(2,1)S(1)}, bf16[16,384,256]{2,1,0:T(8,128)(2,1)S(1)}, u32[]{:S(2)}, u32[]{:S(2)}) collective-permute-start(bf16[16,384,256]{2,1,0:T(8,128)(2,1)S(1)} %slice_bitcast_fusion), channel_id=1, source_target_pairs={{32,0},{48,16},{64,32},{80,48},{96,64},{112,80},{128,96},{144,112}... | collective-permute-start | bytes 9437192 | tf_op jit(solution)/shard_map/ppermute | solution.py:206
  15.4 112.6 %collective-permute-start.1 = (bf16[16,192,256]{2,1,0:T(8,128)(2,1)S(1)}, bf16[16,192,256]{2,1,0:T(8,128)(2,1)}, u32[]{:S(2)}, u32[]{:S(2)}) collective-permute-start(bf16[16,192,256]{2,1,0:T(8,128)(2,1)S(1)} %get-tuple-element.22), channel_id=1, source_target_pairs={{32,0},{48,16},{64,32},{80,48},{96,64},{112,80},{0,96},{16,112},{1... | collective-permute-start | bytes 4718600 | tf_op jit(solution)/shard_map/ppermute | solution.py:207
  122.5 1.7 copy-start.2
  128.0 35.7 %copy-start.4 = (s32[6144]{0:T(1024)S(1)}, s32[6144]{0:T(1024)}, u32[]{:S(2)}) copy-start(s32[6144]{0:T(1024)} %param.5) | copy-start | bytes 73732
  157.0 79.3 %all-to-all-start.1 = ((bf16[16,384,256]{2,1,0:T(8,128)(2,1)}), bf16[16,384,256]{2,1,0:T(8,128)(2,1)S(1)}, u32[]{:S(2)}, u32[]{:S(2)}) async-start(bf16[16,384,256]{2,1,0:T(8,128)(2,1)} %shard_map.37), calls=%async_computation.1 | async-start | bytes 6291456 | tf_op jit(solution)/shard_map/all_to_all | solution.py:198
  162.9 54.0 %collective-permute-start.3 = (bf16[16,192,256]{2,1,0:T(8,128)(2,1)}, bf16[16,192,256]{2,1,0:T(8,128)(2,1)}, u32[]{:S(2)}, u32[]{:S(2)}) collective-permute-start(bf16[16,192,256]{2,1,0:T(8,128)(2,1)} %get-tuple-element.21), channel_id=1, source_target_pairs={{32,0},{48,16},{64,32},{80,48},{96,64},{112,80},{128,96},{144,112}... | collective-permute-start | bytes 4718600 | tf_op jit(solution)/shard_map/ppermute | solution.py:208
  164.3 52.6 %collective-permute-start.2 = (bf16[16,192,256]{2,1,0:T(8,128)(2,1)}, bf16[16,192,256]{2,1,0:T(8,128)(2,1)S(1)}, u32[]{:S(2)}, u32[]{:S(2)}) collective-permute-start(bf16[16,192,256]{2,1,0:T(8,128)(2,1)} %collective-permute-done.1.refs_1_), channel_id=1, source_target_pairs={{224,96},{240,112},{96,224},{112,240},{225,97},{241,113},{97,225},... | collective-permute-start | bytes 4718600 | tf_op jit(solution)/shard_map/ppermute | solution.py:211
  216.9 1.2 copy-start.3
  236.3 77.8 %all-to-all-start.2 = ((bf16[16,384,256]{2,1,0:T(8,128)(2,1)}), bf16[16,384,256]{2,1,0:T(8,128)(2,1)}, u32[]{:S(2)}, u32[]{:S(2)}) async-start(bf16[16,384,256]{2,1,0:T(8,128)(2,1)} %shard_map.39), calls=%async_computation.2 | async-start | bytes 6291456 | tf_op jit(solution)/shard_map/all_to_all | solution.py:198
  249.9 0.8 copy-start
